TPU v7x, 256 devices: a whole 4x4x8 slice. The times are simulated.
256 devices in a mesh: dp: 4 (over y), entity: 64 (over z, x, core).
Axes of the slice: x: 4, y: 4, z: 8, core: 2. Of those that a mesh axis runs over, the one named last changes fastest.
Arguments:
- entities: float32 [64, 4096, 256], P('entity'), may hold values from -20 to 20
- relations: float32 [256, 256, 256], P('entity'), may hold values from -0.375 to 0.375
- candidate_blocks: int32 [256, 8], P('dp'), may hold values from 0 to 63, as said below
- list_lengths: int32 [4, 64], P('dp'), may hold values from 2 to 8, as said below
- head_offsets: int32 [32768], P(('dp', 'entity')), may hold values from 0 to 4095
- relation_offsets: int32 [32768], P(('dp', 'entity')), may hold values from 0 to 3
- target_codes: int32 [32768], P(('dp', 'entity')), may hold values from 0 to 32767
Outputs:
- loss: float32 [32768], P(('dp', 'entity'))
- entity_grad: float32 [64, 4096, 256], P('entity', 'dp')
Inputs may be any that keep to these rules, and one draw needn't show every extreme that they name: `candidate_blocks`: each row names 8 different blocks. Among the entries of the 64 rows of one dp group, used or not, no block is named more than 12 times; in every dp group one block is named exactly 12 times, each time at a used entry. `list_lengths`: the 64 lengths of one dp group sum to 320, and one of them is 8.
All inputs are finite; a program needn't handle non-finite values.
Results may differ from a plain program's by a relative error of at most 0.0025.
The roundings to bfloat16 on the way count: a program that leaves them out, or rounds other values in their place, can miss the bound.
Values may be sent and summed in bfloat16 or wider, within the bound.
No kernel may reach another device: no remote copies, remote signals or barrier semaphores. Data moves between devices by JAX's collectives and lax.ppermute only.
A program may use at most 64 MiB of HBM per device.

v0:
```python
import jax
import jax.numpy as jnp
from jax import lax
from jax.sharding import PartitionSpec as P

CAP = 12


negative_floor = -1e30
slots_per_step = 4


def score_rows(queries, row_block):
    return lax.dot_general(
        queries, row_block, (((1,), (1,)), ((), ())), preferred_element_type=jnp.float32
    )


def step_view(values, slot_count):
    return values.reshape(
        (slot_count // slots_per_step, slots_per_step * values.shape[1]) + values.shape[2:]
    )


def slot_stats(row_block, queries, targets, in_use):
    slot_count, trip_count = targets.shape
    active = jnp.broadcast_to(in_use[:, None], (slot_count, trip_count))
    positions = jnp.arange(row_block.shape[0], dtype=jnp.int32)

    def one_step(inputs):
        step_queries, step_targets = inputs
        scores = score_rows(step_queries, row_block)
        maxima = jnp.max(scores, axis=1)
        masses = jnp.sum(jnp.exp(scores - maxima[:, None]), axis=1)
        is_target = positions[None, :] == step_targets[:, None]
        picked = jnp.sum(jnp.where(is_target, scores, 0.0), axis=1)
        return (maxima, masses, picked)

    maxima, masses, picked = lax.map(
        one_step, (step_view(queries, slot_count), step_view(targets, slot_count))
    )
    maxima = jnp.where(active, maxima.reshape(slot_count, trip_count), negative_floor)
    masses = jnp.where(active, masses.reshape(slot_count, trip_count), 0.0)
    picked = jnp.where(active, picked.reshape(slot_count, trip_count), 0.0)
    return (maxima, masses, picked)


def slot_grads(row_block, queries, targets, in_use, slot_norms):
    slot_count, trip_count = targets.shape
    active = jnp.broadcast_to(in_use[:, None], (slot_count, trip_count))
    positions = jnp.arange(row_block.shape[0], dtype=jnp.int32)

    def one_step(carry, inputs):
        step_queries, step_targets, step_norms, step_active = inputs
        scores = score_rows(step_queries, row_block)
        weights = jnp.exp(scores - step_norms[:, None])
        is_target = (positions[None, :] == step_targets[:, None]).astype(jnp.float32)
        coefficients = jnp.where(step_active[:, None], weights - is_target, 0.0).astype(
            jnp.bfloat16
        )
        update = lax.dot_general(
            coefficients, step_queries, (((0,), (0,)), ((), ())), preferred_element_type=jnp.float32
        )
        return (carry + update, None)

    initial = jnp.zeros((row_block.shape[0], queries.shape[2]), jnp.float32)
    inputs = (
        step_view(queries, slot_count),
        step_view(targets, slot_count),
        step_view(slot_norms, slot_count),
        step_view(active, slot_count),
    )
    result, unused = lax.scan(one_step, initial, inputs)
    return result


def per_device(
    entities,
    relations,
    candidate_blocks,
    list_lengths,
    head_offsets,
    relation_offsets,
    target_codes,
):
    entity_count = lax.axis_size("entity")
    owner = lax.axis_index("entity")
    table = entities[0]
    block_rows = table.shape[0]
    local_relations = relations.shape[0]
    head_rows = jnp.take(table, head_offsets, axis=0)
    products = jnp.einsum("td,rde->tre", head_rows, relations, precision=lax.Precision.HIGHEST)
    selector = (
        relation_offsets[:, None] == jnp.arange(local_relations, dtype=jnp.int32)[None, :]
    ).astype(jnp.float32)
    query = jnp.sum(products * selector[:, :, None], axis=1).astype(jnp.bfloat16)
    gathered, all_codes = (
        lax.all_gather(query[None], "entity", axis=0, tiled=True),
        lax.all_gather(target_codes[None], "entity", axis=0, tiled=True),
    )
    lengths = list_lengths[0]
    entry_index = jnp.arange(candidate_blocks.shape[1], dtype=jnp.int32)
    counted = entry_index[None, :] < lengths[:, None]
    listed = jnp.any(counted & (candidate_blocks == owner), axis=1)
    ranking = jnp.cumsum(listed.astype(jnp.int32)) - 1
    capacity = min(CAP, entity_count)
    slot_index = jnp.arange(capacity, dtype=jnp.int32)
    set_numbers = jnp.arange(entity_count, dtype=jnp.int32)
    matches = listed[None, :] & (ranking[None, :] == slot_index[:, None])
    slot_set = jnp.sum(jnp.where(matches, set_numbers[None, :], 0), axis=1)
    slot_used = jnp.any(matches, axis=1)
    slot_queries = jnp.take(gathered, slot_set, axis=0)
    slot_codes = jnp.take(all_codes, slot_set, axis=0)
    slot_lists = jnp.take(candidate_blocks, slot_set, axis=0)
    slot_lengths = jnp.take(lengths, slot_set)
    chosen = slot_codes // block_rows % slot_lengths[:, None]
    target_block = jnp.sum(
        jnp.where(chosen[:, :, None] == entry_index[None, None, :], slot_lists[:, None, :], 0),
        axis=2,
    )
    slot_targets = jnp.where(target_block == owner, slot_codes % block_rows, -1)
    rounded_table = table.astype(jnp.bfloat16)
    maxima, masses, picked = slot_stats(rounded_table, slot_queries, slot_targets, slot_used)
    safe_rank = jnp.clip(ranking, 0, capacity - 1)
    set_max = jnp.where(listed[:, None], jnp.take(maxima, safe_rank, axis=0), negative_floor)
    set_mass = jnp.where(listed[:, None], jnp.take(masses, safe_rank, axis=0), 0.0)
    set_target = jnp.where(listed[:, None], jnp.take(picked, safe_rank, axis=0), 0.0)
    top_max = lax.pmax(set_max.astype(jnp.bfloat16), "entity").astype(set_max.dtype)
    scaled_mass = set_mass * jnp.exp(set_max - top_max)
    top_mass, top_target = lax.psum((scaled_mass, set_target), "entity")
    log_norm = top_max + jnp.log(top_mass)
    loss = lax.dynamic_index_in_dim(log_norm - top_target, owner, 0, keepdims=False)
    slot_norms = jnp.take(log_norm, slot_set, axis=0)
    gradient = lax.psum_scatter(
        slot_grads(rounded_table, slot_queries, slot_targets, slot_used, slot_norms),
        "dp",
        scatter_dimension=0,
        tiled=True,
    )
    return (loss, gradient[None])


def solution(mesh):
    return jax.shard_map(
        per_device,
        mesh=mesh,
        in_specs=(
            P("entity", None, None),
            P("entity", None, None),
            P("dp", None),
            P("dp", None),
            P(("dp", "entity")),
            P(("dp", "entity")),
            P(("dp", "entity")),
        ),
        out_specs=(P(("dp", "entity")), P("entity", "dp", None)),
        check_vma=False,
    )
```

profile of v0, /device:TPU:32, one launch (start us, length us, event | category | flops | bytes accessed | tf_op | source)
XLA Modules:
  0.0 627.7 jit_solution(7090872939743737753)
XLA Ops:
  7.2 0.0 copy-start
  7.2 0.0 all-gather.5.cloned.1.call-start
  7.2 0.7 compare_select_fusion.5
  8.0 0.7 compare_and_fusion.2
  8.6 0.7 fusion.32
  9.3 2.9 gather_fusion
  12.2 0.0 copy-done
  12.2 1.4 fusion.15
  13.6 0.0 all-gather.5.cloned.1.call-update
  13.6 0.0 all-reduce.3.cloned.1.call-start
  13.7 0.8 copy.18
  14.5 0.7 fusion.31
  15.2 0.1 copy.17
  15.3 0.1 reduce-window.7
  15.4 0.1 add_reduce_fusion
  15.5 0.1 select_reduce_fusion.2
  15.6 0.1 reduce_sum.50
  15.7 0.1 broadcast_bitcast_fusion.1
  15.8 1.3 gather_fusion.3
  17.2 0.6 gather_fusion.4
  17.7 40.9 %all-gather.2 = s32[64,1,128]{2,1,0:T(1,128)S(1)} all-gather(s32[1,1,128]{2,1,0:T(1,128)} %bitcast.89), channel_id=3, replica_groups=mesh['dp'=4,'entity'=64] {'entity'}, dimensions={0}, use_global_device_ids=true | all-gather | bytes 33280 | tf_op jit(solution)/shard_map/all_gather | solution.py:99
  58.6 0.6 gather_fusion.2
  59.2 0.1 broadcast_select_fusion.4
  59.3 0.2 add_select_fusion.1
  59.5 0.1 select_reduce_fusion.1
  59.6 0.1 fusion.28
  59.7 0.1 broadcast_in_dim.226
  59.9 2.4 bitcast_convert_fusion
  62.3 32.3 %all-gather.5.cloned.1.call-done = bf16[8192,256]{1,0:T(8,128)(2,1)} async-done(((bf16[128,256]{1,0:T(8,128)(2,1)}), bf16[8192,256]{1,0:T(8,128)(2,1)}) %all-gather.5.cloned.1.call-update) | async-done | bytes 4194320 | tf_op jit(solution)/shard_map/all_gather | solution.py:98
  94.6 3.7 gather_fusion.1
  98.2 2.3 bitcast_select_fusion
  100.5 31.7 %while.26 = (s32[]{:T(128)}, f32[3,512]{1,0:T(4,128)S(1)}, f32[3,512]{1,0:T(4,128)S(1)}, f32[3,512]{1,0:T(4,128)S(1)}, bf16[3,512,256]{2,1,0:T(8,128)(2,1)}, /*i...) while((s32[]{:T(128)}, f32[3,512]{1,0:T(4,128)S(1)}, ...), condition=%wide.region_10.11_spmd.clone, body=%wide.region_6.10_spmd.clone.sunk | while | flops 1086323200 | bytes 19163256 | solution.py:39
  100.5 5.5 fusion.46
  106.0 4.9 select_reduce_fusion.4
  111.0 0.1 dynamic_update_slice.17
  111.0 0.1 dynamic_update_slice.18
  111.1 5.5 fusion.46
  116.6 4.9 select_reduce_fusion.4
  121.6 0.1 dynamic_update_slice.17
  121.6 0.1 dynamic_update_slice.18
  121.7 5.5 fusion.46
  127.2 4.9 select_reduce_fusion.4
  132.1 0.1 dynamic_update_slice.17
  132.2 0.1 dynamic_update_slice.18
  132.3 0.1 broadcast_select_fusion.2
  132.4 0.6 gather_fusion.6
  133.0 0.1 fusion.22
  133.1 231.5 %pmax.7 = bf16[64,128]{1,0:T(8,128)(2,1)S(1)} all-reduce(bf16[64,128]{1,0:T(8,128)(2,1)S(1)} %fusion.22), channel_id=1, replica_groups=mesh['dp'=4,'entity'=64] {'entity'}, use_global_device_ids=true, to_apply=%region_11.13 | all-reduce | flops 8192 | bytes 32768 | tf_op jit(solution)/shard_map/pmax | solution.py:128
  364.6 0.6 gather_fusion.7
  365.2 0.6 gather_fusion.8
  365.8 0.7 fusion.21
  366.5 0.0 all-reduce.3.cloned.1.call-update
  366.5 0.0 reduce-scatter.2.cloned.1.call-start
  366.6 0.1 broadcast_bitcast_fusion
  366.6 181.4 %all-reduce.3.cloned.1.call-done = (f32[64,128]{1,0:T(8,128)}, f32[64,128]{1,0:T(8,128)}) async-done(((f32[64,128]{1,0:T(8,128)}, f32[64,128]{1,0:T(8,128)}), (f32[64,128]{1,0:T(8,128)}, f32[64,128]{1,0:T(8,128)})) %all-reduce.3.cloned.1.call-update) | async-done | bytes 65552 | tf_op jit(solution)/shard_map/psum | solution.py:130
  548.0 0.8 convert_add_fusion
  548.8 0.6 gather_fusion.5
  549.4 23.7 %while.27 = (s32[]{:T(128)}, f32[4096,256]{1,0:T(8,128)}, pred[3,512]{1,0:T(4,128)(4,1)S(1)}, bf16[3,512,256]{2,1,0:T(8,128)(2,1)}, bf16[4096,256]{1,0:T(8,128)(...) while((s32[]{:T(128)}, f32[4096,256]{1,0:T(8,128)}, ...), condition=%wide.region_15.17_spmd.clone, body=%wide.region_14.16_spmd.clone.sunk | while | flops 2162163712 | bytes 11025530 | solution.py:73
  549.5 7.0 %convolution_add_fusion.2 = f32[4096,256]{1,0:T(8,128)} fusion(f32[4096,256]{1,0:T(8,128)} %get-tuple-element.310, pred[]{:T(512)S(6)} %compare.11, bf16[4096,256]{1,0:T(8,128)(2,1)S(1)} %get-tuple-element.322, s32[512]{0:T(512)S(1)} %bitcast.86, f32[512]{0:T(512)S(1)} %bitcast.87, pred[512]{0:T(512)(128)(4,1)S(1)} %dynamic-slice_reduce_fusion.2, ...), kind=kOutput, calls=%fused_computation.21.clone.1 | convolution fusion | flops 2162163712 | bytes 11016192 | tf_op jit(solution)/shard_map/while/body/eval_jaxpr/dot_general | solution.py:61
  556.5 8.3 %convolution_add_fusion.2 = f32[4096,256]{1,0:T(8,128)} fusion(f32[4096,256]{1,0:T(8,128)} %get-tuple-element.310, pred[]{:T(512)S(6)} %compare.11, bf16[4096,256]{1,0:T(8,128)(2,1)S(1)} %get-tuple-element.322, s32[512]{0:T(512)S(1)} %bitcast.86, f32[512]{0:T(512)S(1)} %bitcast.87, pred[512]{0:T(512)(128)(4,1)S(1)} %dynamic-slice_reduce_fusion.2, ...), kind=kOutput, calls=%fused_computation.21.clone.1 | convolution fusion | flops 2162163712 | bytes 11016192 | tf_op jit(solution)/shard_map/while/body/eval_jaxpr/dot_general | solution.py:61
  564.9 8.3 %convolution_add_fusion.2 = f32[4096,256]{1,0:T(8,128)} fusion(f32[4096,256]{1,0:T(8,128)} %get-tuple-element.310, pred[]{:T(512)S(6)} %compare.11, bf16[4096,256]{1,0:T(8,128)(2,1)S(1)} %get-tuple-element.322, s32[512]{0:T(512)S(1)} %bitcast.86, f32[512]{0:T(512)S(1)} %bitcast.87, pred[512]{0:T(512)(128)(4,1)S(1)} %dynamic-slice_reduce_fusion.2, ...), kind=kOutput, calls=%fused_computation.21.clone.1 | convolution fusion | flops 2162163712 | bytes 11016192 | tf_op jit(solution)/shard_map/while/body/eval_jaxpr/dot_general | solution.py:61
  573.1 0.0 reduce-scatter.2.cloned.1.call-update
  573.2 1.2 fusion.34
  574.4 46.8 %reduce-scatter.2.cloned.1.call-done = f32[1024,256]{1,0:T(8,128)} async-done(((f32[4096,256]{1,0:T(8,128)}), f32[1024,256]{1,0:T(8,128)}) %reduce-scatter.2.cloned.1.call-update) | async-done | bytes 1048592 | tf_op jit(solution)/shard_map/reduce_scatter | solution.py:134
  (38 shorter events, 0.4 us)
Async XLA Ops:
  7.2 5.1 copy-start
  7.2 87.4 %all-gather.5.cloned.1.call-start = ((), (), s32[]{:S(2)}) async-start(), calls=%async_computation.2 | async-start | bytes 4259840 | tf_op jit(solution)/shard_map/all_gather | solution.py:98
  13.6 534.4 %all-reduce.3.cloned.1.call-start = ((), (), s32[]{:S(2)}) async-start(), calls=%async_computation.3 | async-start | bytes 131072 | tf_op jit(solution)/shard_map/psum | solution.py:130
  366.5 254.7 %reduce-scatter.2.cloned.1.call-start = ((), (), s32[]{:S(2)}) async-start(), calls=%async_computation.1 | async-start | bytes 5242880 | tf_op jit(solution)/shard_map/reduce_scatter | solution.py:134
Sparse Core Ops, SparseCore 0:
  13.8 80.7 all-gather.4
  366.6 181.3 all-reduce.2
  573.3 47.8 reduce-scatter.1
where the time goes:
time: 630 us; the launch traced here: 628 us
  blocking collectives  272 us (43%)
  waiting for transfers between devices  261 us (41%)
  matrix products  41.3 us (7%)
  other arithmetic  26 us (4%)
  between operations  13.9 us (2%)
  local copies, waits for them, and re-layouts  13.3 us (2%)
    pmax x1, blocking collectives, per_device(): lax.pmax(set_max.astype(jnp.bfloat16), 'entity').astype(set_max.dtype)  232 us
    psum x1, waiting for transfers between devices, per_device(): top_mass, top_target = lax.psum((scaled_mass, set_target), 'entity')  181 us
    reduce_scatter x1, waiting for transfers between devices, per_device(): lax.psum_scatter(slot_grads(rounded_table, slot_queries, slot_targets, sl...  46.8 us
    all_gather x1, blocking collectives, per_device(): lax.all_gather(target_codes[None], 'entity', axis=0, tiled=True)  40.9 us
    all_gather x1, waiting for transfers between devices, per_device(): lax.all_gather(query[None], 'entity', axis=0, tiled=True)  32.3 us
    dot_general x3, matrix products, one_step(): lax.dot_general(coefficients, step_queries, (((0,), (0,)), ((), ())), pre...  23.6 us
    dot_general x3, matrix products, score_rows(): lax.dot_general(queries, row_block, (((1,), (1,)), ((), ())), preferred_e...  16.4 us
    reduce_sum x3, other arithmetic, one_step(): picked = jnp.sum(jnp.where(is_target, scores, 0.0), axis=1)  14.8 us
  transfers between devices with their start and end apart: 3, of which 3 were waited for; matrix products, arithmetic and copies ran while one was open for 1% of the time, Pallas kernels for 0%

commit v1 on v0

v1 whole, which is shorter than its diff:
```python
import jax
import jax.numpy as jnp
from jax import lax
from jax.experimental import pallas as pl
from jax.experimental.pallas import tpu as pltpu
from jax.sharding import PartitionSpec as P

f32, bf16, i32 = jnp.float32, jnp.bfloat16, jnp.int32
CAP = 12
HALF = CAP // 2
NEG = -1e30
HIGH = lax.Precision.HIGHEST
VMEM_BYTES = 56 * 1024 * 1024


def iota(shape, axis):
    return lax.broadcasted_iota(i32, shape, axis)


def dot(a, b, ca=1, cb=0, precision=None):
    return lax.dot_general(
        a, b, (((ca,), (cb,)), ((), ())), precision=precision, preferred_element_type=f32
    )


def whole(shape):
    return pl.BlockSpec(shape, lambda *_: (0,) * len(shape))


def query_kernel(heads, table, relations, kinds, codes, lists, lengths, out, ranks, rows, sem):
    count = rows.shape[0]
    sets = lists.shape[0]

    def fetch(n, carry):
        pltpu.make_async_copy(
            table.at[pl.ds(heads[n], 1), :], rows.at[pl.ds(n, 1), :], sem
        ).start()
        return carry

    lax.fori_loop(0, count, fetch, 0, unroll=8)
    listed_t = dot(
        lists[...].astype(f32).astype(bf16),
        (iota((sets, sets), 0) == iota((sets, sets), 1)).astype(f32).astype(bf16),
        0,
        0,
    )
    entry = iota(listed_t.shape, 0)
    listed_t = jnp.where(entry < lengths[...], listed_t, -1.0)
    block = iota((sets, sets), 0).astype(f32)
    listed = jnp.zeros((sets, sets), f32)
    for k in range(listed_t.shape[0]):
        listed = jnp.where(listed_t[k : k + 1, :] == block, 1.0, listed)
    before = (iota((sets, sets), 0) < iota((sets, sets), 1)).astype(f32).astype(bf16)
    rank = dot(listed.astype(bf16), before)
    ranks[...] = jnp.where(listed > 0.0, rank, -1.0)
    diagonal = iota((count, count), 0) == iota((count, count), 1)
    kind = jnp.sum(jnp.where(diagonal, kinds[...].astype(f32), 0.0), axis=1, keepdims=True)
    pltpu.make_async_copy(table.at[pl.ds(0, count), :], rows, sem).wait()
    head = rows[...]
    query = jnp.zeros((count, relations.shape[2]), f32)
    for r in range(relations.shape[0]):
        product = dot(head, relations[r], precision=HIGH)
        query = jnp.where(kind == r, product, query)
    query = query.astype(bf16)
    total, width = out.shape[0], query.shape[1]
    row, column = iota((total, width), 0), iota((total, width), 1)
    pick = (row % 8 < 4) & (row // 8 * 4 + row % 8 == column)
    spread = dot(pick.astype(f32).astype(bf16), query, 1, 1)
    row = iota(spread.shape, 0) % 8
    code = codes[...]
    spread = jnp.where(row == 4, (code // 128).astype(f32), spread)
    spread = jnp.where(row == 5, (code % 128).astype(f32), spread)
    out[...] = spread.astype(bf16)


def pack_kernel(me, ranks, held, lists, lengths, out, targets, sets_rows):
    sets = ranks.shape[0]
    size = held.shape[0]
    rank = ranks[...]
    up = (iota((size, sets), 0) // 8 == iota((size, sets), 1)).astype(f32).astype(bf16)
    wide = dot(up, rank.astype(bf16))
    wide = dot(wide.astype(bf16), up, 1, 1)
    row, column = iota((size, size), 0), iota((size, size), 1)
    wide = jnp.where(row % 4 == column % 8, wide - (row % 8 // 4 * HALF).astype(f32), NEG)
    listed = dot(dot(up, (rank >= 0.0).astype(f32).astype(bf16)).astype(bf16), up, 1, 1) > 0.5
    wide = jnp.where(listed, wide, NEG)
    values = held[...]
    lanes = values.shape[1]
    for i in range(HALF):
        chosen = (wide == float(i)).astype(f32).astype(bf16)
        out[:, i * lanes : (i + 1) * lanes] = dot(chosen, values).astype(bf16)
    mine = ranks[pl.ds(me[0], 1), :]
    slots = targets.shape[0]
    slot = iota((slots, sets), 0).astype(f32)
    taken = mine == slot
    onehot = taken.astype(f32).astype(bf16)
    expanded = dot(onehot, up, 1, 1)
    column = iota(expanded.shape, 1) % 8
    high = dot(jnp.where(column == 4, expanded, 0.0).astype(bf16), values).astype(i32)
    low = dot(jnp.where(column == 5, expanded, 0.0).astype(bf16), values).astype(i32)
    code = high * 128 + low
    used = jnp.sum(taken.astype(f32), axis=1, keepdims=True) > 0.5
    length = jnp.sum(jnp.where(taken, lengths[...].astype(f32), 0.0), axis=1, keepdims=True).astype(i32)
    slot_lists = dot(onehot, lists[...].astype(f32).astype(bf16)).astype(i32)
    entry = code // sets_rows
    for _ in range(3):
        entry = jnp.where(entry >= length, entry - length, entry)
    block = jnp.full(code.shape, -1, i32)
    for k in range(slot_lists.shape[1]):
        block = jnp.where(entry == k, slot_lists[:, k : k + 1], block)
    here = (block == me[0]) & used
    targets[...] = jnp.where(here, code % sets_rows, -1)


def stats_kernel(
    me, ranks, received, table, targets, query_t, query, out, top_s, sum_s, tgt_s
):
    step = pl.program_id(0)
    pairs = CAP // 2
    width = 256
    tile = table.shape[0]

    @pl.when(step == 0)
    def _():
        size = received.shape[0]
        half = size // 2
        lanes = received.shape[1]
        values = received[...]
        row, column = iota((half, size), 0), iota((half, size), 1)
        for h in range(2):
            pick = (row // 4 * 8 + h * 4 + row % 4 == column).astype(f32).astype(bf16)
            query_t[:, h * lanes : (h + 1) * lanes] = dot(pick, values).astype(bf16)
            query[h * lanes : (h + 1) * lanes, :] = dot(values, pick, 0, 1).astype(bf16)
        top_s[...] = jnp.full(top_s.shape, NEG, f32)
        sum_s[...] = jnp.zeros(sum_s.shape, f32)
        tgt_s[...] = jnp.zeros(tgt_s.shape, f32)

    rows = table[...].astype(bf16)
    place = iota((tile, width), 0) + step * tile
    for p in range(pairs):
        columns = slice(p * width, (p + 1) * width)
        score = dot(rows, query_t[:, columns])
        target = jnp.concatenate([targets[2 * p : 2 * p + 1, :], targets[2 * p + 1 : 2 * p + 2, :]], axis=1)
        grouped = score.reshape(tile // 8, 8, width)
        old = top_s[:, columns]
        top = jnp.maximum(old, jnp.max(grouped, axis=0))
        mass = jnp.sum(jnp.exp(grouped - top[None]), axis=0)
        sum_s[:, columns] = sum_s[:, columns] * jnp.exp(old - top) + mass
        top_s[:, columns] = top
        hit = jnp.where(place == target, score, 0.0).reshape(tile // 8, 8, width)
        tgt_s[:, columns] = tgt_s[:, columns] + jnp.sum(hit, axis=0)

    @pl.when(step == pl.num_programs(0) - 1)
    def _():
        top = top_s[...]
        best = jnp.max(top, axis=0, keepdims=True)
        mass = jnp.sum(sum_s[...] * jnp.exp(top - best), axis=0, keepdims=True)
        local = best + jnp.log(mass)
        picked = jnp.sum(tgt_s[...], axis=0, keepdims=True)
        blank = jnp.zeros((4, 128), f32)
        stacked = jnp.concatenate(
            [local[:, i * 128 : (i + 1) * 128] for i in range(CAP)]
            + [blank]
            + [picked[:, i * 128 : (i + 1) * 128] for i in range(CAP)]
            + [blank],
            axis=0,
        )
        sets = ranks.shape[0]
        total = out.shape[0]
        rank = ranks[...]
        up = (iota((total, sets), 0) // 16 == iota((total, sets), 1)).astype(f32)
        wide = dot(up.astype(bf16), rank.astype(bf16))
        slot = iota((total, sets), 0) % 16
        shared = (wide == slot.astype(f32)) & (slot < CAP)
        shared = shared | (((slot == CAP) | (slot == CAP + 1)) & (up > 0.5))
        mine = ranks[pl.ds(me[0], 1), :]
        owned = mine == (iota((32, sets), 0) % 16).astype(f32)
        match = dot(shared.astype(f32).astype(bf16), owned.astype(f32).astype(bf16), 1, 1)
        slot, source = iota((total, 32), 0) % 16, iota((total, 32), 1)
        match = jnp.where((slot == CAP + 1) == (source >= 16), match, 0.0)
        picked_rows = dot(match, stacked, precision=HIGH)
        present = dot(match.astype(bf16), jnp.ones((32, 128), bf16))
        missing = jnp.where(iota((total, 128), 0) % 16 == CAP + 1, 0.0, NEG)
        out[...] = jnp.where(present > 0.5, picked_rows, missing)


def merge_kernel(received, norms, loss):
    values = received[...]
    best = jnp.max(values, axis=0)
    mass = jnp.sum(jnp.exp(values - best[None]), axis=0)
    norm = best + jnp.log(mass)
    norms[...] = jnp.where(best <= 0.5 * NEG, -NEG, norm)
    target = jnp.sum(values[:, CAP + 1, :], axis=0, keepdims=True)
    loss[...] = norm[CAP : CAP + 1, :] - target


def grads_kernel(first, norms, targets, table, query_t, query, out, coefficients):
    step = pl.program_id(0)
    tile = table.shape[0]
    width = 256
    rows = table[...].astype(bf16)
    place = iota((tile, width), 0) + (first[0] * (pl.num_programs(0) * tile) + step * tile)
    for p in range(CAP // 2):
        columns = slice(p * width, (p + 1) * width)
        score = dot(rows, query_t[:, columns])
        norm = jnp.concatenate([norms[2 * p : 2 * p + 1, :], norms[2 * p + 1 : 2 * p + 2, :]], axis=1)
        target = jnp.concatenate([targets[2 * p : 2 * p + 1, :], targets[2 * p + 1 : 2 * p + 2, :]], axis=1)
        weight = jnp.exp(score - norm)
        coefficients[:, columns] = jnp.where(place == target, weight - 1.0, weight).astype(bf16)
    out[...] = dot(coefficients[...], query[...]).astype(out.dtype)


def per_device(
    entities,
    relations,
    candidate_blocks,
    list_lengths,
    head_offsets,
    relation_offsets,
    target_codes,
):
    owners = lax.axis_size("entity")
    groups = lax.axis_size("dp")
    table = entities[0]
    block_rows, depth = table.shape
    count = head_offsets.shape[0]
    me = lax.axis_index("entity").astype(i32).reshape(1)
    group = lax.axis_index("dp").astype(i32)
    smem = pl.BlockSpec(memory_space=pltpu.SMEM)
    params = pltpu.CompilerParams(vmem_limit_bytes=VMEM_BYTES)
    kinds = relation_offsets.reshape(1, count)
    codes = target_codes.reshape(1, count)

    spread, ranks = pl.pallas_call(
        query_kernel,
        out_shape=(
            jax.ShapeDtypeStruct((owners * 8, count), bf16),
            jax.ShapeDtypeStruct((owners, owners), f32),
        ),
        in_specs=[smem, pl.BlockSpec(memory_space=pl.ANY)] + [pl.BlockSpec(memory_space=pltpu.VMEM)] * 5,
        scratch_shapes=[pltpu.VMEM((count, depth), f32), pltpu.SemaphoreType.DMA],
        compiler_params=params,
        name="query",
    )(head_offsets, table, relations, kinds, codes, candidate_blocks, list_lengths)

    held = lax.all_to_all(spread.reshape(owners, 8, count), "entity", 0, 0, tiled=True)

    def pack(*refs):
        pack_kernel(*refs, block_rows)

    packed, targets = pl.pallas_call(
        pack,
        out_shape=(
            jax.ShapeDtypeStruct((owners * 8, HALF * count), bf16),
            jax.ShapeDtypeStruct((16, count), i32),
        ),
        in_specs=[smem] + [pl.BlockSpec(memory_space=pltpu.VMEM)] * 4,
        compiler_params=params,
        name="pack",
    )(me, ranks, held.reshape(owners * 8, count), candidate_blocks, list_lengths)

    received = lax.all_to_all(packed.reshape(owners, 8, HALF * count), "entity", 0, 0, tiled=True)

    tile = 1024
    query_t, query, local = pl.pallas_call(
        stats_kernel,
        grid=(block_rows // tile,),
        out_shape=(
            jax.ShapeDtypeStruct((depth, CAP * count), bf16),
            jax.ShapeDtypeStruct((CAP * count, depth), bf16),
            jax.ShapeDtypeStruct((owners * 16, count), f32),
        ),
        in_specs=[
            smem,
            whole((owners, owners)),
            whole((owners * 8, HALF * count)),
            pl.BlockSpec((tile, depth), lambda s: (s, 0)),
            whole((16, count)),
        ],
        out_specs=[whole((depth, CAP * count)), whole((CAP * count, depth)), whole((owners * 16, count))],
        scratch_shapes=[pltpu.VMEM((8, CAP * count), f32)] * 3,
        compiler_params=params,
        name="stats",
    )(me, ranks, received.reshape(owners * 8, HALF * count), table, targets)

    shared = lax.all_to_all(local.reshape(owners, 16, count), "entity", 0, 0, tiled=True)

    norms, loss = pl.pallas_call(
        merge_kernel,
        out_shape=(jax.ShapeDtypeStruct((16, count), f32), jax.ShapeDtypeStruct((1, count), f32)),
        compiler_params=params,
        name="merge",
    )(shared)

    quarter = block_rows // groups
    tile = 512

    def grads(which, dtype):
        return pl.pallas_call(
            grads_kernel,
            grid_spec=pltpu.PrefetchScalarGridSpec(
                num_scalar_prefetch=1,
                grid=(quarter // tile,),
                in_specs=[
                    pl.BlockSpec((16, count), lambda s, w: (0, 0)),
                    pl.BlockSpec((16, count), lambda s, w: (0, 0)),
                    pl.BlockSpec((tile, depth), lambda s, w: (w[0] * (quarter // tile) + s, 0)),
                    pl.BlockSpec((depth, CAP * count), lambda s, w: (0, 0)),
                    pl.BlockSpec((CAP * count, depth), lambda s, w: (0, 0)),
                ],
                out_specs=pl.BlockSpec((tile, depth), lambda s, w: (s, 0)),
                scratch_shapes=[pltpu.VMEM((tile, CAP * count), bf16)],
            ),
            out_shape=jax.ShapeDtypeStruct((quarter, depth), dtype),
            compiler_params=params,
            name="grads",
        )(which.reshape(1), norms, targets, table, query_t, query)

    arrived = []
    for shift in (2, 1, 3):
        part = grads((group + shift) % groups, bf16)
        arrived.append(lax.ppermute(part, "dp", [(i, (i + shift) % groups) for i in range(groups)]))
    gradient = grads(group, f32)
    for part in arrived:
        gradient = gradient + part.astype(f32)
    return (loss.reshape(count), gradient[None])


def solution(mesh):
    return jax.shard_map(
        per_device,
        mesh=mesh,
        in_specs=(
            P("entity", None, None),
            P("entity", None, None),
            P("dp", None),
            P("dp", None),
            P(("dp", "entity")),
            P(("dp", "entity")),
            P(("dp", "entity")),
        ),
        out_specs=(P(("dp", "entity")), P("entity", "dp", None)),
        check_vma=False,
    )
```

time: 630 us -> 146 us (0.23)
  blocking collectives: 272 us -> 28.6 us
  waiting for transfers between devices: 261 us -> 43.5 us
  Pallas kernels: 0 us -> 41.4 us
  matrix products: 41.3 us -> 0 us
  starting transfers between devices: 0.12 us -> 24.7 us
  other arithmetic: 26 us -> 2.4 us
  between operations: 13.9 us -> 0.7 us
  local copies, waits for them, and re-layouts: 13.3 us -> 2.82 us
    pmax x1 -> x0, blocking collectives: 232 us -> none  [per_device(): lax.pmax(set_max.astype(jnp.bfloat16), 'entity').astype(set_max.dtype)]
    psum x1 -> x0, waiting for transfers between devices: 181 us -> none  [per_device(): top_mass, top_target = lax.psum((scaled_mass, set_target), 'entity')]
    reduce_scatter x1 -> x0, waiting for transfers between devices: 46.8 us -> none  [per_device(): lax.psum_scatter(slot_grads(rounded_table, slot_queries, slot_targets, sl...]
    pallas_call x0 -> x8, Pallas kernels: none -> 41.4 us  [the longest x4 18.2 us: grads(): pl.pallas_call(grads_kernel, grid_spec=pltpu.PrefetchScalarGridSpec(num_s...]
    dot_general x7 -> x0, matrix products: 41.3 us -> none  [the longest x3 23.6 us: one_step(): lax.dot_general(coefficients, step_queries, (((0,), (0,)), ((), ())), pre...]
    all_gather x1 -> x0, blocking collectives: 40.9 us -> none  [per_device(): lax.all_gather(target_codes[None], 'entity', axis=0, tiled=True)]
    all_gather x1 -> x0, waiting for transfers between devices: 32.3 us -> none  [per_device(): lax.all_gather(query[None], 'entity', axis=0, tiled=True)]
    all_to_all x0 -> x1, blocking collectives: none -> 28.6 us  [per_device(): lax.all_to_all(packed.reshape(owners, 8, HALF * count), 'entity', 0, 0, t...]
  transfers between devices with their start and end apart: 3 -> 5, of which waited for: 3 -> 5; matrix products, arithmetic and copies ran while one was open for 1% -> 0% of each run, Pallas kernels for 0% -> 3%
where the time goes in v1:
time: 146 us; the launch traced here: 144 us
  waiting for transfers between devices  43.5 us (30%)
  Pallas kernels  41.4 us (28%)
  blocking collectives  28.6 us (20%)
  starting transfers between devices  24.7 us (17%)
  local copies, waits for them, and re-layouts  2.82 us (2%)
  other arithmetic  2.4 us (2%)
    all_to_all x1, blocking collectives, per_device(): lax.all_to_all(packed.reshape(owners, 8, HALF * count), 'entity', 0, 0, t...  28.6 us
    pallas_call x4, Pallas kernels, grads(): pl.pallas_call(grads_kernel, grid_spec=pltpu.PrefetchScalarGridSpec(num_s...  18.2 us
    all_to_all x1, waiting for transfers between devices, per_device(): lax.all_to_all(local.reshape(owners, 16, count), 'entity', 0, 0, tiled=True)  16.7 us
    ppermute x3, waiting for transfers between devices, per_device(): lax.ppermute(part, 'dp', [(i, (i + shift) % groups) for i in range(groups)])  16.6 us
    pallas_call x1, Pallas kernels, per_device(): pl.pallas_call(stats_kernel, grid=(block_rows // tile,), out_shape=(jax.S...  13.8 us
    all_to_all x1, starting transfers between devices, per_device(): lax.all_to_all(spread.reshape(owners, 8, count), 'entity', 0, 0, tiled=True)  11.6 us
    all_to_all x1, waiting for transfers between devices, per_device(): lax.all_to_all(spread.reshape(owners, 8, count), 'entity', 0, 0, tiled=True)  10.2 us
    all_to_all x1, starting transfers between devices, per_device(): lax.all_to_all(local.reshape(owners, 16, count), 'entity', 0, 0, tiled=True)  6.68 us
  transfers between devices with their start and end apart: 5, of which 5 were waited for; matrix products, arithmetic and copies ran while one was open for 0% of the time, Pallas kernels for 3%

profile of v1, /device:TPU:32, one launch (start us, length us, event | category | flops | bytes accessed | tf_op | source)
XLA Modules:
  0.0 144.1 jit_solution(14101886285303525080)
XLA Ops:
  0.6 1.4 copy.9.lists.refs_3_
  2.0 4.3 %query.1 = (bf16[512,128]{1,0:T(8,128)(2,1)}, f32[64,64]{1,0:T(8,128)}) custom-call(s32[128]{0:T(128)} %heads.1, f32[4096,256]{1,0:T(8,128)} %bitcast.16, f32[4,256,256]{2,1,0:T(8,128)} %relations.1, s32[1,128]{1,0:T(1,128)} %bitcast.27, s32[1,128]{1,0:T(1,128)} %bitcast.28, s32[64,8]{1,0:T(8,128)} %copy.9.lists.refs_3_, s32[1,64]{1,0:T(1,128)} %refs_4_.1), custom_call_target="tpu_custom_call" | custom-call | tf_op jit(solution)/shard_map/query/pallas_call | solution.py:234
  6.3 11.6 %all-to-all-start = ((bf16[64,8,128]{2,1,0:T(8,128)(2,1)}), bf16[64,8,128]{2,1,0:T(8,128)(2,1)S(1)}, u32[]{:S(2)}, u32[]{:S(2)}) async-start(bf16[64,8,128]{2,1,0:T(8,128)(2,1)} %bitcast.26), calls=%async_computation | async-start | bytes 262144 | tf_op jit(solution)/shard_map/all_to_all | solution.py:246
  17.9 10.2 %all-to-all-done = bf16[64,8,128]{2,1,0:T(8,128)(2,1)S(1)} async-done(((bf16[64,8,128]{2,1,0:T(8,128)(2,1)}), bf16[64,8,128]{2,1,0:T(8,128)(2,1)S(1)}, u32[]{:S(2)}, u32[]{:S(2)}) %all-to-all-start) | async-done | bytes 131104 | tf_op jit(solution)/shard_map/all_to_all | solution.py:246
  28.1 0.0 copy-start.3
  28.1 0.6 copy-done.3
  28.7 3.4 %pack.1 = (bf16[512,768]{1,0:T(8,128)(2,1)}, s32[16,128]{1,0:T(8,128)}) custom-call(s32[1]{0:T(128)} %bitcast.refs_0_.me, f32[64,64]{1,0:T(8,128)} %get-tuple-element.11.refs_1_.ranks, bf16[512,128]{1,0:T(8,128)(2,1)} %bitcast.25, s32[64,8]{1,0:T(8,128)} %copy.9.lists.refs_3_, s32[1,64]{1,0:T(1,128)} %refs_4_.1), custom_call_target="tpu_custom_call" | custom-call | tf_op jit(solution)/shard_map/pack/pallas_call | solution.py:251
  32.1 28.6 %all_to_all.15 = bf16[64,8,768]{2,1,0:T(8,128)(2,1)} all-to-all(bf16[64,8,768]{2,1,0:T(8,128)(2,1)} %bitcast.23), channel_id=1, replica_groups=mesh['dp'=4,'entity'=64] {'entity'}, dimensions={0} | all-to-all | bytes 1572864 | tf_op jit(solution)/shard_map/all_to_all | solution.py:262
  60.7 13.8 %stats.1 = (bf16[256,1536]{1,0:T(8,128)(2,1)}, bf16[1536,256]{1,0:T(8,128)(2,1)}, f32[1024,128]{1,0:T(8,128)}) custom-call(s32[1]{0:T(128)} %bitcast.refs_0_.me, f32[64,64]{1,0:T(8,128)} %get-tuple-element.11.refs_1_.ranks, bf16[512,768]{1,0:T(8,128)(2,1)} %bitcast.22, f32[4096,256]{1,0:T(8,128)} %bitcast.17, s32[16,128]{1,0:T(8,128)} %get-tuple-element.14.targets), custom_call_target="tpu_custom_call" | custom-call | tf_op jit(solution)/shard_map/stats/pallas_call | solution.py:265
  74.5 6.7 %all-to-all-start.2 = ((f32[64,16,128]{2,1,0:T(8,128)}), f32[64,16,128]{2,1,0:T(8,128)S(1)}, u32[]{:S(2)}, u32[]{:S(2)}) async-start(f32[64,16,128]{2,1,0:T(8,128)} %bitcast.24), calls=%async_computation.2 | async-start | bytes 1048576 | tf_op jit(solution)/shard_map/all_to_all | solution.py:286
  81.2 16.7 %all-to-all-done.2.received = f32[64,16,128]{2,1,0:T(8,128)S(1)} async-done(((f32[64,16,128]{2,1,0:T(8,128)}), f32[64,16,128]{2,1,0:T(8,128)S(1)}, u32[]{:S(2)}, u32[]{:S(2)}) %all-to-all-start.2) | async-done | bytes 524320 | tf_op jit(solution)/shard_map/all_to_all | solution.py:286
  97.9 0.0 copy-start
  97.9 0.8 copy-done
  98.7 1.8 %merge.1 = (f32[16,128]{1,0:T(8,128)}, f32[1,128]{1,0:T(1,128)}) custom-call(f32[64,16,128]{2,1,0:T(8,128)} %copy-done), custom_call_target="tpu_custom_call" | custom-call | tf_op jit(solution)/shard_map/merge/pallas_call | solution.py:288
  100.5 4.5 %grads.7 = bf16[1024,256]{1,0:T(8,128)(2,1)} custom-call(s32[1]{0:T(128)} %bitcast.13.first, f32[16,128]{1,0:T(8,128)} %get-tuple-element.17.norms, s32[16,128]{1,0:T(8,128)} %get-tuple-element.14.targets, f32[4096,256]{1,0:T(8,128)} %bitcast.18, bf16[256,1536]{1,0:T(8,128)(2,1)} %get-tuple-element.18.query_t, bf16[1536,256]{1,0:T(8,128)(2,1)} %get-tuple-element.19.query), custom_call_target="tpu_custom_call" | custom-call | tf_op jit(solution)/shard_map/grads/pallas_call | solution.py:299
  105.0 4.5 %grads.6 = bf16[1024,256]{1,0:T(8,128)(2,1)} custom-call(s32[1]{0:T(128)} %bitcast.12.first, f32[16,128]{1,0:T(8,128)} %get-tuple-element.17.norms, s32[16,128]{1,0:T(8,128)} %get-tuple-element.14.targets, f32[4096,256]{1,0:T(8,128)} %bitcast.19, bf16[256,1536]{1,0:T(8,128)(2,1)} %get-tuple-element.18.query_t, bf16[1536,256]{1,0:T(8,128)(2,1)} %get-tuple-element.19.query), custom_call_target="tpu_custom_call" | custom-call | tf_op jit(solution)/shard_map/grads/pallas_call | solution.py:299
  109.5 0.0 copy-start.2
  109.5 0.0 copy-start.1
  109.5 4.6 %grads.5 = bf16[1024,256]{1,0:T(8,128)(2,1)} custom-call(s32[1]{0:T(128)} %bitcast.11.first, f32[16,128]{1,0:T(8,128)} %get-tuple-element.17.norms, s32[16,128]{1,0:T(8,128)} %get-tuple-element.14.targets, f32[4096,256]{1,0:T(8,128)} %bitcast.20, bf16[256,1536]{1,0:T(8,128)(2,1)} %get-tuple-element.18.query_t, bf16[1536,256]{1,0:T(8,128)(2,1)} %get-tuple-element.19.query), custom_call_target="tpu_custom_call" | custom-call | tf_op jit(solution)/shard_map/grads/pallas_call | solution.py:299
  114.1 3.2 %collective-permute-start = (bf16[1024,256]{1,0:T(8,128)(2,1)}, bf16[1024,256]{1,0:T(8,128)(2,1)S(1)}, u32[]{:S(2)}, u32[]{:S(2)}) collective-permute-start(bf16[1024,256]{1,0:T(8,128)(2,1)} %grads.5), channel_id=1, source_target_pairs={{0,128},{64,192},{128,0},{192,64},{1,129},{65,193},{129,1},{193,65... | collective-permute-start | bytes 1572872 | tf_op jit(solution)/shard_map/ppermute | solution.py:322
  117.3 0.0 copy-done.2
  117.3 0.7 collective-permute-start.1
  117.9 0.0 copy-done.1
  118.0 2.6 %collective-permute-start.2 = (bf16[1024,256]{1,0:T(8,128)(2,1)S(1)}, bf16[1024,256]{1,0:T(8,128)(2,1)S(1)}, u32[]{:S(2)}, u32[]{:S(2)}) collective-permute-start(bf16[1024,256]{1,0:T(8,128)(2,1)S(1)} %copy-done.1), channel_id=1, source_target_pairs={{0,192},{64,0},{128,64},{192,128},{1,193},{65,1},{129,65},{193,129... | collective-permute-start | bytes 1572872 | tf_op jit(solution)/shard_map/ppermute | solution.py:322
  120.5 4.6 %grads.4 = f32[1024,256]{1,0:T(8,128)} custom-call(s32[1]{0:T(128)} %bitcast.10.first, f32[16,128]{1,0:T(8,128)} %get-tuple-element.17.norms, s32[16,128]{1,0:T(8,128)} %get-tuple-element.14.targets, f32[4096,256]{1,0:T(8,128)} %bitcast.21, bf16[256,1536]{1,0:T(8,128)(2,1)} %get-tuple-element.18.query_t, bf16[1536,256]{1,0:T(8,128)(2,1)} %get-tuple-element.19.query), custom_call_target="tpu_custom_call" | custom-call | tf_op jit(solution)/shard_map/grads/pallas_call | solution.py:299
  125.1 5.5 %collective-permute-done = bf16[1024,256]{1,0:T(8,128)(2,1)S(1)} collective-permute-done((bf16[1024,256]{1,0:T(8,128)(2,1)}, bf16[1024,256]{1,0:T(8,128)(2,1)S(1)}, u32[]{:S(2)}, u32[]{:S(2)}) %collective-permute-start) | collective-permute-done | bytes 524320 | tf_op jit(solution)/shard_map/ppermute | solution.py:322
  130.6 10.7 %collective-permute-done.1 = bf16[1024,256]{1,0:T(8,128)(2,1)S(1)} collective-permute-done((bf16[1024,256]{1,0:T(8,128)(2,1)S(1)}, bf16[1024,256]{1,0:T(8,128)(2,1)S(1)}, u32[]{:S(2)}, u32[]{:S(2)}) %collective-permute-start.1) | collective-permute-done | bytes 524320 | tf_op jit(solution)/shard_map/ppermute | solution.py:322
  141.3 0.4 collective-permute-done.2
  141.7 2.4 %add_bitcast_fusion = f32[1,1024,256]{2,1,0:T(8,128)} fusion(bf16[1024,256]{1,0:T(8,128)(2,1)S(1)} %collective-permute-done.2, bf16[1024,256]{1,0:T(8,128)(2,1)S(1)} %collective-permute-done.1, f32[1024,256]{1,0:T(8,128)} %grads.4, bf16[1024,256]{1,0:T(8,128)(2,1)S(1)} %collective-permute-done), kind=kLoop, calls=%fused_computation | loop fusion | flops 1572864 | bytes 3670016 | tf_op jit(solution)/shard_map/broadcast_in_dim | solution.py:326
Async XLA Ops:
  6.3 21.8 %all-to-all-start = ((bf16[64,8,128]{2,1,0:T(8,128)(2,1)}), bf16[64,8,128]{2,1,0:T(8,128)(2,1)S(1)}, u32[]{:S(2)}, u32[]{:S(2)}) async-start(bf16[64,8,128]{2,1,0:T(8,128)(2,1)} %bitcast.26), calls=%async_computation | async-start | bytes 262144 | tf_op jit(solution)/shard_map/all_to_all | solution.py:246
  28.1 0.7 copy-start.3
  74.5 23.4 %all-to-all-start.2 = ((f32[64,16,128]{2,1,0:T(8,128)}), f32[64,16,128]{2,1,0:T(8,128)S(1)}, u32[]{:S(2)}, u32[]{:S(2)}) async-start(f32[64,16,128]{2,1,0:T(8,128)} %bitcast.24), calls=%async_computation.2 | async-start | bytes 1048576 | tf_op jit(solution)/shard_map/all_to_all | solution.py:286
  97.9 0.8 copy-start
  109.5 7.8 %copy-start.2 = (bf16[1024,256]{1,0:T(8,128)(2,1)S(1)}, bf16[1024,256]{1,0:T(8,128)(2,1)}, u32[]{:S(2)}) copy-start(bf16[1024,256]{1,0:T(8,128)(2,1)} %grads.6) | copy-start | bytes 1572868
  109.5 8.5 %copy-start.1 = (bf16[1024,256]{1,0:T(8,128)(2,1)S(1)}, bf16[1024,256]{1,0:T(8,128)(2,1)}, u32[]{:S(2)}) copy-start(bf16[1024,256]{1,0:T(8,128)(2,1)} %grads.7) | copy-start | bytes 1572868
  114.1 16.5 %collective-permute-start = (bf16[1024,256]{1,0:T(8,128)(2,1)}, bf16[1024,256]{1,0:T(8,128)(2,1)S(1)}, u32[]{:S(2)}, u32[]{:S(2)}) collective-permute-start(bf16[1024,256]{1,0:T(8,128)(2,1)} %grads.5), channel_id=1, source_target_pairs={{0,128},{64,192},{128,0},{192,64},{1,129},{65,193},{129,1},{193,65... | collective-permute-start | bytes 1572872 | tf_op jit(solution)/shard_map/ppermute | solution.py:322
  117.3 24.0 %collective-permute-start.1 = (bf16[1024,256]{1,0:T(8,128)(2,1)S(1)}, bf16[1024,256]{1,0:T(8,128)(2,1)S(1)}, u32[]{:S(2)}, u32[]{:S(2)}) collective-permute-start(bf16[1024,256]{1,0:T(8,128)(2,1)S(1)} %copy-done.2), channel_id=1, source_target_pairs={{0,64},{64,128},{128,192},{192,0},{1,65},{65,129},{129,193},{193,1... | collective-permute-start | bytes 1572872 | tf_op jit(solution)/shard_map/ppermute | solution.py:322
  118.0 23.7 %collective-permute-start.2 = (bf16[1024,256]{1,0:T(8,128)(2,1)S(1)}, bf16[1024,256]{1,0:T(8,128)(2,1)S(1)}, u32[]{:S(2)}, u32[]{:S(2)}) collective-permute-start(bf16[1024,256]{1,0:T(8,128)(2,1)S(1)} %copy-done.1), channel_id=1, source_target_pairs={{0,192},{64,0},{128,64},{192,128},{1,193},{65,1},{129,65},{193,129... | collective-permute-start | bytes 1572872 | tf_op jit(solution)/shard_map/ppermute | solution.py:322

commit v2 on v1

--- a/solution.py
+++ b/solution.py
@@ -10,7 +10,6 @@
 HALF = CAP // 2
 NEG = -1e30
 HIGH = lax.Precision.HIGHEST
-VMEM_BYTES = 56 * 1024 * 1024
 
 
 def iota(shape, axis):
@@ -29,7 +28,7 @@
 
 def query_kernel(heads, table, relations, kinds, codes, lists, lengths, out, ranks, rows, sem):
     count = rows.shape[0]
-    sets = lists.shape[0]
+    sets = lists.shape[1]
 
     def fetch(n, carry):
         pltpu.make_async_copy(
@@ -38,14 +37,8 @@
         return carry
 
     lax.fori_loop(0, count, fetch, 0, unroll=8)
-    listed_t = dot(
-        lists[...].astype(f32).astype(bf16),
-        (iota((sets, sets), 0) == iota((sets, sets), 1)).astype(f32).astype(bf16),
-        0,
-        0,
-    )
-    entry = iota(listed_t.shape, 0)
-    listed_t = jnp.where(entry < lengths[...], listed_t, -1.0)
+    listed_t = lists[...].astype(f32)
+    listed_t = jnp.where(iota(listed_t.shape, 0) < lengths[...], listed_t, -1.0)
     block = iota((sets, sets), 0).astype(f32)
     listed = jnp.zeros((sets, sets), f32)
     for k in range(listed_t.shape[0]):
@@ -101,7 +94,7 @@
     code = high * 128 + low
     used = jnp.sum(taken.astype(f32), axis=1, keepdims=True) > 0.5
     length = jnp.sum(jnp.where(taken, lengths[...].astype(f32), 0.0), axis=1, keepdims=True).astype(i32)
-    slot_lists = dot(onehot, lists[...].astype(f32).astype(bf16)).astype(i32)
+    slot_lists = dot(onehot, lists[...].astype(f32).astype(bf16), 1, 1).astype(i32)
     entry = code // sets_rows
     for _ in range(3):
         entry = jnp.where(entry >= length, entry - length, entry)
@@ -227,7 +220,11 @@
     me = lax.axis_index("entity").astype(i32).reshape(1)
     group = lax.axis_index("dp").astype(i32)
     smem = pl.BlockSpec(memory_space=pltpu.SMEM)
-    params = pltpu.CompilerParams(vmem_limit_bytes=VMEM_BYTES)
+
+    def params(mebibytes):
+        return pltpu.CompilerParams(vmem_limit_bytes=mebibytes * 1024 * 1024)
+
+    lists = candidate_blocks.T
     kinds = relation_offsets.reshape(1, count)
     codes = target_codes.reshape(1, count)
 
@@ -237,11 +234,11 @@
             jax.ShapeDtypeStruct((owners * 8, count), bf16),
             jax.ShapeDtypeStruct((owners, owners), f32),
         ),
-        in_specs=[smem, pl.BlockSpec(memory_space=pl.ANY)] + [pl.BlockSpec(memory_space=pltpu.VMEM)] * 5,
+        in_specs=[smem, pl.BlockSpec(memory_space=pltpu.HBM)] + [pl.BlockSpec(memory_space=pltpu.VMEM)] * 5,
         scratch_shapes=[pltpu.VMEM((count, depth), f32), pltpu.SemaphoreType.DMA],
-        compiler_params=params,
+        compiler_params=params(60),
         name="query",
-    )(head_offsets, table, relations, kinds, codes, candidate_blocks, list_lengths)
+    )(head_offsets, table, relations, kinds, codes, lists, list_lengths)
 
     held = lax.all_to_all(spread.reshape(owners, 8, count), "entity", 0, 0, tiled=True)
 
@@ -255,9 +252,9 @@
             jax.ShapeDtypeStruct((16, count), i32),
         ),
         in_specs=[smem] + [pl.BlockSpec(memory_space=pltpu.VMEM)] * 4,
-        compiler_params=params,
+        compiler_params=params(12),
         name="pack",
-    )(me, ranks, held.reshape(owners * 8, count), candidate_blocks, list_lengths)
+    )(me, ranks, held.reshape(owners * 8, count), lists, list_lengths)
 
     received = lax.all_to_all(packed.reshape(owners, 8, HALF * count), "entity", 0, 0, tiled=True)
 
@@ -279,7 +276,7 @@
         ],
         out_specs=[whole((depth, CAP * count)), whole((CAP * count, depth)), whole((owners * 16, count))],
         scratch_shapes=[pltpu.VMEM((8, CAP * count), f32)] * 3,
-        compiler_params=params,
+        compiler_params=params(60),
         name="stats",
     )(me, ranks, received.reshape(owners * 8, HALF * count), table, targets)
 
@@ -288,14 +285,14 @@
     norms, loss = pl.pallas_call(
         merge_kernel,
         out_shape=(jax.ShapeDtypeStruct((16, count), f32), jax.ShapeDtypeStruct((1, count), f32)),
-        compiler_params=params,
+        compiler_params=params(8),
         name="merge",
     )(shared)
 
     quarter = block_rows // groups
     tile = 512
 
-    def grads(which, dtype):
+    def grads(which, dtype, norms):
         return pl.pallas_call(
             grads_kernel,
             grid_spec=pltpu.PrefetchScalarGridSpec(
@@ -312,15 +309,21 @@
                 scratch_shapes=[pltpu.VMEM((tile, CAP * count), bf16)],
             ),
             out_shape=jax.ShapeDtypeStruct((quarter, depth), dtype),
-            compiler_params=params,
+            compiler_params=params(60),
+            cost_estimate=pl.CostEstimate(
+                flops=4 * quarter * CAP * count * depth,
+                transcendentals=quarter * CAP * count,
+                bytes_accessed=4 * quarter * depth * 2 + 4 * CAP * count * depth,
+            ),
             name="grads",
         )(which.reshape(1), norms, targets, table, query_t, query)
 
     arrived = []
     for shift in (2, 1, 3):
-        part = grads((group + shift) % groups, bf16)
+        part = grads((group + shift) % groups, bf16, norms)
         arrived.append(lax.ppermute(part, "dp", [(i, (i + shift) % groups) for i in range(groups)]))
-    gradient = grads(group, f32)
+    last_norms, arrived[0] = lax.optimization_barrier((norms, arrived[0]))
+    gradient = grads(group, f32, last_norms)
     for part in arrived:
         gradient = gradient + part.astype(f32)
     return (loss.reshape(count), gradient[None])

time: 146 us -> 132 us (0.904)
  waiting for transfers between devices: 43.5 us -> 34.5 us
  Pallas kernels: 41.4 us -> 38.7 us
    ppermute x3, waiting for transfers between devices: 16.6 us -> 7.59 us  [per_device(): lax.ppermute(part, 'dp', [(i, (i + shift) % groups) for i in range(groups)])]
    pallas_call x1, Pallas kernels: 3.38 us -> 1.83 us  [per_device(): pl.pallas_call(pack, out_shape=(jax.ShapeDtypeStruct((owners * 8, HALF *...]
  transfers between devices with their start and end apart: 5 -> 5, of which waited for: 5 -> 4; matrix products, arithmetic and copies ran while one was open for 0% -> 0% of each run, Pallas kernels for 3% -> 10%
where the time goes in v2:
time: 132 us; the launch traced here: 130 us
  Pallas kernels  38.7 us (29%)
  waiting for transfers between devices  34.5 us (26%)
  blocking collectives  27.7 us (21%)
  starting transfers between devices  24.7 us (19%)
  other arithmetic  2.4 us (2%)
  local copies, waits for them, and re-layouts  1.37 us (1%)
    all_to_all x1, blocking collectives, per_device(): lax.all_to_all(packed.reshape(owners, 8, HALF * count), 'entity', 0, 0, t...  27.7 us
    pallas_call x4, Pallas kernels, grads(): pl.pallas_call(grads_kernel, grid_spec=pltpu.PrefetchScalarGridSpec(num_s...  18.1 us
    all_to_all x1, waiting for transfers between devices, per_device(): lax.all_to_all(local.reshape(owners, 16, count), 'entity', 0, 0, tiled=True)  16.7 us
    pallas_call x1, Pallas kernels, per_device(): pl.pallas_call(stats_kernel, grid=(block_rows // tile,), out_shape=(jax.S...  13.8 us
    all_to_all x1, starting transfers between devices, per_device(): lax.all_to_all(spread.reshape(owners, 8, count), 'entity', 0, 0, tiled=True)  11.6 us
    all_to_all x1, waiting for transfers between devices, per_device(): lax.all_to_all(spread.reshape(owners, 8, count), 'entity', 0, 0, tiled=True)  10.2 us
    ppermute x3, waiting for transfers between devices, per_device(): lax.ppermute(part, 'dp', [(i, (i + shift) % groups) for i in range(groups)])  7.59 us
    all_to_all x1, starting transfers between devices, per_device(): lax.all_to_all(local.reshape(owners, 16, count), 'entity', 0, 0, tiled=True)  6.67 us
  transfers between devices with their start and end apart: 5, of which 4 were waited for; matrix products, arithmetic and copies ran while one was open for 0% of the time, Pallas kernels for 10%

profile of v2, /device:TPU:32, one launch (start us, length us, event | category | flops | bytes accessed | tf_op | source)
XLA Modules:
  0.0 130.1 jit_solution(11301438993416825971)
XLA Ops:
  0.6 0.0 copy-start.4
  0.6 0.0 copy-start.3
  0.7 4.3 %query.1 = (bf16[512,128]{1,0:T(8,128)(2,1)}, f32[64,64]{1,0:T(8,128)}) custom-call(s32[128]{0:T(128)} %heads.1, f32[4096,256]{1,0:T(8,128)} %bitcast.21, f32[4,256,256]{2,1,0:T(8,128)} %relations.1, s32[1,128]{1,0:T(1,128)} %bitcast.30, s32[1,128]{1,0:T(1,128)} %bitcast.31, s32[8,64]{1,0:T(8,128)} %bitcast.19, s32[1,64]{1,0:T(1,128)} %refs_4_.1), custom_call_target="tpu_custom_call" | custom-call | tf_op jit(solution)/shard_map/query/pallas_call | solution.py:231
  4.9 11.6 %all-to-all-start = ((bf16[64,8,128]{2,1,0:T(8,128)(2,1)}), bf16[64,8,128]{2,1,0:T(8,128)(2,1)S(1)}, u32[]{:S(2)}, u32[]{:S(2)}) async-start(bf16[64,8,128]{2,1,0:T(8,128)(2,1)} %bitcast.29), calls=%async_computation | async-start | bytes 262144 | tf_op jit(solution)/shard_map/all_to_all | solution.py:243
  16.6 10.2 %all-to-all-done = bf16[64,8,128]{2,1,0:T(8,128)(2,1)S(1)} async-done(((bf16[64,8,128]{2,1,0:T(8,128)(2,1)}), bf16[64,8,128]{2,1,0:T(8,128)(2,1)S(1)}, u32[]{:S(2)}, u32[]{:S(2)}) %all-to-all-start) | async-done | bytes 131104 | tf_op jit(solution)/shard_map/all_to_all | solution.py:243
  26.7 0.0 copy-done.4
  26.7 0.0 copy-done.3
  26.7 0.0 copy-start.2
  26.7 0.8 copy-done.2
  27.5 1.8 %pack.1 = (bf16[512,768]{1,0:T(8,128)(2,1)S(1)}, s32[16,128]{1,0:T(8,128)S(1)}) custom-call(s32[1]{0:T(128)} %bitcast.refs_0_.me, f32[64,64]{1,0:T(8,128)S(1)} %copy-done.2, bf16[512,128]{1,0:T(8,128)(2,1)S(1)} %bitcast.18, s32[8,64]{1,0:T(8,128)S(1)} %bitcast.20, s32[1,64]{1,0:T(1,128)S(1)} %copy-done.4), custom_call_target="tpu_custom_call" | custom-call | tf_op jit(solution)/shard_map/pack/pallas_call | solution.py:248
  29.3 0.0 copy-start
  29.3 27.7 %all_to_all.15 = bf16[64,8,768]{2,1,0:T(8,128)(2,1)} all-to-all(bf16[64,8,768]{2,1,0:T(8,128)(2,1)S(1)} %bitcast.17), channel_id=1, replica_groups=mesh['dp'=4,'entity'=64] {'entity'}, dimensions={0} | all-to-all | bytes 1572864 | tf_op jit(solution)/shard_map/all_to_all | solution.py:259
  57.0 0.0 copy-done
  57.0 13.8 %stats.1 = (bf16[256,1536]{1,0:T(8,128)(2,1)}, bf16[1536,256]{1,0:T(8,128)(2,1)}, f32[1024,128]{1,0:T(8,128)}) custom-call(s32[1]{0:T(128)} %bitcast.refs_0_.me, f32[64,64]{1,0:T(8,128)} %get-tuple-element.13.refs_1_.ranks, bf16[512,768]{1,0:T(8,128)(2,1)} %bitcast.27, f32[4096,256]{1,0:T(8,128)} %bitcast.22, s32[16,128]{1,0:T(8,128)} %copy-done), custom_call_target="tpu_custom_call" | custom-call | tf_op jit(solution)/shard_map/stats/pallas_call | solution.py:262
  70.8 6.7 %all-to-all-start.2 = ((f32[64,16,128]{2,1,0:T(8,128)}), f32[64,16,128]{2,1,0:T(8,128)S(1)}, u32[]{:S(2)}, u32[]{:S(2)}) async-start(f32[64,16,128]{2,1,0:T(8,128)} %bitcast.28), calls=%async_computation.2 | async-start | bytes 1048576 | tf_op jit(solution)/shard_map/all_to_all | solution.py:283
  77.5 16.7 %all-to-all-done.2.received = f32[64,16,128]{2,1,0:T(8,128)S(1)} async-done(((f32[64,16,128]{2,1,0:T(8,128)}), f32[64,16,128]{2,1,0:T(8,128)S(1)}, u32[]{:S(2)}, u32[]{:S(2)}) %all-to-all-start.2) | async-done | bytes 524320 | tf_op jit(solution)/shard_map/all_to_all | solution.py:283
  94.2 0.6 merge.1
  94.9 0.0 copy-start.1
  94.9 0.6 copy-done.1
  95.5 4.5 %grads.4 = bf16[1024,256]{1,0:T(8,128)(2,1)} custom-call(s32[1]{0:T(128)} %bitcast.12.first, f32[16,128]{1,0:T(8,128)} %copy-done.1, s32[16,128]{1,0:T(8,128)} %copy-done, f32[4096,256]{1,0:T(8,128)} %bitcast.23, bf16[256,1536]{1,0:T(8,128)(2,1)} %get-tuple-element.20.query_t, bf16[1536,256]{1,0:T(8,128)(2,1)} %get-tuple-element.21.query), custom_call_target="tpu_custom_call" | custom-call | flops 1610612736 | bytes 3670016 | tf_op jit(solution)/shard_map/grads/pallas_call | solution.py:296
  100.0 3.2 %collective-permute-start = (bf16[1024,256]{1,0:T(8,128)(2,1)}, bf16[1024,256]{1,0:T(8,128)(2,1)S(1)}, u32[]{:S(2)}, u32[]{:S(2)}) collective-permute-start(bf16[1024,256]{1,0:T(8,128)(2,1)} %grads.4), channel_id=1, source_target_pairs={{0,128},{64,192},{128,0},{192,64},{1,129},{65,193},{129,1},{193,65... | collective-permute-start | bytes 1572872 | tf_op jit(solution)/shard_map/ppermute | solution.py:324
  103.2 4.5 %grads.7 = bf16[1024,256]{1,0:T(8,128)(2,1)} custom-call(s32[1]{0:T(128)} %bitcast.14.first, f32[16,128]{1,0:T(8,128)} %copy-done.1, s32[16,128]{1,0:T(8,128)} %copy-done, f32[4096,256]{1,0:T(8,128)} %bitcast.24, bf16[256,1536]{1,0:T(8,128)(2,1)} %get-tuple-element.20.query_t, bf16[1536,256]{1,0:T(8,128)(2,1)} %get-tuple-element.21.query), custom_call_target="tpu_custom_call" | custom-call | flops 1610612736 | bytes 3670016 | tf_op jit(solution)/shard_map/grads/pallas_call | solution.py:296
  107.6 0.0 copy-start.5
  107.7 4.6 %grads.6 = bf16[1024,256]{1,0:T(8,128)(2,1)} custom-call(s32[1]{0:T(128)} %bitcast.13.first, f32[16,128]{1,0:T(8,128)} %copy-done.1, s32[16,128]{1,0:T(8,128)} %copy-done, f32[4096,256]{1,0:T(8,128)} %bitcast.25, bf16[256,1536]{1,0:T(8,128)(2,1)} %get-tuple-element.20.query_t, bf16[1536,256]{1,0:T(8,128)(2,1)} %get-tuple-element.21.query), custom_call_target="tpu_custom_call" | custom-call | flops 1610612736 | bytes 3670016 | tf_op jit(solution)/shard_map/grads/pallas_call | solution.py:296
  112.2 0.7 collective-permute-start.1
  112.9 0.0 copy-done.5
  112.9 2.6 %collective-permute-start.2 = (bf16[1024,256]{1,0:T(8,128)(2,1)S(1)}, bf16[1024,256]{1,0:T(8,128)(2,1)S(1)}, u32[]{:S(2)}, u32[]{:S(2)}) collective-permute-start(bf16[1024,256]{1,0:T(8,128)(2,1)S(1)} %copy-done.5), channel_id=1, source_target_pairs={{0,192},{64,0},{128,64},{192,128},{1,193},{65,1},{129,65},{193,129... | collective-permute-start | bytes 1572872 | tf_op jit(solution)/shard_map/ppermute | solution.py:324
  115.5 0.6 collective-permute-done
  116.1 4.6 %grads.5 = f32[1024,256]{1,0:T(8,128)} custom-call(s32[1]{0:T(128)} %bitcast.11.first, f32[16,128]{1,0:T(8,128)} %copy-done.1, s32[16,128]{1,0:T(8,128)} %copy-done, f32[4096,256]{1,0:T(8,128)} %bitcast.26, bf16[256,1536]{1,0:T(8,128)(2,1)} %get-tuple-element.20.query_t, bf16[1536,256]{1,0:T(8,128)(2,1)} %get-tuple-element.21.query), custom_call_target="tpu_custom_call" | custom-call | flops 1610612736 | bytes 3670016 | tf_op jit(solution)/shard_map/grads/pallas_call | solution.py:296
  120.7 7.0 %collective-permute-done.1 = bf16[1024,256]{1,0:T(8,128)(2,1)S(1)} collective-permute-done((bf16[1024,256]{1,0:T(8,128)(2,1)}, bf16[1024,256]{1,0:T(8,128)(2,1)S(1)}, u32[]{:S(2)}, u32[]{:S(2)}) %collective-permute-start.1) | collective-permute-done | bytes 524320 | tf_op jit(solution)/shard_map/ppermute | solution.py:324
  127.6 0.0 collective-permute-done.2
  127.7 2.4 %add_bitcast_fusion = f32[1,1024,256]{2,1,0:T(8,128)} fusion(bf16[1024,256]{1,0:T(8,128)(2,1)S(1)} %collective-permute-done.2, bf16[1024,256]{1,0:T(8,128)(2,1)S(1)} %collective-permute-done.1, f32[1024,256]{1,0:T(8,128)} %grads.5, bf16[1024,256]{1,0:T(8,128)(2,1)S(1)} %collective-permute-done), kind=kLoop, calls=%fused_computation | loop fusion | flops 1572864 | bytes 3670016 | tf_op jit(solution)/shard_map/broadcast_in_dim | solution.py:329
Async XLA Ops:
  0.6 26.1 %copy-start.4 = (s32[1,64]{1,0:T(1,128)S(1)}, s32[1,64]{1,0:T(1,128)}, u32[]{:S(2)}) copy-start(s32[1,64]{1,0:T(1,128)} %refs_4_.1) | copy-start | bytes 772
  0.6 26.1 %copy-start.3 = (s32[64,8]{0,1:T(8,128)S(1)}, s32[64,8]{0,1:T(8,128)}, u32[]{:S(2)}) copy-start(s32[64,8]{0,1:T(8,128)} %param.9) | copy-start | bytes 6148
  4.9 21.8 %all-to-all-start = ((bf16[64,8,128]{2,1,0:T(8,128)(2,1)}), bf16[64,8,128]{2,1,0:T(8,128)(2,1)S(1)}, u32[]{:S(2)}, u32[]{:S(2)}) async-start(bf16[64,8,128]{2,1,0:T(8,128)(2,1)} %bitcast.29), calls=%async_computation | async-start | bytes 262144 | tf_op jit(solution)/shard_map/all_to_all | solution.py:243
  26.7 0.8 copy-start.2
  29.3 27.7 %copy-start = (s32[16,128]{1,0:T(8,128)}, s32[16,128]{1,0:T(8,128)S(1)}, u32[]{:S(2)}) copy-start(s32[16,128]{1,0:T(8,128)S(1)} %get-tuple-element.16.targets) | copy-start | bytes 24580
  70.8 23.4 %all-to-all-start.2 = ((f32[64,16,128]{2,1,0:T(8,128)}), f32[64,16,128]{2,1,0:T(8,128)S(1)}, u32[]{:S(2)}, u32[]{:S(2)}) async-start(f32[64,16,128]{2,1,0:T(8,128)} %bitcast.28), calls=%async_computation.2 | async-start | bytes 1048576 | tf_op jit(solution)/shard_map/all_to_all | solution.py:283
  94.9 0.6 copy-start.1
  100.0 16.2 %collective-permute-start = (bf16[1024,256]{1,0:T(8,128)(2,1)}, bf16[1024,256]{1,0:T(8,128)(2,1)S(1)}, u32[]{:S(2)}, u32[]{:S(2)}) collective-permute-start(bf16[1024,256]{1,0:T(8,128)(2,1)} %grads.4), channel_id=1, source_target_pairs={{0,128},{64,192},{128,0},{192,64},{1,129},{65,193},{129,1},{193,65... | collective-permute-start | bytes 1572872 | tf_op jit(solution)/shard_map/ppermute | solution.py:324
  107.6 5.3 %copy-start.5 = (bf16[1024,256]{1,0:T(8,128)(2,1)S(1)}, bf16[1024,256]{1,0:T(8,128)(2,1)}, u32[]{:S(2)}) copy-start(bf16[1024,256]{1,0:T(8,128)(2,1)} %grads.7) | copy-start | bytes 1572868
  112.2 15.4 %collective-permute-start.1 = (bf16[1024,256]{1,0:T(8,128)(2,1)}, bf16[1024,256]{1,0:T(8,128)(2,1)S(1)}, u32[]{:S(2)}, u32[]{:S(2)}) collective-permute-start(bf16[1024,256]{1,0:T(8,128)(2,1)} %grads.6), channel_id=1, source_target_pairs={{0,64},{64,128},{128,192},{192,0},{1,65},{65,129},{129,193},{193,1... | collective-permute-start | bytes 1572872 | tf_op jit(solution)/shard_map/ppermute | solution.py:324
  112.9 14.7 %collective-permute-start.2 = (bf16[1024,256]{1,0:T(8,128)(2,1)S(1)}, bf16[1024,256]{1,0:T(8,128)(2,1)S(1)}, u32[]{:S(2)}, u32[]{:S(2)}) collective-permute-start(bf16[1024,256]{1,0:T(8,128)(2,1)S(1)} %copy-done.5), channel_id=1, source_target_pairs={{0,192},{64,0},{128,64},{192,128},{1,193},{65,1},{129,65},{193,129... | collective-permute-start | bytes 1572872 | tf_op jit(solution)/shard_map/ppermute | solution.py:324

commit v3 on v2

--- a/solution.py
+++ b/solution.py
@@ -8,6 +8,9 @@
 f32, bf16, i32 = jnp.float32, jnp.bfloat16, jnp.int32
 CAP = 12
 HALF = CAP // 2
+WIDE = 4
+TILE = 1024
+CHUNK = 128
 NEG = -1e30
 HIGH = lax.Precision.HIGHEST
 
@@ -105,76 +108,82 @@
     targets[...] = jnp.where(here, code % sets_rows, -1)
 
 
-def stats_kernel(
-    me, ranks, received, table, targets, query_t, query, out, top_s, sum_s, tgt_s
-):
-    step = pl.program_id(0)
-    pairs = CAP // 2
-    width = 256
-    tile = table.shape[0]
-
-    @pl.when(step == 0)
-    def _():
-        size = received.shape[0]
-        half = size // 2
-        lanes = received.shape[1]
-        values = received[...]
-        row, column = iota((half, size), 0), iota((half, size), 1)
-        for h in range(2):
-            pick = (row // 4 * 8 + h * 4 + row % 4 == column).astype(f32).astype(bf16)
-            query_t[:, h * lanes : (h + 1) * lanes] = dot(pick, values).astype(bf16)
-            query[h * lanes : (h + 1) * lanes, :] = dot(values, pick, 0, 1).astype(bf16)
-        top_s[...] = jnp.full(top_s.shape, NEG, f32)
-        sum_s[...] = jnp.zeros(sum_s.shape, f32)
-        tgt_s[...] = jnp.zeros(tgt_s.shape, f32)
-
-    rows = table[...].astype(bf16)
-    place = iota((tile, width), 0) + step * tile
-    for p in range(pairs):
-        columns = slice(p * width, (p + 1) * width)
-        score = dot(rows, query_t[:, columns])
-        target = jnp.concatenate([targets[2 * p : 2 * p + 1, :], targets[2 * p + 1 : 2 * p + 2, :]], axis=1)
-        grouped = score.reshape(tile // 8, 8, width)
-        old = top_s[:, columns]
-        top = jnp.maximum(old, jnp.max(grouped, axis=0))
-        mass = jnp.sum(jnp.exp(grouped - top[None]), axis=0)
-        sum_s[:, columns] = sum_s[:, columns] * jnp.exp(old - top) + mass
-        top_s[:, columns] = top
-        hit = jnp.where(place == target, score, 0.0).reshape(tile // 8, 8, width)
-        tgt_s[:, columns] = tgt_s[:, columns] + jnp.sum(hit, axis=0)
-
-    @pl.when(step == pl.num_programs(0) - 1)
-    def _():
-        top = top_s[...]
-        best = jnp.max(top, axis=0, keepdims=True)
-        mass = jnp.sum(sum_s[...] * jnp.exp(top - best), axis=0, keepdims=True)
-        local = best + jnp.log(mass)
-        picked = jnp.sum(tgt_s[...], axis=0, keepdims=True)
-        blank = jnp.zeros((4, 128), f32)
-        stacked = jnp.concatenate(
-            [local[:, i * 128 : (i + 1) * 128] for i in range(CAP)]
-            + [blank]
-            + [picked[:, i * 128 : (i + 1) * 128] for i in range(CAP)]
-            + [blank],
-            axis=0,
-        )
-        sets = ranks.shape[0]
-        total = out.shape[0]
-        rank = ranks[...]
-        up = (iota((total, sets), 0) // 16 == iota((total, sets), 1)).astype(f32)
-        wide = dot(up.astype(bf16), rank.astype(bf16))
-        slot = iota((total, sets), 0) % 16
-        shared = (wide == slot.astype(f32)) & (slot < CAP)
-        shared = shared | (((slot == CAP) | (slot == CAP + 1)) & (up > 0.5))
-        mine = ranks[pl.ds(me[0], 1), :]
-        owned = mine == (iota((32, sets), 0) % 16).astype(f32)
-        match = dot(shared.astype(f32).astype(bf16), owned.astype(f32).astype(bf16), 1, 1)
-        slot, source = iota((total, 32), 0) % 16, iota((total, 32), 1)
-        match = jnp.where((slot == CAP + 1) == (source >= 16), match, 0.0)
-        picked_rows = dot(match, stacked, precision=HIGH)
+def stats_kernel(received, table, targets, query_t, out, top_s, sum_s, tgt_s):
+    size, lanes = received.shape
+    half = size // 2
+    values = received[...]
+    row, column = iota((half, size), 0), iota((half, size), 1)
+    for h in range(2):
+        pick = (row // 4 * 8 + h * 4 + row % 4 == column).astype(f32).astype(bf16)
+        query_t[:, h * lanes : (h + 1) * lanes] = dot(pick, values).astype(bf16)
+    top_s[...] = jnp.full(top_s.shape, NEG, f32)
+    sum_s[...] = jnp.zeros(sum_s.shape, f32)
+    tgt_s[...] = jnp.zeros(tgt_s.shape, f32)
+
+    def visit(step, carry):
+        rows = table[pl.ds(step * TILE, TILE), :]
+        for p in range(CAP // WIDE):
+            columns = slice(p * WIDE * 128, (p + 1) * WIDE * 128)
+            weights = query_t[:, columns]
+            target = slot_lanes(targets, p)
+            wanted = target - iota((8, target.shape[1]), 0) - step * TILE
+            top, mass, hit = top_s[:, columns], sum_s[:, columns], tgt_s[:, columns]
+            for c in range(TILE // CHUNK):
+                score = dot(rows[c * CHUNK : (c + 1) * CHUNK, :], weights)
+                score = score.reshape(CHUNK // 8, 8, score.shape[1])
+                above = jnp.maximum(top, jnp.max(score, axis=0))
+                mass = mass * jnp.exp(top - above) + jnp.sum(jnp.exp(score - above[None]), axis=0)
+                top = above
+                for k in range(CHUNK // 8):
+                    hit = jnp.where(wanted == c * CHUNK + k * 8, score[k], hit)
+            top_s[:, columns], sum_s[:, columns], tgt_s[:, columns] = top, mass, hit
+        return carry
+
+    lax.fori_loop(0, table.shape[0] // TILE, visit, 0)
+    top = top_s[...]
+    best = jnp.max(top, axis=0, keepdims=True)
+    mass = jnp.sum(sum_s[...] * jnp.exp(top - best), axis=0, keepdims=True)
+    local = best + jnp.log(mass)
+    picked = jnp.sum(tgt_s[...], axis=0, keepdims=True)
+    out[...] = jnp.zeros(out.shape, f32)
+    for i in range(CAP):
+        out[i : i + 1, :] = local[:, i * 128 : (i + 1) * 128]
+        out[16 + i : 17 + i, :] = picked[:, i * 128 : (i + 1) * 128]
+
+
+def slot_lanes(ref, p):
+    return jnp.concatenate([ref[i : i + 1, :] for i in range(WIDE * p, WIDE * p + WIDE)], axis=1)
+
+
+def share_kernel(me, ranks, mine, other, out):
+    sets = ranks.shape[0]
+    total = out.shape[0]
+    core = me[0] % 2
+    rank = ranks[...]
+    row = iota((total, sets), 0)
+    place = row // 16 * 2 + core
+    up = (place == iota((total, sets), 1)).astype(f32)
+    wide = dot(up.astype(bf16), rank.astype(bf16))
+    slot = row % 16
+    shared = (wide == slot.astype(f32)) & (slot < CAP)
+    shared = shared | (((slot == CAP) | (slot == CAP + 1)) & (up > 0.5))
+    shared = shared.astype(f32).astype(bf16)
+    slot, source = iota((total, 32), 0) % 16, iota((total, 32), 1)
+    keep = (slot == CAP + 1) == (source >= 16)
+    wants_target = iota((total, 128), 0) % 16 == CAP + 1
+
+    def rows_of(owner, values):
+        owned = ranks[pl.ds(owner, 1), :] == (iota((32, sets), 0) % 16).astype(f32)
+        match = jnp.where(keep, dot(shared, owned.astype(f32).astype(bf16), 1, 1), 0.0)
+        found = dot(match, values[...], precision=HIGH)
         present = dot(match.astype(bf16), jnp.ones((32, 128), bf16))
-        missing = jnp.where(iota((total, 128), 0) % 16 == CAP + 1, 0.0, NEG)
-        out[...] = jnp.where(present > 0.5, picked_rows, missing)
+        return jnp.where(present > 0.5, found, jnp.where(wants_target, 0.0, NEG))
+
+    first = rows_of(me[0], mine)
+    second = rows_of(me[0] + 1 - 2 * core, other)
+    best = jnp.maximum(first, second)
+    both = best + jnp.log(jnp.exp(first - best) + jnp.exp(second - best))
+    out[...] = jnp.where(wants_target, first + second, both)
 
 
 def merge_kernel(received, norms, loss):
@@ -187,20 +196,24 @@
     loss[...] = norm[CAP : CAP + 1, :] - target
 
 
-def grads_kernel(first, norms, targets, table, query_t, query, out, coefficients):
-    step = pl.program_id(0)
-    tile = table.shape[0]
-    width = 256
-    rows = table[...].astype(bf16)
-    place = iota((tile, width), 0) + (first[0] * (pl.num_programs(0) * tile) + step * tile)
-    for p in range(CAP // 2):
-        columns = slice(p * width, (p + 1) * width)
-        score = dot(rows, query_t[:, columns])
-        norm = jnp.concatenate([norms[2 * p : 2 * p + 1, :], norms[2 * p + 1 : 2 * p + 2, :]], axis=1)
-        target = jnp.concatenate([targets[2 * p : 2 * p + 1, :], targets[2 * p + 1 : 2 * p + 2, :]], axis=1)
-        weight = jnp.exp(score - norm)
-        coefficients[:, columns] = jnp.where(place == target, weight - 1.0, weight).astype(bf16)
-    out[...] = dot(coefficients[...], query[...]).astype(out.dtype)
+def grads_kernel(first, norms, targets, table, query_t, out, coefficients):
+    count = out.shape[0]
+    start = pl.multiple_of(first[0] * count, count)
+    rows = table[pl.ds(start, count), :]
+    for p in range(CAP // WIDE):
+        columns = slice(p * WIDE * 128, (p + 1) * WIDE * 128)
+        weights = query_t[:, columns]
+        norm = slot_lanes(norms, p)
+        target = slot_lanes(targets, p)
+        wanted = target - iota((8, target.shape[1]), 0) - start
+        for c in range(count // CHUNK):
+            score = dot(rows[c * CHUNK : (c + 1) * CHUNK, :], weights)
+            score = score.reshape(CHUNK // 8, 8, score.shape[1])
+            weight = jnp.exp(score - norm[None])
+            place = iota(score.shape, 0) * 8 + c * CHUNK
+            weight = jnp.where(place == wanted[None], weight - 1.0, weight)
+            coefficients[c * CHUNK : (c + 1) * CHUNK, columns] = weight.reshape(CHUNK, -1).astype(bf16)
+    out[...] = dot(coefficients[...], query_t[...], 1, 1).astype(out.dtype)
 
 
 def per_device(
@@ -236,7 +249,7 @@
         ),
         in_specs=[smem, pl.BlockSpec(memory_space=pltpu.HBM)] + [pl.BlockSpec(memory_space=pltpu.VMEM)] * 5,
         scratch_shapes=[pltpu.VMEM((count, depth), f32), pltpu.SemaphoreType.DMA],
-        compiler_params=params(60),
+        compiler_params=params(61),
         name="query",
     )(head_offsets, table, relations, kinds, codes, lists, list_lengths)
 
@@ -258,29 +271,31 @@
 
     received = lax.all_to_all(packed.reshape(owners, 8, HALF * count), "entity", 0, 0, tiled=True)
 
-    tile = 1024
-    query_t, query, local = pl.pallas_call(
+    rounded = table.astype(bf16)
+    query_t, local = pl.pallas_call(
         stats_kernel,
-        grid=(block_rows // tile,),
         out_shape=(
             jax.ShapeDtypeStruct((depth, CAP * count), bf16),
-            jax.ShapeDtypeStruct((CAP * count, depth), bf16),
-            jax.ShapeDtypeStruct((owners * 16, count), f32),
+            jax.ShapeDtypeStruct((32, count), f32),
         ),
-        in_specs=[
-            smem,
-            whole((owners, owners)),
-            whole((owners * 8, HALF * count)),
-            pl.BlockSpec((tile, depth), lambda s: (s, 0)),
-            whole((16, count)),
-        ],
-        out_specs=[whole((depth, CAP * count)), whole((CAP * count, depth)), whole((owners * 16, count))],
+        in_specs=[pl.BlockSpec(memory_space=pltpu.VMEM)] * 3,
         scratch_shapes=[pltpu.VMEM((8, CAP * count), f32)] * 3,
-        compiler_params=params(60),
+        compiler_params=params(16),
         name="stats",
-    )(me, ranks, received.reshape(owners * 8, HALF * count), table, targets)
-
-    shared = lax.all_to_all(local.reshape(owners, 16, count), "entity", 0, 0, tiled=True)
+    )(received.reshape(owners * 8, HALF * count), rounded, targets)
+
+    other = lax.ppermute(local, "entity", [(i, i ^ 1) for i in range(owners)])
+    share = pl.pallas_call(
+        share_kernel,
+        out_shape=jax.ShapeDtypeStruct((owners // 2 * 16, count), f32),
+        in_specs=[smem] + [pl.BlockSpec(memory_space=pltpu.VMEM)] * 3,
+        compiler_params=params(8),
+        name="share",
+    )(me, ranks, local, other)
+    cores = [[i for i in range(owners) if i % 2 == core] for core in range(2)]
+    shared = lax.all_to_all(
+        share.reshape(owners // 2, 16, count), "entity", 0, 0, tiled=True, axis_index_groups=cores
+    )
 
     norms, loss = pl.pallas_call(
         merge_kernel,
@@ -290,33 +305,21 @@
     )(shared)
 
     quarter = block_rows // groups
-    tile = 512
 
     def grads(which, dtype, norms):
         return pl.pallas_call(
             grads_kernel,
-            grid_spec=pltpu.PrefetchScalarGridSpec(
-                num_scalar_prefetch=1,
-                grid=(quarter // tile,),
-                in_specs=[
-                    pl.BlockSpec((16, count), lambda s, w: (0, 0)),
-                    pl.BlockSpec((16, count), lambda s, w: (0, 0)),
-                    pl.BlockSpec((tile, depth), lambda s, w: (w[0] * (quarter // tile) + s, 0)),
-                    pl.BlockSpec((depth, CAP * count), lambda s, w: (0, 0)),
-                    pl.BlockSpec((CAP * count, depth), lambda s, w: (0, 0)),
-                ],
-                out_specs=pl.BlockSpec((tile, depth), lambda s, w: (s, 0)),
-                scratch_shapes=[pltpu.VMEM((tile, CAP * count), bf16)],
-            ),
             out_shape=jax.ShapeDtypeStruct((quarter, depth), dtype),
-            compiler_params=params(60),
+            in_specs=[smem] + [pl.BlockSpec(memory_space=pltpu.VMEM)] * 4,
+            scratch_shapes=[pltpu.VMEM((quarter, CAP * count), bf16)],
+            compiler_params=params(16),
             cost_estimate=pl.CostEstimate(
                 flops=4 * quarter * CAP * count * depth,
                 transcendentals=quarter * CAP * count,
-                bytes_accessed=4 * quarter * depth * 2 + 4 * CAP * count * depth,
+                bytes_accessed=4 * quarter * depth + 4 * CAP * count * depth,
             ),
             name="grads",
-        )(which.reshape(1), norms, targets, table, query_t, query)
+        )(which.reshape(1), norms, targets, rounded, query_t)
 
     arrived = []
     for shift in (2, 1, 3):

time: 132 us -> 120 us (0.909)
  blocking collectives: 27.7 us -> 0 us
  waiting for transfers between devices: 34.5 us -> 55.3 us
  Pallas kernels: 38.7 us -> 25.9 us
  starting transfers between devices: 24.7 us -> 30.4 us
  local copies, waits for them, and re-layouts: 1.37 us -> 2.78 us
    all_to_all x1 -> x0, blocking collectives: 27.7 us -> none  [per_device(): lax.all_to_all(packed.reshape(owners, 8, HALF * count), 'entity', 0, 0, t...]
    all_to_all x1 -> x2, waiting for transfers between devices: 16.7 us -> 32.4 us  [the longest x1 20 us: per_device(): lax.all_to_all(packed.reshape(owners, 8, HALF * count), 'entity', 0, 0, t...]
    pallas_call x5 -> x6, Pallas kernels: 31.9 us -> 18.6 us  [the longest x4 8.62 us: grads(): pl.pallas_call(grads_kernel, out_shape=jax.ShapeDtypeStruct((quarter, dep...]
    all_to_all x1 -> x2, starting transfers between devices: 6.67 us -> 11.7 us  [the longest x1 6.27 us: per_device(): lax.all_to_all(share.reshape(owners // 2, 16, count), 'entity', 0, 0, til...]
    ppermute x3, waiting for transfers between devices: 7.59 us -> 11.8 us  [per_device(): lax.ppermute(part, 'dp', [(i, (i + shift) % groups) for i in range(groups)])]
    convert_element_type x0 -> x1, other arithmetic: none -> 2.4 us  [per_device(): rounded = table.astype(bf16)]
    unnamed x12, local copies, waits for them, and re-layouts: 1.37 us -> 2.78 us
  transfers between devices with their start and end apart: 5 -> 7, of which waited for: 4 -> 7; matrix products, arithmetic and copies ran while one was open for 0% -> 2% of each run, Pallas kernels for 10% -> 5%
where the time goes in v3:
time: 120 us; the launch traced here: 119 us
  waiting for transfers between devices  55.3 us (46%)
  starting transfers between devices  30.4 us (25%)
  Pallas kernels  25.9 us (22%)
  other arithmetic  3.57 us (3%)
  local copies, waits for them, and re-layouts  2.78 us (2%)
    all_to_all x1, waiting for transfers between devices, per_device(): lax.all_to_all(packed.reshape(owners, 8, HALF * count), 'entity', 0, 0, t...  20 us
    all_to_all x1, waiting for transfers between devices, per_device(): lax.all_to_all(share.reshape(owners // 2, 16, count), 'entity', 0, 0, til...  12.5 us
    ppermute x3, waiting for transfers between devices, per_device(): lax.ppermute(part, 'dp', [(i, (i + shift) % groups) for i in range(groups)])  11.8 us
    all_to_all x1, starting transfers between devices, per_device(): lax.all_to_all(spread.reshape(owners, 8, count), 'entity', 0, 0, tiled=True)  11.6 us
    all_to_all x1, waiting for transfers between devices, per_device(): lax.all_to_all(spread.reshape(owners, 8, count), 'entity', 0, 0, tiled=True)  10.2 us
    pallas_call x4, Pallas kernels, grads(): pl.pallas_call(grads_kernel, out_shape=jax.ShapeDtypeStruct((quarter, dep...  8.62 us
    pallas_call x1, Pallas kernels, per_device(): pl.pallas_call(stats_kernel, out_shape=(jax.ShapeDtypeStruct((depth, CAP...  8.24 us
    ppermute x3, starting transfers between devices, per_device(): lax.ppermute(part, 'dp', [(i, (i + shift) % groups) for i in range(groups)])  6.79 us
  transfers between devices with their start and end apart: 7, of which 7 were waited for; matrix products, arithmetic and copies ran while one was open for 2% of the time, Pallas kernels for 5%

profile of v3, /device:TPU:32, one launch (start us, length us, event | category | flops | bytes accessed | tf_op | source)
XLA Modules:
  0.0 118.8 jit_solution(8989390369675781728)
XLA Ops:
  0.6 0.0 copy-start.3
  0.6 0.0 copy-start.2
  0.7 4.3 %query.1 = (bf16[512,128]{1,0:T(8,128)(2,1)}, f32[64,64]{1,0:T(8,128)}) custom-call(s32[128]{0:T(128)} %heads.1, f32[4096,256]{1,0:T(8,128)} %bitcast.22, f32[4,256,256]{2,1,0:T(8,128)} %relations.1, s32[1,128]{1,0:T(1,128)} %bitcast.24, s32[1,128]{1,0:T(1,128)} %bitcast.25, s32[8,64]{1,0:T(8,128)} %bitcast.20, s32[1,64]{1,0:T(1,128)} %refs_4_.1), custom_call_target="tpu_custom_call" | custom-call | tf_op jit(solution)/shard_map/query/pallas_call | solution.py:244
  4.9 11.6 %all-to-all-start = ((bf16[64,8,128]{2,1,0:T(8,128)(2,1)}), bf16[64,8,128]{2,1,0:T(8,128)(2,1)S(1)}, u32[]{:S(2)}, u32[]{:S(2)}) async-start(bf16[64,8,128]{2,1,0:T(8,128)(2,1)} %bitcast.23), calls=%async_computation | async-start | bytes 262144 | tf_op jit(solution)/shard_map/all_to_all | solution.py:256
  16.6 10.2 %all-to-all-done = bf16[64,8,128]{2,1,0:T(8,128)(2,1)S(1)} async-done(((bf16[64,8,128]{2,1,0:T(8,128)(2,1)}), bf16[64,8,128]{2,1,0:T(8,128)(2,1)S(1)}, u32[]{:S(2)}, u32[]{:S(2)}) %all-to-all-start) | async-done | bytes 131104 | tf_op jit(solution)/shard_map/all_to_all | solution.py:256
  26.7 0.0 copy-done.3
  26.7 0.0 copy-done.2
  26.7 0.0 copy-start
  26.7 0.8 copy-done
  27.5 2.5 %pack.1 = (bf16[512,768]{1,0:T(8,128)(2,1)}, s32[16,128]{1,0:T(8,128)S(1)}) custom-call(s32[1]{0:T(128)} %bitcast.refs_0_.me, f32[64,64]{1,0:T(8,128)S(1)} %copy-done, bf16[512,128]{1,0:T(8,128)(2,1)S(1)} %bitcast.19, s32[8,64]{1,0:T(8,128)S(1)} %bitcast.21, s32[1,64]{1,0:T(1,128)S(1)} %copy-done.3), custom_call_target="tpu_custom_call" | custom-call | tf_op jit(solution)/shard_map/pack/pallas_call | solution.py:261
  30.0 5.4 %all-to-all-start.1 = ((bf16[64,8,768]{2,1,0:T(8,128)(2,1)}), bf16[64,8,768]{2,1,0:T(8,128)(2,1)S(1)}, u32[]{:S(2)}, u32[]{:S(2)}) async-start(bf16[64,8,768]{2,1,0:T(8,128)(2,1)} %bitcast.7), calls=%async_computation.1 | async-start | bytes 1572864 | tf_op jit(solution)/shard_map/all_to_all | solution.py:272
  35.4 0.0 copy-start.1
  35.4 2.4 %bitcast_convert_fusion.table = bf16[4096,256]{1,0:T(8,128)(2,1)S(1)} fusion(f32[1,4096,256]{2,1,0:T(8,128)} %param.7), kind=kLoop, calls=%fused_computation.1 | loop fusion | flops 1048576 | bytes 6291456 | tf_op jit(solution)/shard_map/convert_element_type | solution.py:274
  37.8 20.0 %all-to-all-done.1 = bf16[64,8,768]{2,1,0:T(8,128)(2,1)S(1)} async-done(((bf16[64,8,768]{2,1,0:T(8,128)(2,1)}), bf16[64,8,768]{2,1,0:T(8,128)(2,1)S(1)}, u32[]{:S(2)}, u32[]{:S(2)}) %all-to-all-start.1) | async-done | bytes 786464 | tf_op jit(solution)/shard_map/all_to_all | solution.py:272
  57.8 8.2 %stats.1 = (bf16[256,1536]{1,0:T(8,128)(2,1)S(1)}, f32[32,128]{1,0:T(8,128)S(1)}) custom-call(bf16[512,768]{1,0:T(8,128)(2,1)S(1)} %bitcast.18, bf16[4096,256]{1,0:T(8,128)(2,1)S(1)} %bitcast_convert_fusion.table, s32[16,128]{1,0:T(8,128)S(1)} %get-tuple-element.15.targets), custom_call_target="tpu_custom_call" | custom-call | tf_op jit(solution)/shard_map/stats/pallas_call | solution.py:275
  66.1 0.0 copy-start.4
  66.1 0.9 copy-done.4
  66.9 0.3 collective-permute-start
  67.3 0.9 collective-permute-done.other
  68.1 0.0 copy-done.1
  68.1 1.8 %share.1 = f32[512,128]{1,0:T(8,128)} custom-call(s32[1]{0:T(128)} %bitcast.refs_0_.me, f32[64,64]{1,0:T(8,128)S(1)} %copy-done.1, f32[32,128]{1,0:T(8,128)S(1)} %get-tuple-element.16.mine, f32[32,128]{1,0:T(8,128)S(1)} %collective-permute-done.other), custom_call_target="tpu_custom_call" | custom-call | tf_op jit(solution)/shard_map/share/pallas_call | solution.py:288
  69.9 6.3 %all-to-all-start.2 = ((f32[32,16,128]{2,1,0:T(8,128)}), f32[32,16,128]{2,1,0:T(8,128)S(1)}, u32[]{:S(2)}, u32[]{:S(2)}) async-start(f32[32,16,128]{2,1,0:T(8,128)} %bitcast.9), calls=%async_computation.2 | async-start | bytes 524288 | tf_op jit(solution)/shard_map/all_to_all | solution.py:296
  76.2 12.5 %all-to-all-done.2.received = f32[32,16,128]{2,1,0:T(8,128)S(1)} async-done(((f32[32,16,128]{2,1,0:T(8,128)}), f32[32,16,128]{2,1,0:T(8,128)S(1)}, u32[]{:S(2)}, u32[]{:S(2)}) %all-to-all-start.2) | async-done | bytes 262176 | tf_op jit(solution)/shard_map/all_to_all | solution.py:296
  88.6 0.6 merge.1
  89.2 0.0 copy-start.5
  89.2 1.1 copy-done.5
  90.4 2.2 %grads.4 = bf16[1024,256]{1,0:T(8,128)(2,1)S(1)} custom-call(s32[1]{0:T(128)} %bitcast.12.first, f32[16,128]{1,0:T(8,128)S(1)} %get-tuple-element.20.norms, s32[16,128]{1,0:T(8,128)S(1)} %get-tuple-element.15.targets, bf16[4096,256]{1,0:T(8,128)(2,1)S(1)} %bitcast_convert_fusion.table, bf16[256,1536]{1,0:T(8,128)(2,1)S(1)} %copy-done.5), custom_call_target="tpu_custom_call" | custom-call | flops 1610612736 | bytes 2621440 | tf_op jit(solution)/shard_map/grads/pallas_call | solution.py:310
  92.5 3.5 %collective-permute-start.1 = (bf16[1024,256]{1,0:T(8,128)(2,1)S(1)}, bf16[1024,256]{1,0:T(8,128)(2,1)S(1)}, u32[]{:S(2)}, u32[]{:S(2)}) collective-permute-start(bf16[1024,256]{1,0:T(8,128)(2,1)S(1)} %grads.4), channel_id=1, source_target_pairs={{0,128},{64,192},{128,0},{192,64},{1,129},{65,193},{129,1},{193,65... | collective-permute-start | bytes 1572872 | tf_op jit(solution)/shard_map/ppermute | solution.py:327
  96.0 2.2 %grads.7 = bf16[1024,256]{1,0:T(8,128)(2,1)S(1)} custom-call(s32[1]{0:T(128)} %bitcast.14.first, f32[16,128]{1,0:T(8,128)S(1)} %get-tuple-element.20.norms, s32[16,128]{1,0:T(8,128)S(1)} %get-tuple-element.15.targets, bf16[4096,256]{1,0:T(8,128)(2,1)S(1)} %bitcast_convert_fusion.table, bf16[256,1536]{1,0:T(8,128)(2,1)S(1)} %copy-done.5), custom_call_target="tpu_custom_call" | custom-call | flops 1610612736 | bytes 2621440 | tf_op jit(solution)/shard_map/grads/pallas_call | solution.py:310
  98.2 2.2 %grads.6 = bf16[1024,256]{1,0:T(8,128)(2,1)S(1)} custom-call(s32[1]{0:T(128)} %bitcast.13.first, f32[16,128]{1,0:T(8,128)S(1)} %get-tuple-element.20.norms, s32[16,128]{1,0:T(8,128)S(1)} %get-tuple-element.15.targets, bf16[4096,256]{1,0:T(8,128)(2,1)S(1)} %bitcast_convert_fusion.table, bf16[256,1536]{1,0:T(8,128)(2,1)S(1)} %copy-done.5), custom_call_target="tpu_custom_call" | custom-call | flops 1610612736 | bytes 2621440 | tf_op jit(solution)/shard_map/grads/pallas_call | solution.py:310
  100.3 0.8 collective-permute-start.2
  101.1 2.6 %collective-permute-start.3 = (bf16[1024,256]{1,0:T(8,128)(2,1)S(1)}, bf16[1024,256]{1,0:T(8,128)(2,1)S(1)}, u32[]{:S(2)}, u32[]{:S(2)}) collective-permute-start(bf16[1024,256]{1,0:T(8,128)(2,1)S(1)} %grads.7), channel_id=1, source_target_pairs={{0,192},{64,0},{128,64},{192,128},{1,193},{65,1},{129,65},{193,129... | collective-permute-start | bytes 1572872 | tf_op jit(solution)/shard_map/ppermute | solution.py:327
  103.6 5.5 %collective-permute-done.1 = bf16[1024,256]{1,0:T(8,128)(2,1)S(1)} collective-permute-done((bf16[1024,256]{1,0:T(8,128)(2,1)S(1)}, bf16[1024,256]{1,0:T(8,128)(2,1)S(1)}, u32[]{:S(2)}, u32[]{:S(2)}) %collective-permute-start.1) | collective-permute-done | bytes 524320 | tf_op jit(solution)/shard_map/ppermute | solution.py:327
  109.2 2.1 %grads.5 = f32[1024,256]{1,0:T(8,128)S(1)} custom-call(s32[1]{0:T(128)} %bitcast.11.first, f32[16,128]{1,0:T(8,128)S(1)} %get-tuple-element.20.norms, s32[16,128]{1,0:T(8,128)S(1)} %get-tuple-element.15.targets, bf16[4096,256]{1,0:T(8,128)(2,1)S(1)} %bitcast_convert_fusion.table, bf16[256,1536]{1,0:T(8,128)(2,1)S(1)} %copy-done.5), custom_call_target="tpu_custom_call" | custom-call | flops 1610612736 | bytes 2621440 | tf_op jit(solution)/shard_map/grads/pallas_call | solution.py:310
  111.3 6.0 %collective-permute-done.2 = bf16[1024,256]{1,0:T(8,128)(2,1)S(1)} collective-permute-done((bf16[1024,256]{1,0:T(8,128)(2,1)S(1)}, bf16[1024,256]{1,0:T(8,128)(2,1)S(1)}, u32[]{:S(2)}, u32[]{:S(2)}) %collective-permute-start.2) | collective-permute-done | bytes 524320 | tf_op jit(solution)/shard_map/ppermute | solution.py:327
  117.3 0.4 collective-permute-done.3
  117.6 1.2 add_bitcast_fusion
Async XLA Ops:
  0.6 26.1 %copy-start.3 = (s32[1,64]{1,0:T(1,128)S(1)}, s32[1,64]{1,0:T(1,128)}, u32[]{:S(2)}) copy-start(s32[1,64]{1,0:T(1,128)} %refs_4_.1) | copy-start | bytes 772
  0.6 26.1 %copy-start.2 = (s32[64,8]{0,1:T(8,128)S(1)}, s32[64,8]{0,1:T(8,128)}, u32[]{:S(2)}) copy-start(s32[64,8]{0,1:T(8,128)} %param.9) | copy-start | bytes 6148
  4.9 21.8 %all-to-all-start = ((bf16[64,8,128]{2,1,0:T(8,128)(2,1)}), bf16[64,8,128]{2,1,0:T(8,128)(2,1)S(1)}, u32[]{:S(2)}, u32[]{:S(2)}) async-start(bf16[64,8,128]{2,1,0:T(8,128)(2,1)} %bitcast.23), calls=%async_computation | async-start | bytes 262144 | tf_op jit(solution)/shard_map/all_to_all | solution.py:256
  26.7 0.8 copy-start
  30.0 27.8 %all-to-all-start.1 = ((bf16[64,8,768]{2,1,0:T(8,128)(2,1)}), bf16[64,8,768]{2,1,0:T(8,128)(2,1)S(1)}, u32[]{:S(2)}, u32[]{:S(2)}) async-start(bf16[64,8,768]{2,1,0:T(8,128)(2,1)} %bitcast.7), calls=%async_computation.1 | async-start | bytes 1572864 | tf_op jit(solution)/shard_map/all_to_all | solution.py:272
  35.4 32.7 %copy-start.1 = (f32[64,64]{1,0:T(8,128)S(1)}, f32[64,64]{1,0:T(8,128)}, u32[]{:S(2)}) copy-start(f32[64,64]{1,0:T(8,128)} %get-tuple-element.12.refs_1_.ranks) | copy-start | bytes 49156
  66.1 0.9 copy-start.4
  66.9 1.2 collective-permute-start
  69.9 18.8 %all-to-all-start.2 = ((f32[32,16,128]{2,1,0:T(8,128)}), f32[32,16,128]{2,1,0:T(8,128)S(1)}, u32[]{:S(2)}, u32[]{:S(2)}) async-start(f32[32,16,128]{2,1,0:T(8,128)} %bitcast.9), calls=%async_computation.2 | async-start | bytes 524288 | tf_op jit(solution)/shard_map/all_to_all | solution.py:296
  89.2 1.1 copy-start.5
  92.5 16.6 %collective-permute-start.1 = (bf16[1024,256]{1,0:T(8,128)(2,1)S(1)}, bf16[1024,256]{1,0:T(8,128)(2,1)S(1)}, u32[]{:S(2)}, u32[]{:S(2)}) collective-permute-start(bf16[1024,256]{1,0:T(8,128)(2,1)S(1)} %grads.4), channel_id=1, source_target_pairs={{0,128},{64,192},{128,0},{192,64},{1,129},{65,193},{129,1},{193,65... | collective-permute-start | bytes 1572872 | tf_op jit(solution)/shard_map/ppermute | solution.py:327
  100.3 17.0 %collective-permute-start.2 = (bf16[1024,256]{1,0:T(8,128)(2,1)S(1)}, bf16[1024,256]{1,0:T(8,128)(2,1)S(1)}, u32[]{:S(2)}, u32[]{:S(2)}) collective-permute-start(bf16[1024,256]{1,0:T(8,128)(2,1)S(1)} %grads.6), channel_id=1, source_target_pairs={{0,64},{64,128},{128,192},{192,0},{1,65},{65,129},{129,193},{193,1... | collective-permute-start | bytes 1572872 | tf_op jit(solution)/shard_map/ppermute | solution.py:327
  101.1 16.6 %collective-permute-start.3 = (bf16[1024,256]{1,0:T(8,128)(2,1)S(1)}, bf16[1024,256]{1,0:T(8,128)(2,1)S(1)}, u32[]{:S(2)}, u32[]{:S(2)}) collective-permute-start(bf16[1024,256]{1,0:T(8,128)(2,1)S(1)} %grads.7), channel_id=1, source_target_pairs={{0,192},{64,0},{128,64},{192,128},{1,193},{65,1},{129,65},{193,129... | collective-permute-start | bytes 1572872 | tf_op jit(solution)/shard_map/ppermute | solution.py:327

commit v4 on v3

--- a/solution.py
+++ b/solution.py
@@ -7,7 +7,7 @@
 
 f32, bf16, i32 = jnp.float32, jnp.bfloat16, jnp.int32
 CAP = 12
-HALF = CAP // 2
+PARTS = 8
 WIDE = 4
 TILE = 1024
 CHUNK = 128
@@ -29,9 +29,8 @@
     return pl.BlockSpec(shape, lambda *_: (0,) * len(shape))
 
 
-def query_kernel(heads, table, relations, kinds, codes, lists, lengths, out, ranks, rows, sem):
+def query_kernel(heads, table, relations, kinds, codes, out, rows, sem):
     count = rows.shape[0]
-    sets = lists.shape[1]
 
     def fetch(n, carry):
         pltpu.make_async_copy(
@@ -40,82 +39,92 @@
         return carry
 
     lax.fori_loop(0, count, fetch, 0, unroll=8)
-    listed_t = lists[...].astype(f32)
-    listed_t = jnp.where(iota(listed_t.shape, 0) < lengths[...], listed_t, -1.0)
-    block = iota((sets, sets), 0).astype(f32)
-    listed = jnp.zeros((sets, sets), f32)
-    for k in range(listed_t.shape[0]):
-        listed = jnp.where(listed_t[k : k + 1, :] == block, 1.0, listed)
-    before = (iota((sets, sets), 0) < iota((sets, sets), 1)).astype(f32).astype(bf16)
-    rank = dot(listed.astype(bf16), before)
-    ranks[...] = jnp.where(listed > 0.0, rank, -1.0)
     diagonal = iota((count, count), 0) == iota((count, count), 1)
     kind = jnp.sum(jnp.where(diagonal, kinds[...].astype(f32), 0.0), axis=1, keepdims=True)
+    depth = relations.shape[2]
+    part = depth // PARTS
+    total = PARTS * (part + 8)
+    row, column = iota((total, depth), 0), iota((total, depth), 1)
+    place = row % (part + 8)
+    pick = (place < part) & (row // (part + 8) * part + place == column)
+    pick = pick.astype(f32).astype(bf16)
     pltpu.make_async_copy(table.at[pl.ds(0, count), :], rows, sem).wait()
     head = rows[...]
-    query = jnp.zeros((count, relations.shape[2]), f32)
+    query = jnp.zeros((count, depth), f32)
     for r in range(relations.shape[0]):
         product = dot(head, relations[r], precision=HIGH)
         query = jnp.where(kind == r, product, query)
-    query = query.astype(bf16)
-    total, width = out.shape[0], query.shape[1]
-    row, column = iota((total, width), 0), iota((total, width), 1)
-    pick = (row % 8 < 4) & (row // 8 * 4 + row % 8 == column)
-    spread = dot(pick.astype(f32).astype(bf16), query, 1, 1)
-    row = iota(spread.shape, 0) % 8
+    spread = dot(pick, query.astype(bf16), 1, 1)
+    place = iota(spread.shape, 0) % (part + 8)
     code = codes[...]
-    spread = jnp.where(row == 4, (code // 128).astype(f32), spread)
-    spread = jnp.where(row == 5, (code % 128).astype(f32), spread)
-    out[...] = spread.astype(bf16)
-
-
-def pack_kernel(me, ranks, held, lists, lengths, out, targets, sets_rows):
-    sets = ranks.shape[0]
-    size = held.shape[0]
-    rank = ranks[...]
-    up = (iota((size, sets), 0) // 8 == iota((size, sets), 1)).astype(f32).astype(bf16)
-    wide = dot(up, rank.astype(bf16))
-    wide = dot(wide.astype(bf16), up, 1, 1)
-    row, column = iota((size, size), 0), iota((size, size), 1)
-    wide = jnp.where(row % 4 == column % 8, wide - (row % 8 // 4 * HALF).astype(f32), NEG)
-    listed = dot(dot(up, (rank >= 0.0).astype(f32).astype(bf16)).astype(bf16), up, 1, 1) > 0.5
-    wide = jnp.where(listed, wide, NEG)
-    values = held[...]
-    lanes = values.shape[1]
-    for i in range(HALF):
-        chosen = (wide == float(i)).astype(f32).astype(bf16)
-        out[:, i * lanes : (i + 1) * lanes] = dot(chosen, values).astype(bf16)
-    mine = ranks[pl.ds(me[0], 1), :]
-    slots = targets.shape[0]
-    slot = iota((slots, sets), 0).astype(f32)
-    taken = mine == slot
+    spread = jnp.where(place == part, (code // 128).astype(f32), spread)
+    spread = jnp.where(place == part + 1, (code % 128).astype(f32), spread)
+    spread = spread.astype(bf16)
+    for z in range(out.shape[0] // total):
+        out[z * total : (z + 1) * total, :] = spread
+
+
+def plan_kernel(me, lists, lengths, ranks, slots, mine):
+    sets = lists.shape[1]
+    lists_t = lists[...].astype(f32)
+    used_t = jnp.where(iota(lists_t.shape, 0) < lengths[...], lists_t, -1.0)
+    block = iota((sets, sets), 0).astype(f32)
+    listed = jnp.zeros((sets, sets), f32)
+    for k in range(lists_t.shape[0]):
+        listed = jnp.where(used_t[k : k + 1, :] == block, 1.0, listed)
+    before = (iota((sets, sets), 0) < iota((sets, sets), 1)).astype(f32).astype(bf16)
+    rank = jnp.where(listed > 0.0, dot(listed.astype(bf16), before), -1.0)
+    ranks[...] = rank
+    number = iota((sets, sets), 1).astype(f32)
+    lane = iota(slots.shape, 1)
+    table = jnp.zeros(slots.shape, f32)
+    for i in range(CAP):
+        held = jnp.sum(jnp.where(rank == float(i), number, 0.0), axis=1, keepdims=True)
+        table = jnp.where(lane == i, held, table)
+    slots[...] = table.astype(i32)
+    own = ranks[pl.ds(me[0], 1), :]
+    count = mine.shape[0]
+    taken = own == iota((count, sets), 0).astype(f32)
     onehot = taken.astype(f32).astype(bf16)
-    expanded = dot(onehot, up, 1, 1)
-    column = iota(expanded.shape, 1) % 8
-    high = dot(jnp.where(column == 4, expanded, 0.0).astype(bf16), values).astype(i32)
-    low = dot(jnp.where(column == 5, expanded, 0.0).astype(bf16), values).astype(i32)
-    code = high * 128 + low
-    used = jnp.sum(taken.astype(f32), axis=1, keepdims=True) > 0.5
-    length = jnp.sum(jnp.where(taken, lengths[...].astype(f32), 0.0), axis=1, keepdims=True).astype(i32)
-    slot_lists = dot(onehot, lists[...].astype(f32).astype(bf16), 1, 1).astype(i32)
-    entry = code // sets_rows
+    width = lists_t.shape[0]
+    spread = (iota((width, 128), 0) == iota((width, 128), 1)).astype(f32).astype(bf16)
+    padded = dot(lists_t.astype(bf16), spread, 0, 0)
+    result = dot(onehot, padded.astype(bf16))
+    length = jnp.sum(jnp.where(taken, lengths[...].astype(f32), 0.0), axis=1, keepdims=True)
+    used = jnp.sum(taken.astype(f32), axis=1, keepdims=True)
+    lane = iota(result.shape, 1)
+    result = jnp.where(lane == width, length, result)
+    mine[...] = jnp.where(lane == width + 1, used, result)
+
+
+def pack_kernel(me, slots, held, mine, out, targets, codes, block_rows):
+    part = out.shape[0] // PARTS
+    stride = part + 8
+    first = me[0] // PARTS * PARTS
+    for p in range(PARTS):
+        for i in range(CAP):
+            start = pl.multiple_of(slots[first + p, i] * stride, 8)
+            out[p * part : (p + 1) * part, i * 128 : (i + 1) * 128] = held[pl.ds(start, part), :]
+    codes[...] = jnp.zeros(codes.shape, f32)
+    for i in range(CAP):
+        start = pl.multiple_of(slots[me[0], i] * stride + part, 8)
+        pair = held[pl.ds(start, 8), :].astype(f32)
+        codes[i : i + 1, :] = pair[0:1, :] * 128.0 + pair[1:2, :]
+    code = codes[...].astype(i32)
+    info = mine[...].astype(i32)
+    width = 8
+    length = info[:, width : width + 1]
+    used = info[:, width + 1 : width + 2] > 0
+    entry = code // block_rows
     for _ in range(3):
         entry = jnp.where(entry >= length, entry - length, entry)
     block = jnp.full(code.shape, -1, i32)
-    for k in range(slot_lists.shape[1]):
-        block = jnp.where(entry == k, slot_lists[:, k : k + 1], block)
-    here = (block == me[0]) & used
-    targets[...] = jnp.where(here, code % sets_rows, -1)
-
-
-def stats_kernel(received, table, targets, query_t, out, top_s, sum_s, tgt_s):
-    size, lanes = received.shape
-    half = size // 2
-    values = received[...]
-    row, column = iota((half, size), 0), iota((half, size), 1)
-    for h in range(2):
-        pick = (row // 4 * 8 + h * 4 + row % 4 == column).astype(f32).astype(bf16)
-        query_t[:, h * lanes : (h + 1) * lanes] = dot(pick, values).astype(bf16)
+    for k in range(width):
+        block = jnp.where(entry == k, info[:, k : k + 1], block)
+    targets[...] = jnp.where((block == me[0]) & used, code % block_rows, -1)
+
+
+def stats_kernel(query_t, table, targets, out, top_s, sum_s, tgt_s):
     top_s[...] = jnp.full(top_s.shape, NEG, f32)
     sum_s[...] = jnp.zeros(sum_s.shape, f32)
     tgt_s[...] = jnp.zeros(tgt_s.shape, f32)
@@ -196,8 +205,9 @@
     loss[...] = norm[CAP : CAP + 1, :] - target
 
 
-def grads_kernel(first, norms, targets, table, query_t, out, coefficients):
-    count = out.shape[0]
+def grads_kernel(first, norms, targets, table, query_t, early, late, coefficients):
+    half = early.shape[0]
+    count = 2 * half
     start = pl.multiple_of(first[0] * count, count)
     rows = table[pl.ds(start, count), :]
     for p in range(CAP // WIDE):
@@ -213,7 +223,8 @@
             place = iota(score.shape, 0) * 8 + c * CHUNK
             weight = jnp.where(place == wanted[None], weight - 1.0, weight)
             coefficients[c * CHUNK : (c + 1) * CHUNK, columns] = weight.reshape(CHUNK, -1).astype(bf16)
-    out[...] = dot(coefficients[...], query_t[...], 1, 1).astype(out.dtype)
+    early[...] = dot(coefficients[:half, :], query_t[...], 1, 1).astype(early.dtype)
+    late[...] = dot(coefficients[half:, :], query_t[...], 1, 1).astype(late.dtype)
 
 
 def per_device(
@@ -241,19 +252,29 @@
     kinds = relation_offsets.reshape(1, count)
     codes = target_codes.reshape(1, count)
 
-    spread, ranks = pl.pallas_call(
+    vmem = pl.BlockSpec(memory_space=pltpu.VMEM)
+    stride = depth // PARTS + 8
+    spread = pl.pallas_call(
         query_kernel,
-        out_shape=(
-            jax.ShapeDtypeStruct((owners * 8, count), bf16),
-            jax.ShapeDtypeStruct((owners, owners), f32),
-        ),
-        in_specs=[smem, pl.BlockSpec(memory_space=pltpu.HBM)] + [pl.BlockSpec(memory_space=pltpu.VMEM)] * 5,
+        out_shape=jax.ShapeDtypeStruct((owners * stride, count), bf16),
+        in_specs=[smem, pl.BlockSpec(memory_space=pltpu.HBM)] + [vmem] * 3,
         scratch_shapes=[pltpu.VMEM((count, depth), f32), pltpu.SemaphoreType.DMA],
         compiler_params=params(61),
         name="query",
-    )(head_offsets, table, relations, kinds, codes, lists, list_lengths)
-
-    held = lax.all_to_all(spread.reshape(owners, 8, count), "entity", 0, 0, tiled=True)
+    )(head_offsets, table, relations, kinds, codes)
+    held = lax.all_to_all(spread.reshape(owners, stride, count), "entity", 0, 0, tiled=True)
+
+    ranks, slots, mine = pl.pallas_call(
+        plan_kernel,
+        out_shape=(
+            jax.ShapeDtypeStruct((owners, owners), f32),
+            jax.ShapeDtypeStruct((owners, 128), i32),
+            jax.ShapeDtypeStruct((16, 128), f32),
+        ),
+        in_specs=[smem] + [vmem] * 2,
+        compiler_params=params(8),
+        name="plan",
+    )(me, lists, list_lengths)
 
     def pack(*refs):
         pack_kernel(*refs, block_rows)
@@ -261,34 +282,39 @@
     packed, targets = pl.pallas_call(
         pack,
         out_shape=(
-            jax.ShapeDtypeStruct((owners * 8, HALF * count), bf16),
+            jax.ShapeDtypeStruct((depth, CAP * count), bf16),
             jax.ShapeDtypeStruct((16, count), i32),
         ),
-        in_specs=[smem] + [pl.BlockSpec(memory_space=pltpu.VMEM)] * 4,
-        compiler_params=params(12),
+        in_specs=[smem, smem] + [vmem] * 2,
+        scratch_shapes=[pltpu.VMEM((16, count), f32)],
+        compiler_params=params(8),
         name="pack",
-    )(me, ranks, held.reshape(owners * 8, count), lists, list_lengths)
-
-    received = lax.all_to_all(packed.reshape(owners, 8, HALF * count), "entity", 0, 0, tiled=True)
+    )(me, slots, held.reshape(owners * stride, count), mine)
+    planes = [[z * PARTS + p for p in range(PARTS)] for z in range(owners // PARTS)]
+    query_t = lax.all_to_all(
+        packed.reshape(PARTS, depth // PARTS, CAP * count),
+        "entity",
+        0,
+        0,
+        tiled=True,
+        axis_index_groups=planes,
+    ).reshape(depth, CAP * count)
 
     rounded = table.astype(bf16)
-    query_t, local = pl.pallas_call(
+    local = pl.pallas_call(
         stats_kernel,
-        out_shape=(
-            jax.ShapeDtypeStruct((depth, CAP * count), bf16),
-            jax.ShapeDtypeStruct((32, count), f32),
-        ),
-        in_specs=[pl.BlockSpec(memory_space=pltpu.VMEM)] * 3,
+        out_shape=jax.ShapeDtypeStruct((32, count), f32),
+        in_specs=[vmem] * 3,
         scratch_shapes=[pltpu.VMEM((8, CAP * count), f32)] * 3,
         compiler_params=params(16),
         name="stats",
-    )(received.reshape(owners * 8, HALF * count), rounded, targets)
+    )(query_t, rounded, targets)
 
     other = lax.ppermute(local, "entity", [(i, i ^ 1) for i in range(owners)])
     share = pl.pallas_call(
         share_kernel,
         out_shape=jax.ShapeDtypeStruct((owners // 2 * 16, count), f32),
-        in_specs=[smem] + [pl.BlockSpec(memory_space=pltpu.VMEM)] * 3,
+        in_specs=[smem] + [vmem] * 3,
         compiler_params=params(8),
         name="share",
     )(me, ranks, local, other)
@@ -306,11 +332,14 @@
 
     quarter = block_rows // groups
 
-    def grads(which, dtype, norms):
+    def grads(which, early, late):
         return pl.pallas_call(
             grads_kernel,
-            out_shape=jax.ShapeDtypeStruct((quarter, depth), dtype),
-            in_specs=[smem] + [pl.BlockSpec(memory_space=pltpu.VMEM)] * 4,
+            out_shape=(
+                jax.ShapeDtypeStruct((quarter // 2, depth), early),
+                jax.ShapeDtypeStruct((quarter // 2, depth), late),
+            ),
+            in_specs=[smem] + [vmem] * 4,
             scratch_shapes=[pltpu.VMEM((quarter, CAP * count), bf16)],
             compiler_params=params(16),
             cost_estimate=pl.CostEstimate(
@@ -319,16 +348,27 @@
                 bytes_accessed=4 * quarter * depth + 4 * CAP * count * depth,
             ),
             name="grads",
-        )(which.reshape(1), norms, targets, rounded, query_t)
-
-    arrived = []
-    for shift in (2, 1, 3):
-        part = grads((group + shift) % groups, bf16, norms)
-        arrived.append(lax.ppermute(part, "dp", [(i, (i + shift) % groups) for i in range(groups)]))
-    last_norms, arrived[0] = lax.optimization_barrier((norms, arrived[0]))
-    gradient = grads(group, f32, last_norms)
-    for part in arrived:
-        gradient = gradient + part.astype(f32)
+        )((which % groups).reshape(1), norms, targets, rounded, query_t)
+
+    assert groups == 4
+
+    def up(value):
+        return lax.ppermute(value, "dp", [(i, (i + 1) % groups) for i in range(groups)])
+
+    def down(value):
+        return lax.ppermute(value, "dp", [(i, (i - 1) % groups) for i in range(groups)])
+
+    far_early, far_late = grads(group + 2, bf16, bf16)
+    relay_early, relay_late = up(far_early), down(far_late)
+    next_early, next_late = grads(group + 1, f32, bf16)
+    last_early, last_late = grads(group + 3, bf16, f32)
+    from_below_late, from_above_early = up(next_late), down(last_early)
+    own_early, own_late = grads(group, f32, f32)
+    from_below_early = up((next_early + relay_early.astype(f32)).astype(bf16))
+    from_above_late = down((last_late + relay_late.astype(f32)).astype(bf16))
+    early = own_early + from_above_early.astype(f32) + from_below_early.astype(f32)
+    late = own_late + from_below_late.astype(f32) + from_above_late.astype(f32)
+    gradient = jnp.concatenate([early, late], axis=0)
     return (loss.reshape(count), gradient[None])
 
 

time: 120 us -> 110 us (0.917); the launches traced: 119 us -> 110 us
  waiting for transfers between devices: 55.3 us -> 50 us
  local copies, waits for them, and re-layouts: 2.78 us -> 0.01 us
    ppermute x3 -> x6, waiting for transfers between devices: 11.8 us -> 6.44 us  [the longest x3 4.88 us: down(): lax.ppermute(value, 'dp', [(i, (i - 1) % groups) for i in range(groups)])]
    unnamed x12 -> x4, local copies, waits for them, and re-layouts: 2.78 us -> 0.01 us
    ppermute x3 -> x6, starting transfers between devices: 6.79 us -> 8.91 us  [the longest x3 5.54 us: down(): lax.ppermute(value, 'dp', [(i, (i - 1) % groups) for i in range(groups)])]
    pallas_call x7 -> x8, Pallas kernels: 23.6 us -> 22.8 us  [the longest x4 8.21 us: grads(): pl.pallas_call(grads_kernel, out_shape=(jax.ShapeDtypeStruct((quarter //...]
  transfers between devices with their start and end apart: 7 -> 10, of which waited for: 7 -> 8; matrix products, arithmetic and copies ran while one was open for 2% -> 2% of each run, Pallas kernels for 5% -> 6%
where the time goes in v4:
time: 110 us
  waiting for transfers between devices  50 us (45%)
  starting transfers between devices  30.4 us (28%)
  Pallas kernels  25.2 us (23%)
  other arithmetic  3.7 us (3%)
    all_to_all x1, waiting for transfers between devices, per_device(): lax.all_to_all(spread.reshape(owners, stride, count), 'entity', 0, 0, til...  19.2 us
    all_to_all x1, waiting for transfers between devices, per_device(): lax.all_to_all(share.reshape(owners // 2, 16, count), 'entity', 0, 0, til...  12.5 us
    all_to_all x1, starting transfers between devices, per_device(): lax.all_to_all(spread.reshape(owners, stride, count), 'entity', 0, 0, til...  11.6 us
    all_to_all x1, waiting for transfers between devices, per_device(): lax.all_to_all(packed.reshape(PARTS, depth // PARTS, CAP * count), 'entit...  10.8 us
    pallas_call x4, Pallas kernels, grads(): pl.pallas_call(grads_kernel, out_shape=(jax.ShapeDtypeStruct((quarter //...  8.21 us
    pallas_call x1, Pallas kernels, per_device(): pl.pallas_call(stats_kernel, out_shape=jax.ShapeDtypeStruct((32, count),...  7.68 us
    ppermute x3, starting transfers between devices, down(): lax.ppermute(value, 'dp', [(i, (i - 1) % groups) for i in range(groups)])  5.54 us
    all_to_all x1, starting transfers between devices, per_device(): lax.all_to_all(share.reshape(owners // 2, 16, count), 'entity', 0, 0, til...  5.48 us
  transfers between devices with their start and end apart: 10, of which 8 were waited for; matrix products, arithmetic and copies ran while one was open for 2% of the time, Pallas kernels for 6%

profile of v4, /device:TPU:32, one launch (start us, length us, event | category | flops | bytes accessed | tf_op | source)
XLA Modules:
  0.0 110.0 jit_solution(7584517533806386958)
XLA Ops:
  0.6 0.0 copy-start.1
  0.6 0.0 copy-start
  0.7 4.4 %query.1 = bf16[2560,128]{1,0:T(8,128)(2,1)} custom-call(s32[128]{0:T(128)} %heads.1, f32[4096,256]{1,0:T(8,128)} %bitcast.25, f32[4,256,256]{2,1,0:T(8,128)} %relations.1, s32[1,128]{1,0:T(1,128)} %bitcast.27, s32[1,128]{1,0:T(1,128)} %bitcast.28), custom_call_target="tpu_custom_call" | custom-call | tf_op jit(solution)/shard_map/query/pallas_call | solution.py:257
  5.0 11.6 %all-to-all-start = ((bf16[64,40,128]{2,1,0:T(8,128)(2,1)}), bf16[64,40,128]{2,1,0:T(8,128)(2,1)S(1)}, u32[]{:S(2)}, u32[]{:S(2)}) async-start(bf16[64,40,128]{2,1,0:T(8,128)(2,1)} %bitcast.26), calls=%async_computation | async-start | bytes 1310720 | tf_op jit(solution)/shard_map/all_to_all | solution.py:265
  16.7 0.0 copy-done.1
  16.7 0.0 copy-done
  16.7 0.3 plan.1
  17.0 19.2 %all-to-all-done = bf16[64,40,128]{2,1,0:T(8,128)(2,1)S(1)} async-done(((bf16[64,40,128]{2,1,0:T(8,128)(2,1)}), bf16[64,40,128]{2,1,0:T(8,128)(2,1)S(1)}, u32[]{:S(2)}, u32[]{:S(2)}) %all-to-all-start) | async-done | bytes 655392 | tf_op jit(solution)/shard_map/all_to_all | solution.py:265
  36.2 2.2 %pack.1 = (bf16[256,1536]{1,0:T(8,128)(2,1)}, s32[16,128]{1,0:T(8,128)S(1)}) custom-call(s32[1]{0:T(128)} %bitcast.me.refs_0_, s32[64,128]{1,0:T(8,128)S(1)} %get-tuple-element.18.refs_1_, bf16[2560,128]{1,0:T(8,128)(2,1)S(1)} %bitcast.23, f32[16,128]{1,0:T(8,128)S(1)} %get-tuple-element.19.refs_3_), custom_call_target="tpu_custom_call" | custom-call | tf_op jit(solution)/shard_map/pack/pallas_call | solution.py:282
  38.4 4.3 %all-to-all-start.1 = ((bf16[8,32,1536]{2,1,0:T(8,128)(2,1)}), bf16[8,32,1536]{2,1,0:T(8,128)(2,1)S(1)}, u32[]{:S(2)}, u32[]{:S(2)}) async-start(bf16[8,32,1536]{2,1,0:T(8,128)(2,1)} %bitcast.7), calls=%async_computation.1 | async-start | bytes 1572864 | tf_op jit(solution)/shard_map/all_to_all | solution.py:294
  42.7 2.4 %bitcast_convert_fusion.table = bf16[4096,256]{1,0:T(8,128)(2,1)S(1)} fusion(f32[1,4096,256]{2,1,0:T(8,128)} %param.7), kind=kLoop, calls=%fused_computation.5 | loop fusion | flops 1048576 | bytes 6291456 | tf_op jit(solution)/shard_map/convert_element_type | solution.py:303
  45.1 10.8 %all-to-all-done.1 = bf16[8,32,1536]{2,1,0:T(8,128)(2,1)S(1)} async-done(((bf16[8,32,1536]{2,1,0:T(8,128)(2,1)}), bf16[8,32,1536]{2,1,0:T(8,128)(2,1)S(1)}, u32[]{:S(2)}, u32[]{:S(2)}) %all-to-all-start.1) | async-done | bytes 786464 | tf_op jit(solution)/shard_map/all_to_all | solution.py:294
  55.8 7.7 %stats.1.mine = f32[32,128]{1,0:T(8,128)S(1)} custom-call(bf16[256,1536]{1,0:T(8,128)(2,1)S(1)} %bitcast.18, bf16[4096,256]{1,0:T(8,128)(2,1)S(1)} %bitcast_convert_fusion.table, s32[16,128]{1,0:T(8,128)S(1)} %get-tuple-element.21.targets), custom_call_target="tpu_custom_call" | custom-call | tf_op jit(solution)/shard_map/stats/pallas_call | solution.py:304
  63.5 0.1 collective-permute-start
  63.6 1.2 %collective-permute-done.other = f32[32,128]{1,0:T(8,128)S(1)} collective-permute-done((f32[32,128]{1,0:T(8,128)S(1)}, f32[32,128]{1,0:T(8,128)S(1)}, u32[]{:S(2)}, u32[]{:S(2)}) %collective-permute-start) | collective-permute-done | bytes 16416 | tf_op jit(solution)/shard_map/ppermute | solution.py:313
  64.8 1.8 %share.1 = f32[512,128]{1,0:T(8,128)} custom-call(s32[1]{0:T(128)} %bitcast.me.refs_0_, f32[64,64]{1,0:T(8,128)S(1)} %get-tuple-element.17.ranks, f32[32,128]{1,0:T(8,128)S(1)} %stats.1.mine, f32[32,128]{1,0:T(8,128)S(1)} %collective-permute-done.other), custom_call_target="tpu_custom_call" | custom-call | tf_op jit(solution)/shard_map/share/pallas_call | solution.py:314
  66.5 5.5 %all-to-all-start.2 = ((f32[32,16,128]{2,1,0:T(8,128)}), f32[32,16,128]{2,1,0:T(8,128)S(1)}, u32[]{:S(2)}, u32[]{:S(2)}) async-start(f32[32,16,128]{2,1,0:T(8,128)} %bitcast.9), calls=%async_computation.2 | async-start | bytes 524288 | tf_op jit(solution)/shard_map/all_to_all | solution.py:322
  72.1 12.5 %all-to-all-done.2.received = f32[32,16,128]{2,1,0:T(8,128)S(1)} async-done(((f32[32,16,128]{2,1,0:T(8,128)}), f32[32,16,128]{2,1,0:T(8,128)S(1)}, u32[]{:S(2)}, u32[]{:S(2)}) %all-to-all-start.2) | async-done | bytes 262176 | tf_op jit(solution)/shard_map/all_to_all | solution.py:322
  84.5 0.6 merge.1
  85.1 2.1 %grads.7 = (bf16[512,256]{1,0:T(8,128)(2,1)S(1)}, bf16[512,256]{1,0:T(8,128)(2,1)S(1)}) custom-call(s32[1]{0:T(128)} %bitcast.14.first, f32[16,128]{1,0:T(8,128)S(1)} %get-tuple-element.23.norms, s32[16,128]{1,0:T(8,128)S(1)} %get-tuple-element.21.targets, bf16[4096,256]{1,0:T(8,128)(2,1)S(1)} %bitcast_convert_fusion.table, bf16[256,1536]{1,0:T(8,128)(2,1)S(1)} %bitcast.19), custom_call_target="tpu_custom_call" | custom-call | flops 1610612736 | bytes 2621440 | tf_op jit(solution)/shard_map/grads/pallas_call | solution.py:336
  87.2 1.7 %collective-permute-start.2 = (bf16[512,256]{1,0:T(8,128)(2,1)S(1)}, bf16[512,256]{1,0:T(8,128)(2,1)S(1)}, u32[]{:S(2)}, u32[]{:S(2)}) collective-permute-start(bf16[512,256]{1,0:T(8,128)(2,1)S(1)} %get-tuple-element.27), channel_id=1, source_target_pairs={{0,64},{64,128},{128,192},{192,0},{1,65},{65,129},{129,193},{193,1... | collective-permute-start | bytes 786440 | tf_op jit(solution)/shard_map/ppermute | solution.py:356
  88.8 1.7 %collective-permute-start.5 = (bf16[512,256]{1,0:T(8,128)(2,1)S(1)}, bf16[512,256]{1,0:T(8,128)(2,1)S(1)}, u32[]{:S(2)}, u32[]{:S(2)}) collective-permute-start(bf16[512,256]{1,0:T(8,128)(2,1)S(1)} %get-tuple-element.31), channel_id=1, source_target_pairs={{0,192},{64,0},{128,64},{192,128},{1,193},{65,1},{129,65},{193,129... | collective-permute-start | bytes 786440 | tf_op jit(solution)/shard_map/ppermute | solution.py:359
  90.5 2.1 %grads.6 = (f32[512,256]{1,0:T(8,128)S(1)}, bf16[512,256]{1,0:T(8,128)(2,1)S(1)}) custom-call(s32[1]{0:T(128)} %bitcast.13.first, f32[16,128]{1,0:T(8,128)S(1)} %get-tuple-element.23.norms, s32[16,128]{1,0:T(8,128)S(1)} %get-tuple-element.21.targets, bf16[4096,256]{1,0:T(8,128)(2,1)S(1)} %bitcast_convert_fusion.table, bf16[256,1536]{1,0:T(8,128)(2,1)S(1)} %bitcast.20), custom_call_target="tpu_custom_call" | custom-call | flops 1610612736 | bytes 2621440 | tf_op jit(solution)/shard_map/grads/pallas_call | solution.py:336
  92.6 0.4 collective-permute-start.4
  93.0 2.0 %grads.5 = (bf16[512,256]{1,0:T(8,128)(2,1)S(1)}, f32[512,256]{1,0:T(8,128)S(1)}) custom-call(s32[1]{0:T(128)} %bitcast.12.first, f32[16,128]{1,0:T(8,128)S(1)} %get-tuple-element.23.norms, s32[16,128]{1,0:T(8,128)S(1)} %get-tuple-element.21.targets, bf16[4096,256]{1,0:T(8,128)(2,1)S(1)} %bitcast_convert_fusion.table, bf16[256,1536]{1,0:T(8,128)(2,1)S(1)} %bitcast.21), custom_call_target="tpu_custom_call" | custom-call | flops 1610612736 | bytes 2621440 | tf_op jit(solution)/shard_map/grads/pallas_call | solution.py:336
  95.0 0.2 collective-permute-done.5
  95.2 0.1 add_convert_fusion
  95.3 3.0 %collective-permute-start.6 = (bf16[512,256]{1,0:T(8,128)(2,1)S(1)}, bf16[512,256]{1,0:T(8,128)(2,1)S(1)}, u32[]{:S(2)}, u32[]{:S(2)}) collective-permute-start(bf16[512,256]{1,0:T(8,128)(2,1)S(1)} %add_convert_fusion), channel_id=1, source_target_pairs={{0,192},{64,0},{128,64},{192,128},{1,193},{65,1},{129,65},{193,129... | collective-permute-start | bytes 786440 | tf_op jit(solution)/shard_map/ppermute | solution.py:359
  98.3 2.1 %grads.4 = (f32[512,256]{1,0:T(8,128)S(1)}, f32[512,256]{1,0:T(8,128)S(1)}) custom-call(s32[1]{0:T(128)} %bitcast.11.first, f32[16,128]{1,0:T(8,128)S(1)} %get-tuple-element.23.norms, s32[16,128]{1,0:T(8,128)S(1)} %get-tuple-element.21.targets, bf16[4096,256]{1,0:T(8,128)(2,1)S(1)} %bitcast_convert_fusion.table, bf16[256,1536]{1,0:T(8,128)(2,1)S(1)} %bitcast.22), custom_call_target="tpu_custom_call" | custom-call | flops 1610612736 | bytes 2621440 | tf_op jit(solution)/shard_map/grads/pallas_call | solution.py:336
  100.3 0.9 collective-permute-start.1
  101.2 0.0 collective-permute-done.2
  101.2 0.1 add_convert_fusion.1
  101.2 1.3 %collective-permute-start.3 = (bf16[512,256]{1,0:T(8,128)(2,1)S(1)}, bf16[512,256]{1,0:T(8,128)(2,1)S(1)}, u32[]{:S(2)}, u32[]{:S(2)}) collective-permute-start(bf16[512,256]{1,0:T(8,128)(2,1)S(1)} %add_convert_fusion.1), channel_id=1, source_target_pairs={{0,64},{64,128},{128,192},{192,0},{1,65},{65,129},{129,193},{193,1... | collective-permute-start | bytes 786440 | tf_op jit(solution)/shard_map/ppermute | solution.py:356
  102.6 0.0 collective-permute-done.4
  102.6 1.4 %collective-permute-done.6 = bf16[512,256]{1,0:T(8,128)(2,1)S(1)} collective-permute-done((bf16[512,256]{1,0:T(8,128)(2,1)S(1)}, bf16[512,256]{1,0:T(8,128)(2,1)S(1)}, u32[]{:S(2)}, u32[]{:S(2)}) %collective-permute-start.6) | collective-permute-done | bytes 262176 | tf_op jit(solution)/shard_map/ppermute | solution.py:359
  104.0 0.1 convert_add_fusion
  104.1 3.3 %collective-permute-done.1 = bf16[512,256]{1,0:T(8,128)(2,1)S(1)} collective-permute-done((bf16[512,256]{1,0:T(8,128)(2,1)S(1)}, bf16[512,256]{1,0:T(8,128)(2,1)S(1)}, u32[]{:S(2)}, u32[]{:S(2)}) %collective-permute-start.1) | collective-permute-done | bytes 262176 | tf_op jit(solution)/shard_map/ppermute | solution.py:359
  107.3 1.6 %collective-permute-done.3 = bf16[512,256]{1,0:T(8,128)(2,1)S(1)} collective-permute-done((bf16[512,256]{1,0:T(8,128)(2,1)S(1)}, bf16[512,256]{1,0:T(8,128)(2,1)S(1)}, u32[]{:S(2)}, u32[]{:S(2)}) %collective-permute-start.3) | collective-permute-done | bytes 262176 | tf_op jit(solution)/shard_map/ppermute | solution.py:356
  108.9 0.1 convert_add_fusion.1
  109.0 1.0 maximum_bitcast_fusion
Async XLA Ops:
  0.6 16.0 %copy-start.1 = (s32[1,64]{1,0:T(1,128)S(1)}, s32[1,64]{1,0:T(1,128)}, u32[]{:S(2)}) copy-start(s32[1,64]{1,0:T(1,128)} %lengths.1) | copy-start | bytes 772
  0.6 16.0 %copy-start = (s32[64,8]{0,1:T(8,128)S(1)}, s32[64,8]{0,1:T(8,128)}, u32[]{:S(2)}) copy-start(s32[64,8]{0,1:T(8,128)} %param.9) | copy-start | bytes 6148
  5.0 31.1 %all-to-all-start = ((bf16[64,40,128]{2,1,0:T(8,128)(2,1)}), bf16[64,40,128]{2,1,0:T(8,128)(2,1)S(1)}, u32[]{:S(2)}, u32[]{:S(2)}) async-start(bf16[64,40,128]{2,1,0:T(8,128)(2,1)} %bitcast.26), calls=%async_computation | async-start | bytes 1310720 | tf_op jit(solution)/shard_map/all_to_all | solution.py:265
  38.4 17.4 %all-to-all-start.1 = ((bf16[8,32,1536]{2,1,0:T(8,128)(2,1)}), bf16[8,32,1536]{2,1,0:T(8,128)(2,1)S(1)}, u32[]{:S(2)}, u32[]{:S(2)}) async-start(bf16[8,32,1536]{2,1,0:T(8,128)(2,1)} %bitcast.7), calls=%async_computation.1 | async-start | bytes 1572864 | tf_op jit(solution)/shard_map/all_to_all | solution.py:294
  63.5 1.3 %collective-permute-start = (f32[32,128]{1,0:T(8,128)S(1)}, f32[32,128]{1,0:T(8,128)S(1)}, u32[]{:S(2)}, u32[]{:S(2)}) collective-permute-start(f32[32,128]{1,0:T(8,128)S(1)} %stats.1.mine), channel_id=1, source_target_pairs={{0,1},{1,0},{2,3},{3,2},{4,5},{5,4},{6,7},{7,6},{8,9},{9,8},{10,11... | collective-permute-start | bytes 49160 | tf_op jit(solution)/shard_map/ppermute | solution.py:313
  66.5 18.0 %all-to-all-start.2 = ((f32[32,16,128]{2,1,0:T(8,128)}), f32[32,16,128]{2,1,0:T(8,128)S(1)}, u32[]{:S(2)}, u32[]{:S(2)}) async-start(f32[32,16,128]{2,1,0:T(8,128)} %bitcast.9), calls=%async_computation.2 | async-start | bytes 524288 | tf_op jit(solution)/shard_map/all_to_all | solution.py:322
  87.2 14.0 %collective-permute-start.2 = (bf16[512,256]{1,0:T(8,128)(2,1)S(1)}, bf16[512,256]{1,0:T(8,128)(2,1)S(1)}, u32[]{:S(2)}, u32[]{:S(2)}) collective-permute-start(bf16[512,256]{1,0:T(8,128)(2,1)S(1)} %get-tuple-element.27), channel_id=1, source_target_pairs={{0,64},{64,128},{128,192},{192,0},{1,65},{65,129},{129,193},{193,1... | collective-permute-start | bytes 786440 | tf_op jit(solution)/shard_map/ppermute | solution.py:356
  88.8 6.4 %collective-permute-start.5 = (bf16[512,256]{1,0:T(8,128)(2,1)S(1)}, bf16[512,256]{1,0:T(8,128)(2,1)S(1)}, u32[]{:S(2)}, u32[]{:S(2)}) collective-permute-start(bf16[512,256]{1,0:T(8,128)(2,1)S(1)} %get-tuple-element.31), channel_id=1, source_target_pairs={{0,192},{64,0},{128,64},{192,128},{1,193},{65,1},{129,65},{193,129... | collective-permute-start | bytes 786440 | tf_op jit(solution)/shard_map/ppermute | solution.py:359
  92.6 10.0 %collective-permute-start.4 = (bf16[512,256]{1,0:T(8,128)(2,1)S(1)}, bf16[512,256]{1,0:T(8,128)(2,1)S(1)}, u32[]{:S(2)}, u32[]{:S(2)}) collective-permute-start(bf16[512,256]{1,0:T(8,128)(2,1)S(1)} %get-tuple-element.29), channel_id=1, source_target_pairs={{0,64},{64,128},{128,192},{192,0},{1,65},{65,129},{129,193},{193,1... | collective-permute-start | bytes 786440 | tf_op jit(solution)/shard_map/ppermute | solution.py:356
  95.3 8.7 %collective-permute-start.6 = (bf16[512,256]{1,0:T(8,128)(2,1)S(1)}, bf16[512,256]{1,0:T(8,128)(2,1)S(1)}, u32[]{:S(2)}, u32[]{:S(2)}) collective-permute-start(bf16[512,256]{1,0:T(8,128)(2,1)S(1)} %add_convert_fusion), channel_id=1, source_target_pairs={{0,192},{64,0},{128,64},{192,128},{1,193},{65,1},{129,65},{193,129... | collective-permute-start | bytes 786440 | tf_op jit(solution)/shard_map/ppermute | solution.py:359
  100.3 7.0 %collective-permute-start.1 = (bf16[512,256]{1,0:T(8,128)(2,1)S(1)}, bf16[512,256]{1,0:T(8,128)(2,1)S(1)}, u32[]{:S(2)}, u32[]{:S(2)}) collective-permute-start(bf16[512,256]{1,0:T(8,128)(2,1)S(1)} %get-tuple-element.25), channel_id=1, source_target_pairs={{0,192},{64,0},{128,64},{192,128},{1,193},{65,1},{129,65},{193,129... | collective-permute-start | bytes 786440 | tf_op jit(solution)/shard_map/ppermute | solution.py:359
  101.2 7.7 %collective-permute-start.3 = (bf16[512,256]{1,0:T(8,128)(2,1)S(1)}, bf16[512,256]{1,0:T(8,128)(2,1)S(1)}, u32[]{:S(2)}, u32[]{:S(2)}) collective-permute-start(bf16[512,256]{1,0:T(8,128)(2,1)S(1)} %add_convert_fusion.1), channel_id=1, source_target_pairs={{0,64},{64,128},{128,192},{192,0},{1,65},{65,129},{129,193},{193,1... | collective-permute-start | bytes 786440 | tf_op jit(solution)/shard_map/ppermute | solution.py:356

commit v5 on v4

--- a/solution.py
+++ b/solution.py
@@ -7,11 +7,12 @@
 
 f32, bf16, i32 = jnp.float32, jnp.bfloat16, jnp.int32
 CAP = 12
-PARTS = 8
+PARTS = 16
 WIDE = 4
 TILE = 1024
 CHUNK = 128
 NEG = -1e30
+NONE_ROW = 14
 HIGH = lax.Precision.HIGHEST
 
 
@@ -29,8 +30,10 @@
     return pl.BlockSpec(shape, lambda *_: (0,) * len(shape))
 
 
-def query_kernel(heads, table, relations, kinds, codes, out, rows, sem):
+def query_kernel(heads, table, operators, kinds, codes, out, rows, relations, sem, other_sem):
     count = rows.shape[0]
+    load = pltpu.make_async_copy(operators, relations, other_sem)
+    load.start()
 
     def fetch(n, carry):
         pltpu.make_async_copy(
@@ -48,6 +51,7 @@
     place = row % (part + 8)
     pick = (place < part) & (row // (part + 8) * part + place == column)
     pick = pick.astype(f32).astype(bf16)
+    load.wait()
     pltpu.make_async_copy(table.at[pl.ds(0, count), :], rows, sem).wait()
     head = rows[...]
     query = jnp.zeros((count, depth), f32)
@@ -64,7 +68,7 @@
         out[z * total : (z + 1) * total, :] = spread
 
 
-def plan_kernel(me, lists, lengths, ranks, slots, mine):
+def plan_kernel(me, lists, lengths, slots, mine, matches, ranks):
     sets = lists.shape[1]
     lists_t = lists[...].astype(f32)
     used_t = jnp.where(iota(lists_t.shape, 0) < lengths[...], lists_t, -1.0)
@@ -75,11 +79,12 @@
     before = (iota((sets, sets), 0) < iota((sets, sets), 1)).astype(f32).astype(bf16)
     rank = jnp.where(listed > 0.0, dot(listed.astype(bf16), before), -1.0)
     ranks[...] = rank
-    number = iota((sets, sets), 1).astype(f32)
+    group = ranks[pl.ds(pl.multiple_of(me[0] // PARTS * PARTS, PARTS), PARTS), :]
+    number = iota(group.shape, 1).astype(f32)
     lane = iota(slots.shape, 1)
     table = jnp.zeros(slots.shape, f32)
     for i in range(CAP):
-        held = jnp.sum(jnp.where(rank == float(i), number, 0.0), axis=1, keepdims=True)
+        held = jnp.sum(jnp.where(group == float(i), number, 0.0), axis=1, keepdims=True)
         table = jnp.where(lane == i, held, table)
     slots[...] = table.astype(i32)
     own = ranks[pl.ds(me[0], 1), :]
@@ -95,19 +100,35 @@
     lane = iota(result.shape, 1)
     result = jnp.where(lane == width, length, result)
     mine[...] = jnp.where(lane == width + 1, used, result)
+    total = matches.shape[1]
+    core = me[0] % 2
+    row = iota((total, sets), 0)
+    up = (row // 16 * 2 + core == iota((total, sets), 1)).astype(f32)
+    wide = dot(up.astype(bf16), rank.astype(bf16))
+    slot = row % 16
+    shared = (wide == slot.astype(f32)) & (slot < CAP)
+    shared = shared | (((slot == CAP) | (slot == CAP + 1)) & (up > 0.5))
+    shared = shared.astype(f32).astype(bf16)
+    slot, source = iota((total, 32), 0) % 16, iota((total, 32), 1)
+    keep = (slot == CAP + 1) == (source >= 16)
+    for which, owner in enumerate((me[0], me[0] + 1 - 2 * core)):
+        owned = ranks[pl.ds(owner, 1), :] == (iota((32, sets), 0) % 16).astype(f32)
+        match = jnp.where(keep, dot(shared, owned.astype(f32).astype(bf16), 1, 1), 0.0)
+        found = jnp.sum(match, axis=1, keepdims=True) > 0.5
+        nothing = (source == NONE_ROW) & (slot != CAP + 1) & jnp.logical_not(found)
+        matches[which] = jnp.where(nothing, 1.0, match)
 
 
 def pack_kernel(me, slots, held, mine, out, targets, codes, block_rows):
     part = out.shape[0] // PARTS
     stride = part + 8
-    first = me[0] // PARTS * PARTS
     for p in range(PARTS):
         for i in range(CAP):
-            start = pl.multiple_of(slots[first + p, i] * stride, 8)
+            start = pl.multiple_of(slots[p, i] * stride, 8)
             out[p * part : (p + 1) * part, i * 128 : (i + 1) * 128] = held[pl.ds(start, part), :]
     codes[...] = jnp.zeros(codes.shape, f32)
     for i in range(CAP):
-        start = pl.multiple_of(slots[me[0], i] * stride + part, 8)
+        start = pl.multiple_of(slots[me[0] % PARTS, i] * stride + part, 8)
         pair = held[pl.ds(start, 8), :].astype(f32)
         codes[i : i + 1, :] = pair[0:1, :] * 128.0 + pair[1:2, :]
     code = codes[...].astype(i32)
@@ -154,7 +175,7 @@
     mass = jnp.sum(sum_s[...] * jnp.exp(top - best), axis=0, keepdims=True)
     local = best + jnp.log(mass)
     picked = jnp.sum(tgt_s[...], axis=0, keepdims=True)
-    out[...] = jnp.zeros(out.shape, f32)
+    out[...] = jnp.where(iota(out.shape, 0) == NONE_ROW, NEG, 0.0)
     for i in range(CAP):
         out[i : i + 1, :] = local[:, i * 128 : (i + 1) * 128]
         out[16 + i : 17 + i, :] = picked[:, i * 128 : (i + 1) * 128]
@@ -164,32 +185,10 @@
     return jnp.concatenate([ref[i : i + 1, :] for i in range(WIDE * p, WIDE * p + WIDE)], axis=1)
 
 
-def share_kernel(me, ranks, mine, other, out):
-    sets = ranks.shape[0]
-    total = out.shape[0]
-    core = me[0] % 2
-    rank = ranks[...]
-    row = iota((total, sets), 0)
-    place = row // 16 * 2 + core
-    up = (place == iota((total, sets), 1)).astype(f32)
-    wide = dot(up.astype(bf16), rank.astype(bf16))
-    slot = row % 16
-    shared = (wide == slot.astype(f32)) & (slot < CAP)
-    shared = shared | (((slot == CAP) | (slot == CAP + 1)) & (up > 0.5))
-    shared = shared.astype(f32).astype(bf16)
-    slot, source = iota((total, 32), 0) % 16, iota((total, 32), 1)
-    keep = (slot == CAP + 1) == (source >= 16)
-    wants_target = iota((total, 128), 0) % 16 == CAP + 1
-
-    def rows_of(owner, values):
-        owned = ranks[pl.ds(owner, 1), :] == (iota((32, sets), 0) % 16).astype(f32)
-        match = jnp.where(keep, dot(shared, owned.astype(f32).astype(bf16), 1, 1), 0.0)
-        found = dot(match, values[...], precision=HIGH)
-        present = dot(match.astype(bf16), jnp.ones((32, 128), bf16))
-        return jnp.where(present > 0.5, found, jnp.where(wants_target, 0.0, NEG))
-
-    first = rows_of(me[0], mine)
-    second = rows_of(me[0] + 1 - 2 * core, other)
+def share_kernel(matches, mine, other, out):
+    wants_target = iota(out.shape, 0) % 16 == CAP + 1
+    first = dot(matches[0], mine[...], precision=HIGH)
+    second = dot(matches[1], other[...], precision=HIGH)
     best = jnp.maximum(first, second)
     both = best + jnp.log(jnp.exp(first - best) + jnp.exp(second - best))
     out[...] = jnp.where(wants_target, first + second, both)
@@ -257,21 +256,28 @@
     spread = pl.pallas_call(
         query_kernel,
         out_shape=jax.ShapeDtypeStruct((owners * stride, count), bf16),
-        in_specs=[smem, pl.BlockSpec(memory_space=pltpu.HBM)] + [vmem] * 3,
-        scratch_shapes=[pltpu.VMEM((count, depth), f32), pltpu.SemaphoreType.DMA],
+        in_specs=[smem] + [pl.BlockSpec(memory_space=pltpu.HBM)] * 2 + [vmem] * 2,
+        scratch_shapes=[
+            pltpu.VMEM((count, depth), f32),
+            pltpu.VMEM(relations.shape, f32),
+            pltpu.SemaphoreType.DMA,
+            pltpu.SemaphoreType.DMA,
+        ],
         compiler_params=params(61),
         name="query",
     )(head_offsets, table, relations, kinds, codes)
     held = lax.all_to_all(spread.reshape(owners, stride, count), "entity", 0, 0, tiled=True)
 
-    ranks, slots, mine = pl.pallas_call(
+    share_rows = owners // 2 * 16
+    slots, mine, matches = pl.pallas_call(
         plan_kernel,
         out_shape=(
-            jax.ShapeDtypeStruct((owners, owners), f32),
-            jax.ShapeDtypeStruct((owners, 128), i32),
+            jax.ShapeDtypeStruct((PARTS, 128), i32),
             jax.ShapeDtypeStruct((16, 128), f32),
+            jax.ShapeDtypeStruct((2, share_rows, 32), f32),
         ),
         in_specs=[smem] + [vmem] * 2,
+        scratch_shapes=[pltpu.VMEM((owners, owners), f32)],
         compiler_params=params(8),
         name="plan",
     )(me, lists, list_lengths)
@@ -313,11 +319,11 @@
     other = lax.ppermute(local, "entity", [(i, i ^ 1) for i in range(owners)])
     share = pl.pallas_call(
         share_kernel,
-        out_shape=jax.ShapeDtypeStruct((owners // 2 * 16, count), f32),
-        in_specs=[smem] + [vmem] * 3,
+        out_shape=jax.ShapeDtypeStruct((share_rows, count), f32),
+        in_specs=[vmem] * 3,
         compiler_params=params(8),
         name="share",
-    )(me, ranks, local, other)
+    )(matches, local, other)
     cores = [[i for i in range(owners) if i % 2 == core] for core in range(2)]
     shared = lax.all_to_all(
         share.reshape(owners // 2, 16, count), "entity", 0, 0, tiled=True, axis_index_groups=cores
@@ -332,7 +338,7 @@
 
     quarter = block_rows // groups
 
-    def grads(which, early, late):
+    def grads(which, early, late, norms=norms):
         return pl.pallas_call(
             grads_kernel,
             out_shape=(
@@ -363,9 +369,11 @@
     next_early, next_late = grads(group + 1, f32, bf16)
     last_early, last_late = grads(group + 3, bf16, f32)
     from_below_late, from_above_early = up(next_late), down(last_early)
-    own_early, own_late = grads(group, f32, f32)
-    from_below_early = up((next_early + relay_early.astype(f32)).astype(bf16))
-    from_above_late = down((last_late + relay_late.astype(f32)).astype(bf16))
+    next_early = (next_early + relay_early.astype(f32)).astype(bf16)
+    last_late = (last_late + relay_late.astype(f32)).astype(bf16)
+    from_below_early, from_above_late = up(next_early), down(last_late)
+    own_norms, next_early, last_late = lax.optimization_barrier((norms, next_early, last_late))
+    own_early, own_late = grads(group, f32, f32, own_norms)
     early = own_early + from_above_early.astype(f32) + from_below_early.astype(f32)
     late = own_late + from_below_late.astype(f32) + from_above_late.astype(f32)
     gradient = jnp.concatenate([early, late], axis=0)

time: 110 us -> 105 us (0.955)
  waiting for transfers between devices: 50 us -> 43.4 us
  starting transfers between devices: 30.4 us -> 32.1 us
    all_to_all x1, waiting for transfers between devices: 19.2 us -> 13.4 us  [per_device(): lax.all_to_all(spread.reshape(owners, stride, count), 'entity', 0, 0, til...]
    ppermute x3, waiting for transfers between devices: 4.88 us -> 0.01 us  [down(): lax.ppermute(value, 'dp', [(i, (i - 1) % groups) for i in range(groups)])]
    ppermute x3, waiting for transfers between devices: 1.57 us -> 6.26 us  [up(): lax.ppermute(value, 'dp', [(i, (i + 1) % groups) for i in range(groups)])]
    ppermute x3, starting transfers between devices: 5.54 us -> 7.02 us  [down(): lax.ppermute(value, 'dp', [(i, (i - 1) % groups) for i in range(groups)])]
    all_to_all x1, starting transfers between devices: 4.27 us -> 5.74 us  [per_device(): lax.all_to_all(packed.reshape(PARTS, depth // PARTS, CAP * count), 'entit...]
  transfers between devices with their start and end apart: 10 -> 10, of which waited for: 8 -> 5; matrix products, arithmetic and copies ran while one was open for 2% -> 2% of each run, Pallas kernels for 6% -> 6%
where the time goes in v5:
time: 105 us
  waiting for transfers between devices  43.4 us (41%)
  starting transfers between devices  32.1 us (31%)
  Pallas kernels  24.4 us (23%)
  other arithmetic  3.69 us (4%)
    all_to_all x1, waiting for transfers between devices, per_device(): lax.all_to_all(spread.reshape(owners, stride, count), 'entity', 0, 0, til...  13.4 us
    all_to_all x1, waiting for transfers between devices, per_device(): lax.all_to_all(share.reshape(owners // 2, 16, count), 'entity', 0, 0, til...  12.6 us
    all_to_all x1, starting transfers between devices, per_device(): lax.all_to_all(spread.reshape(owners, stride, count), 'entity', 0, 0, til...  11.6 us
    all_to_all x1, waiting for transfers between devices, per_device(): lax.all_to_all(packed.reshape(PARTS, depth // PARTS, CAP * count), 'entit...  9.96 us
    pallas_call x4, Pallas kernels, grads(): pl.pallas_call(grads_kernel, out_shape=(jax.ShapeDtypeStruct((quarter //...  8.2 us
    pallas_call x1, Pallas kernels, per_device(): pl.pallas_call(stats_kernel, out_shape=jax.ShapeDtypeStruct((32, count),...  7.78 us
    ppermute x3, starting transfers between devices, down(): lax.ppermute(value, 'dp', [(i, (i - 1) % groups) for i in range(groups)])  7.02 us
    ppermute x3, waiting for transfers between devices, up(): lax.ppermute(value, 'dp', [(i, (i + 1) % groups) for i in range(groups)])  6.26 us
  transfers between devices with their start and end apart: 10, of which 5 were waited for; matrix products, arithmetic and copies ran while one was open for 2% of the time, Pallas kernels for 6%

profile of v5, /device:TPU:32, one launch (start us, length us, event | category | flops | bytes accessed | tf_op | source)
XLA Modules:
  0.0 104.5 jit_solution(3087398017203796763)
XLA Ops:
  0.6 0.0 copy-start.1
  0.6 0.0 copy-start
  0.7 4.1 %query.1 = bf16[1536,128]{1,0:T(8,128)(2,1)} custom-call(s32[128]{0:T(128)} %heads.1, f32[4096,256]{1,0:T(8,128)} %bitcast.25, f32[4,256,256]{2,1,0:T(8,128)} %operators.1, s32[1,128]{1,0:T(1,128)} %bitcast.27, s32[1,128]{1,0:T(1,128)} %bitcast.28), custom_call_target="tpu_custom_call" | custom-call | tf_op jit(solution)/shard_map/query/pallas_call | solution.py:256
  4.7 11.6 %all-to-all-start = ((bf16[64,24,128]{2,1,0:T(8,128)(2,1)}), bf16[64,24,128]{2,1,0:T(8,128)(2,1)S(1)}, u32[]{:S(2)}, u32[]{:S(2)}) async-start(bf16[64,24,128]{2,1,0:T(8,128)(2,1)} %bitcast.26), calls=%async_computation | async-start | bytes 786432 | tf_op jit(solution)/shard_map/all_to_all | solution.py:269
  16.3 0.0 copy-done.1
  16.3 0.0 copy-done
  16.3 0.6 plan.1
  17.0 13.4 %all-to-all-done = bf16[64,24,128]{2,1,0:T(8,128)(2,1)S(1)} async-done(((bf16[64,24,128]{2,1,0:T(8,128)(2,1)}), bf16[64,24,128]{2,1,0:T(8,128)(2,1)S(1)}, u32[]{:S(2)}, u32[]{:S(2)}) %all-to-all-start) | async-done | bytes 393248 | tf_op jit(solution)/shard_map/all_to_all | solution.py:269
  30.4 1.9 %pack.1 = (bf16[256,1536]{1,0:T(8,128)(2,1)}, s32[16,128]{1,0:T(8,128)S(1)}) custom-call(s32[1]{0:T(128)} %bitcast.me.refs_0_, s32[16,128]{1,0:T(8,128)S(1)} %get-tuple-element.19.refs_1_, bf16[1536,128]{1,0:T(8,128)(2,1)S(1)} %bitcast.23, f32[16,128]{1,0:T(8,128)S(1)} %get-tuple-element.20.refs_3_), custom_call_target="tpu_custom_call" | custom-call | tf_op jit(solution)/shard_map/pack/pallas_call | solution.py:288
  32.3 5.7 %all-to-all-start.1 = ((bf16[16,16,1536]{2,1,0:T(8,128)(2,1)}), bf16[16,16,1536]{2,1,0:T(8,128)(2,1)S(1)}, u32[]{:S(2)}, u32[]{:S(2)}) async-start(bf16[16,16,1536]{2,1,0:T(8,128)(2,1)} %bitcast.7), calls=%async_computation.1 | async-start | bytes 1572864 | tf_op jit(solution)/shard_map/all_to_all | solution.py:300
  38.0 2.4 %bitcast_convert_fusion.table = bf16[4096,256]{1,0:T(8,128)(2,1)S(1)} fusion(f32[1,4096,256]{2,1,0:T(8,128)} %param.7), kind=kLoop, calls=%fused_computation.5 | loop fusion | flops 1048576 | bytes 6291456 | tf_op jit(solution)/shard_map/convert_element_type | solution.py:309
  40.4 10.0 %all-to-all-done.1 = bf16[16,16,1536]{2,1,0:T(8,128)(2,1)S(1)} async-done(((bf16[16,16,1536]{2,1,0:T(8,128)(2,1)}), bf16[16,16,1536]{2,1,0:T(8,128)(2,1)S(1)}, u32[]{:S(2)}, u32[]{:S(2)}) %all-to-all-start.1) | async-done | bytes 786464 | tf_op jit(solution)/shard_map/all_to_all | solution.py:300
  50.4 7.8 %stats.1.mine = f32[32,128]{1,0:T(8,128)S(1)} custom-call(bf16[256,1536]{1,0:T(8,128)(2,1)S(1)} %bitcast.18, bf16[4096,256]{1,0:T(8,128)(2,1)S(1)} %bitcast_convert_fusion.table, s32[16,128]{1,0:T(8,128)S(1)} %get-tuple-element.22.targets), custom_call_target="tpu_custom_call" | custom-call | tf_op jit(solution)/shard_map/stats/pallas_call | solution.py:310
  58.2 0.1 collective-permute-start
  58.3 1.2 %collective-permute-done.other = f32[32,128]{1,0:T(8,128)S(1)} collective-permute-done((f32[32,128]{1,0:T(8,128)S(1)}, f32[32,128]{1,0:T(8,128)S(1)}, u32[]{:S(2)}, u32[]{:S(2)}) %collective-permute-start) | collective-permute-done | bytes 16416 | tf_op jit(solution)/shard_map/ppermute | solution.py:319
  59.4 1.3 %share.1 = f32[512,128]{1,0:T(8,128)} custom-call(f32[2,512,32]{2,1,0:T(8,128)S(1)} %get-tuple-element.18.matches, f32[32,128]{1,0:T(8,128)S(1)} %stats.1.mine, f32[32,128]{1,0:T(8,128)S(1)} %collective-permute-done.other), custom_call_target="tpu_custom_call" | custom-call | tf_op jit(solution)/shard_map/share/pallas_call | solution.py:320
  60.8 5.3 %all-to-all-start.2 = ((f32[32,16,128]{2,1,0:T(8,128)}), f32[32,16,128]{2,1,0:T(8,128)S(1)}, u32[]{:S(2)}, u32[]{:S(2)}) async-start(f32[32,16,128]{2,1,0:T(8,128)} %bitcast.9), calls=%async_computation.2 | async-start | bytes 524288 | tf_op jit(solution)/shard_map/all_to_all | solution.py:328
  66.1 12.6 %all-to-all-done.2.received = f32[32,16,128]{2,1,0:T(8,128)S(1)} async-done(((f32[32,16,128]{2,1,0:T(8,128)}), f32[32,16,128]{2,1,0:T(8,128)S(1)}, u32[]{:S(2)}, u32[]{:S(2)}) %all-to-all-start.2) | async-done | bytes 262176 | tf_op jit(solution)/shard_map/all_to_all | solution.py:328
  78.7 0.6 merge.1
  79.3 2.1 %grads.5 = (bf16[512,256]{1,0:T(8,128)(2,1)S(1)}, bf16[512,256]{1,0:T(8,128)(2,1)S(1)}) custom-call(s32[1]{0:T(128)} %bitcast.13.first, f32[16,128]{1,0:T(8,128)S(1)} %get-tuple-element.29.norms, s32[16,128]{1,0:T(8,128)S(1)} %get-tuple-element.22.targets, bf16[4096,256]{1,0:T(8,128)(2,1)S(1)} %bitcast_convert_fusion.table, bf16[256,1536]{1,0:T(8,128)(2,1)S(1)} %bitcast.19), custom_call_target="tpu_custom_call" | custom-call | flops 1610612736 | bytes 2621440 | tf_op jit(solution)/shard_map/grads/pallas_call | solution.py:342
  81.3 1.6 %collective-permute-start.1 = (bf16[512,256]{1,0:T(8,128)(2,1)S(1)}, bf16[512,256]{1,0:T(8,128)(2,1)S(1)}, u32[]{:S(2)}, u32[]{:S(2)}) collective-permute-start(bf16[512,256]{1,0:T(8,128)(2,1)S(1)} %get-tuple-element.26), channel_id=1, source_target_pairs={{0,64},{64,128},{128,192},{192,0},{1,65},{65,129},{129,193},{193,1... | collective-permute-start | bytes 786440 | tf_op jit(solution)/shard_map/ppermute | solution.py:362
  83.0 1.7 %collective-permute-start.2 = (bf16[512,256]{1,0:T(8,128)(2,1)S(1)}, bf16[512,256]{1,0:T(8,128)(2,1)S(1)}, u32[]{:S(2)}, u32[]{:S(2)}) collective-permute-start(bf16[512,256]{1,0:T(8,128)(2,1)S(1)} %get-tuple-element.28), channel_id=1, source_target_pairs={{0,192},{64,0},{128,64},{192,128},{1,193},{65,1},{129,65},{193,129... | collective-permute-start | bytes 786440 | tf_op jit(solution)/shard_map/ppermute | solution.py:365
  84.7 2.0 %grads.6 = (bf16[512,256]{1,0:T(8,128)(2,1)S(1)}, f32[512,256]{1,0:T(8,128)S(1)}) custom-call(s32[1]{0:T(128)} %bitcast.14.first, f32[16,128]{1,0:T(8,128)S(1)} %get-tuple-element.29.norms, s32[16,128]{1,0:T(8,128)S(1)} %get-tuple-element.22.targets, bf16[4096,256]{1,0:T(8,128)(2,1)S(1)} %bitcast_convert_fusion.table, bf16[256,1536]{1,0:T(8,128)(2,1)S(1)} %bitcast.20), custom_call_target="tpu_custom_call" | custom-call | flops 1610612736 | bytes 2621440 | tf_op jit(solution)/shard_map/grads/pallas_call | solution.py:342
  86.8 1.8 %collective-permute-start.3 = (bf16[512,256]{1,0:T(8,128)(2,1)S(1)}, bf16[512,256]{1,0:T(8,128)(2,1)S(1)}, u32[]{:S(2)}, u32[]{:S(2)}) collective-permute-start(bf16[512,256]{1,0:T(8,128)(2,1)S(1)} %get-tuple-element.31), channel_id=1, source_target_pairs={{0,192},{64,0},{128,64},{192,128},{1,193},{65,1},{129,65},{193,129... | collective-permute-start | bytes 786440 | tf_op jit(solution)/shard_map/ppermute | solution.py:365
  88.6 2.1 %grads.4 = (f32[512,256]{1,0:T(8,128)S(1)}, bf16[512,256]{1,0:T(8,128)(2,1)S(1)}) custom-call(s32[1]{0:T(128)} %bitcast.12.first, f32[16,128]{1,0:T(8,128)S(1)} %get-tuple-element.29.norms, s32[16,128]{1,0:T(8,128)S(1)} %get-tuple-element.22.targets, bf16[4096,256]{1,0:T(8,128)(2,1)S(1)} %bitcast_convert_fusion.table, bf16[256,1536]{1,0:T(8,128)(2,1)S(1)} %bitcast.21), custom_call_target="tpu_custom_call" | custom-call | flops 1610612736 | bytes 2621440 | tf_op jit(solution)/shard_map/grads/pallas_call | solution.py:342
  90.7 0.4 collective-permute-start.5
  91.0 0.0 collective-permute-done.1
  91.0 0.1 add_convert_fusion.1
  91.1 0.4 collective-permute-start.4
  91.4 0.0 collective-permute-done.2
  91.4 0.1 add_convert_fusion
  91.5 3.5 %collective-permute-start.6 = (bf16[512,256]{1,0:T(8,128)(2,1)S(1)}, bf16[512,256]{1,0:T(8,128)(2,1)S(1)}, u32[]{:S(2)}, u32[]{:S(2)}) collective-permute-start(bf16[512,256]{1,0:T(8,128)(2,1)S(1)} %add_convert_fusion), channel_id=1, source_target_pairs={{0,192},{64,0},{128,64},{192,128},{1,193},{65,1},{129,65},{193,129... | collective-permute-start | bytes 786440 | tf_op jit(solution)/shard_map/ppermute | solution.py:365
  95.0 2.0 %grads.7 = (f32[512,256]{1,0:T(8,128)S(1)}, f32[512,256]{1,0:T(8,128)S(1)}) custom-call(s32[1]{0:T(128)} %bitcast.11.first, f32[16,128]{1,0:T(8,128)S(1)} %get-tuple-element.29.norms, s32[16,128]{1,0:T(8,128)S(1)} %get-tuple-element.22.targets, bf16[4096,256]{1,0:T(8,128)(2,1)S(1)} %bitcast_convert_fusion.table, bf16[256,1536]{1,0:T(8,128)(2,1)S(1)} %bitcast.22), custom_call_target="tpu_custom_call" | custom-call | flops 1610612736 | bytes 2621440 | tf_op jit(solution)/shard_map/grads/pallas_call | solution.py:342
  97.0 0.0 collective-permute-done.3
  97.0 6.3 %collective-permute-done.4 = bf16[512,256]{1,0:T(8,128)(2,1)S(1)} collective-permute-done((bf16[512,256]{1,0:T(8,128)(2,1)S(1)}, bf16[512,256]{1,0:T(8,128)(2,1)S(1)}, u32[]{:S(2)}, u32[]{:S(2)}) %collective-permute-start.4) | collective-permute-done | bytes 262176 | tf_op jit(solution)/shard_map/ppermute | solution.py:362
  103.3 0.1 convert_add_fusion.1
  103.4 0.0 collective-permute-done.5
  103.4 0.0 collective-permute-done.6
  103.4 0.1 convert_add_fusion
  103.5 1.0 maximum_bitcast_fusion
Async XLA Ops:
  0.6 15.7 %copy-start.1 = (s32[1,64]{1,0:T(1,128)S(1)}, s32[1,64]{1,0:T(1,128)}, u32[]{:S(2)}) copy-start(s32[1,64]{1,0:T(1,128)} %lengths.1) | copy-start | bytes 772
  0.6 15.7 %copy-start = (s32[64,8]{0,1:T(8,128)S(1)}, s32[64,8]{0,1:T(8,128)}, u32[]{:S(2)}) copy-start(s32[64,8]{0,1:T(8,128)} %param.9) | copy-start | bytes 6148
  4.7 25.7 %all-to-all-start = ((bf16[64,24,128]{2,1,0:T(8,128)(2,1)}), bf16[64,24,128]{2,1,0:T(8,128)(2,1)S(1)}, u32[]{:S(2)}, u32[]{:S(2)}) async-start(bf16[64,24,128]{2,1,0:T(8,128)(2,1)} %bitcast.26), calls=%async_computation | async-start | bytes 786432 | tf_op jit(solution)/shard_map/all_to_all | solution.py:269
  32.3 18.1 %all-to-all-start.1 = ((bf16[16,16,1536]{2,1,0:T(8,128)(2,1)}), bf16[16,16,1536]{2,1,0:T(8,128)(2,1)S(1)}, u32[]{:S(2)}, u32[]{:S(2)}) async-start(bf16[16,16,1536]{2,1,0:T(8,128)(2,1)} %bitcast.7), calls=%async_computation.1 | async-start | bytes 1572864 | tf_op jit(solution)/shard_map/all_to_all | solution.py:300
  58.2 1.3 %collective-permute-start = (f32[32,128]{1,0:T(8,128)S(1)}, f32[32,128]{1,0:T(8,128)S(1)}, u32[]{:S(2)}, u32[]{:S(2)}) collective-permute-start(f32[32,128]{1,0:T(8,128)S(1)} %stats.1.mine), channel_id=1, source_target_pairs={{0,1},{1,0},{2,3},{3,2},{4,5},{5,4},{6,7},{7,6},{8,9},{9,8},{10,11... | collective-permute-start | bytes 49160 | tf_op jit(solution)/shard_map/ppermute | solution.py:319
  60.8 17.9 %all-to-all-start.2 = ((f32[32,16,128]{2,1,0:T(8,128)}), f32[32,16,128]{2,1,0:T(8,128)S(1)}, u32[]{:S(2)}, u32[]{:S(2)}) async-start(f32[32,16,128]{2,1,0:T(8,128)} %bitcast.9), calls=%async_computation.2 | async-start | bytes 524288 | tf_op jit(solution)/shard_map/all_to_all | solution.py:328
  81.3 9.7 %collective-permute-start.1 = (bf16[512,256]{1,0:T(8,128)(2,1)S(1)}, bf16[512,256]{1,0:T(8,128)(2,1)S(1)}, u32[]{:S(2)}, u32[]{:S(2)}) collective-permute-start(bf16[512,256]{1,0:T(8,128)(2,1)S(1)} %get-tuple-element.26), channel_id=1, source_target_pairs={{0,64},{64,128},{128,192},{192,0},{1,65},{65,129},{129,193},{193,1... | collective-permute-start | bytes 786440 | tf_op jit(solution)/shard_map/ppermute | solution.py:362
  83.0 8.5 %collective-permute-start.2 = (bf16[512,256]{1,0:T(8,128)(2,1)S(1)}, bf16[512,256]{1,0:T(8,128)(2,1)S(1)}, u32[]{:S(2)}, u32[]{:S(2)}) collective-permute-start(bf16[512,256]{1,0:T(8,128)(2,1)S(1)} %get-tuple-element.28), channel_id=1, source_target_pairs={{0,192},{64,0},{128,64},{192,128},{1,193},{65,1},{129,65},{193,129... | collective-permute-start | bytes 786440 | tf_op jit(solution)/shard_map/ppermute | solution.py:365
  86.8 10.3 %collective-permute-start.3 = (bf16[512,256]{1,0:T(8,128)(2,1)S(1)}, bf16[512,256]{1,0:T(8,128)(2,1)S(1)}, u32[]{:S(2)}, u32[]{:S(2)}) collective-permute-start(bf16[512,256]{1,0:T(8,128)(2,1)S(1)} %get-tuple-element.31), channel_id=1, source_target_pairs={{0,192},{64,0},{128,64},{192,128},{1,193},{65,1},{129,65},{193,129... | collective-permute-start | bytes 786440 | tf_op jit(solution)/shard_map/ppermute | solution.py:365
  90.7 12.7 %collective-permute-start.5 = (bf16[512,256]{1,0:T(8,128)(2,1)S(1)}, bf16[512,256]{1,0:T(8,128)(2,1)S(1)}, u32[]{:S(2)}, u32[]{:S(2)}) collective-permute-start(bf16[512,256]{1,0:T(8,128)(2,1)S(1)} %get-tuple-element.33), channel_id=1, source_target_pairs={{0,64},{64,128},{128,192},{192,0},{1,65},{65,129},{129,193},{193,1... | collective-permute-start | bytes 786440 | tf_op jit(solution)/shard_map/ppermute | solution.py:362
  91.1 12.2 %collective-permute-start.4 = (bf16[512,256]{1,0:T(8,128)(2,1)S(1)}, bf16[512,256]{1,0:T(8,128)(2,1)S(1)}, u32[]{:S(2)}, u32[]{:S(2)}) collective-permute-start(bf16[512,256]{1,0:T(8,128)(2,1)S(1)} %add_convert_fusion.1), channel_id=1, source_target_pairs={{0,64},{64,128},{128,192},{192,0},{1,65},{65,129},{129,193},{193,1... | collective-permute-start | bytes 786440 | tf_op jit(solution)/shard_map/ppermute | solution.py:362
  91.5 11.9 %collective-permute-start.6 = (bf16[512,256]{1,0:T(8,128)(2,1)S(1)}, bf16[512,256]{1,0:T(8,128)(2,1)S(1)}, u32[]{:S(2)}, u32[]{:S(2)}) collective-permute-start(bf16[512,256]{1,0:T(8,128)(2,1)S(1)} %add_convert_fusion), channel_id=1, source_target_pairs={{0,192},{64,0},{128,64},{192,128},{1,193},{65,1},{129,65},{193,129... | collective-permute-start | bytes 786440 | tf_op jit(solution)/shard_map/ppermute | solution.py:365

commit v6 on v5

--- a/solution.py
+++ b/solution.py
@@ -181,8 +181,9 @@
         out[16 + i : 17 + i, :] = picked[:, i * 128 : (i + 1) * 128]
 
 
-def slot_lanes(ref, p):
-    return jnp.concatenate([ref[i : i + 1, :] for i in range(WIDE * p, WIDE * p + WIDE)], axis=1)
+def slot_lanes(ref, p, base=0):
+    first = base + WIDE * p
+    return jnp.concatenate([ref[i : i + 1, :] for i in range(first, first + WIDE)], axis=1)
 
 
 def share_kernel(matches, mine, other, out):
@@ -194,26 +195,24 @@
     out[...] = jnp.where(wants_target, first + second, both)
 
 
-def merge_kernel(received, norms, loss):
+def merge_kernel(received, targets, info, loss):
     values = received[...]
     best = jnp.max(values, axis=0)
     mass = jnp.sum(jnp.exp(values - best[None]), axis=0)
     norm = best + jnp.log(mass)
-    norms[...] = jnp.where(best <= 0.5 * NEG, -NEG, norm)
+    info[0:16, :] = jnp.where(best <= 0.5 * NEG, -NEG, norm)
+    info[16:32, :] = targets[...].astype(f32)
     target = jnp.sum(values[:, CAP + 1, :], axis=0, keepdims=True)
     loss[...] = norm[CAP : CAP + 1, :] - target
 
 
-def grads_kernel(first, norms, targets, table, query_t, early, late, coefficients):
-    half = early.shape[0]
-    count = 2 * half
-    start = pl.multiple_of(first[0] * count, count)
-    rows = table[pl.ds(start, count), :]
+def rows_gradient(start, rows, info, query_t, coefficients):
+    count = rows.shape[0]
     for p in range(CAP // WIDE):
         columns = slice(p * WIDE * 128, (p + 1) * WIDE * 128)
         weights = query_t[:, columns]
-        norm = slot_lanes(norms, p)
-        target = slot_lanes(targets, p)
+        norm = slot_lanes(info, p)
+        target = slot_lanes(info, p, 16).astype(i32)
         wanted = target - iota((8, target.shape[1]), 0) - start
         for c in range(count // CHUNK):
             score = dot(rows[c * CHUNK : (c + 1) * CHUNK, :], weights)
@@ -222,8 +221,48 @@
             place = iota(score.shape, 0) * 8 + c * CHUNK
             weight = jnp.where(place == wanted[None], weight - 1.0, weight)
             coefficients[c * CHUNK : (c + 1) * CHUNK, columns] = weight.reshape(CHUNK, -1).astype(bf16)
-    early[...] = dot(coefficients[:half, :], query_t[...], 1, 1).astype(early.dtype)
-    late[...] = dot(coefficients[half:, :], query_t[...], 1, 1).astype(late.dtype)
+    return dot(coefficients[...], query_t[...], 1, 1)
+
+
+def own_kernel(group, info, table, query_t, out, coefficients):
+    half = coefficients.shape[0]
+    for h in range(out.shape[0] // half):
+        start = pl.multiple_of(group[0] * out.shape[0] + h * half, half)
+        rows = table[pl.ds(start, half), :]
+        out[h * half : (h + 1) * half, :] = rows_gradient(start, rows, info, query_t, coefficients)
+
+
+def rest_kernel(
+    group, infos, table, own, next_t, last_t, far_t, out, total, queries, coefficients, load_sems, own_sem, sems
+):
+    half = coefficients.shape[0]
+    groups = infos.shape[0]
+    loads = [
+        pltpu.make_async_copy(query_t, queries.at[i], load_sems.at[i])
+        for i, query_t in enumerate((next_t, last_t, far_t))
+    ]
+    for load in loads:
+        load.start()
+    own_load = pltpu.make_async_copy(own, total, own_sem)
+    own_load.start()
+    copies = []
+    for h in range(out.shape[0] // half):
+        start = pl.multiple_of(group[0] * out.shape[0] + h * half, half)
+        rows = table[pl.ds(start, half), :]
+        here = slice(h * half, (h + 1) * half)
+        gradient = jnp.zeros((half, out.shape[1]), f32)
+        for i, shift in enumerate((1, 3, 2)):
+            if h == 0:
+                loads[i].wait()
+            info = infos.at[(group[0] + shift) % groups]
+            gradient = gradient + rows_gradient(start, rows, info, queries.at[i], coefficients)
+        if h == 0:
+            own_load.wait()
+        total[here, :] = total[here, :] + gradient
+        copies.append(pltpu.make_async_copy(total.at[here, :], out.at[here, :], sems.at[h]))
+        copies[-1].start()
+    for copy in copies:
+        copy.wait()
 
 
 def per_device(
@@ -281,6 +320,8 @@
         compiler_params=params(8),
         name="plan",
     )(me, lists, list_lengths)
+
+    held, rounded = lax.optimization_barrier((held, table.astype(bf16)))
 
     def pack(*refs):
         pack_kernel(*refs, block_rows)
@@ -305,8 +346,11 @@
         tiled=True,
         axis_index_groups=planes,
     ).reshape(depth, CAP * count)
-
-    rounded = table.astype(bf16)
+    assert groups == 4
+    far_t, next_t, last_t = (
+        lax.ppermute(query_t, "dp", [(i, (i - shift) % groups) for i in range(groups)]) for shift in (2, 1, 3)
+    )
+
     local = pl.pallas_call(
         stats_kernel,
         out_shape=jax.ShapeDtypeStruct((32, count), f32),
@@ -329,54 +373,54 @@
         share.reshape(owners // 2, 16, count), "entity", 0, 0, tiled=True, axis_index_groups=cores
     )
 
-    norms, loss = pl.pallas_call(
+    info, loss = pl.pallas_call(
         merge_kernel,
-        out_shape=(jax.ShapeDtypeStruct((16, count), f32), jax.ShapeDtypeStruct((1, count), f32)),
+        out_shape=(jax.ShapeDtypeStruct((32, count), f32), jax.ShapeDtypeStruct((1, count), f32)),
         compiler_params=params(8),
         name="merge",
-    )(shared)
+    )(shared, targets)
 
     quarter = block_rows // groups
-
-    def grads(which, early, late, norms=norms):
-        return pl.pallas_call(
-            grads_kernel,
-            out_shape=(
-                jax.ShapeDtypeStruct((quarter // 2, depth), early),
-                jax.ShapeDtypeStruct((quarter // 2, depth), late),
-            ),
-            in_specs=[smem] + [vmem] * 4,
-            scratch_shapes=[pltpu.VMEM((quarter, CAP * count), bf16)],
-            compiler_params=params(16),
-            cost_estimate=pl.CostEstimate(
-                flops=4 * quarter * CAP * count * depth,
-                transcendentals=quarter * CAP * count,
-                bytes_accessed=4 * quarter * depth + 4 * CAP * count * depth,
-            ),
-            name="grads",
-        )((which % groups).reshape(1), norms, targets, rounded, query_t)
-
-    assert groups == 4
-
-    def up(value):
-        return lax.ppermute(value, "dp", [(i, (i + 1) % groups) for i in range(groups)])
-
-    def down(value):
-        return lax.ppermute(value, "dp", [(i, (i - 1) % groups) for i in range(groups)])
-
-    far_early, far_late = grads(group + 2, bf16, bf16)
-    relay_early, relay_late = up(far_early), down(far_late)
-    next_early, next_late = grads(group + 1, f32, bf16)
-    last_early, last_late = grads(group + 3, bf16, f32)
-    from_below_late, from_above_early = up(next_late), down(last_early)
-    next_early = (next_early + relay_early.astype(f32)).astype(bf16)
-    last_late = (last_late + relay_late.astype(f32)).astype(bf16)
-    from_below_early, from_above_late = up(next_early), down(last_late)
-    own_norms, next_early, last_late = lax.optimization_barrier((norms, next_early, last_late))
-    own_early, own_late = grads(group, f32, f32, own_norms)
-    early = own_early + from_above_early.astype(f32) + from_below_early.astype(f32)
-    late = own_late + from_below_late.astype(f32) + from_above_late.astype(f32)
-    gradient = jnp.concatenate([early, late], axis=0)
+    half = quarter // 2
+    mine_first = group.reshape(1)
+    infos = lax.all_to_all(
+        jnp.broadcast_to(info[None], (groups,) + info.shape), "dp", 0, 0, tiled=True
+    )
+
+    def cost(several):
+        return pl.CostEstimate(
+            flops=several * 4 * quarter * CAP * count * depth,
+            transcendentals=several * quarter * CAP * count,
+            bytes_accessed=8 * quarter * depth + several * 2 * CAP * count * depth,
+        )
+
+    own = pl.pallas_call(
+        own_kernel,
+        out_shape=jax.ShapeDtypeStruct((quarter, depth), f32),
+        in_specs=[smem] + [vmem] * 3,
+        scratch_shapes=[pltpu.VMEM((half, CAP * count), bf16)],
+        compiler_params=params(16),
+        cost_estimate=cost(1),
+        name="own",
+    )(mine_first, info, rounded, query_t)
+    gradient = pl.pallas_call(
+        rest_kernel,
+        out_shape=jax.ShapeDtypeStruct((quarter, depth), f32),
+        in_specs=[smem] + [vmem] * 2 + [pl.BlockSpec(memory_space=pltpu.HBM)] * 4,
+        out_specs=pl.BlockSpec(memory_space=pltpu.HBM),
+        scratch_shapes=[
+            pltpu.VMEM((quarter, depth), f32),
+            pltpu.VMEM((groups - 1, depth, CAP * count), bf16),
+            pltpu.VMEM((half, CAP * count), bf16),
+            pltpu.SemaphoreType.DMA((groups - 1,)),
+            pltpu.SemaphoreType.DMA,
+            pltpu.SemaphoreType.DMA((2,)),
+        ],
+        input_output_aliases={3: 0},
+        compiler_params=params(16),
+        cost_estimate=cost(groups - 1),
+        name="rest",
+    )(mine_first, infos, rounded, own, next_t, last_t, far_t)
     return (loss.reshape(count), gradient[None])
 
 

time: 105 us -> 103 us (0.981)
  blocking collectives: 0 us -> 17.9 us
  waiting for transfers between devices: 43.4 us -> 27.3 us
  starting transfers between devices: 32.1 us -> 26.5 us
  Pallas kernels: 24.4 us -> 27.3 us
  other arithmetic: 3.69 us -> 2.39 us
    all_to_all x0 -> x1, blocking collectives: none -> 17.9 us  [per_device(): lax.all_to_all(packed.reshape(PARTS, depth // PARTS, CAP * count), 'entit...]
    all_to_all x1, waiting for transfers between devices: 9.96 us -> 2.24 us  [per_device(): lax.all_to_all(jnp.broadcast_to(info[None], (groups,) + info.shape), 'dp'...]
    ppermute x6 -> x3, waiting for transfers between devices: 6.27 us -> 0.01 us  [per_device(): lax.ppermute(query_t, 'dp', [(i, (i - shift) % groups) for i in range(gro...]
    pallas_call x5 -> x3, Pallas kernels: 8.77 us -> 13 us  [the longest x1 9.22 us: per_device(): pl.pallas_call(rest_kernel, out_shape=jax.ShapeDtypeStruct((quarter, dept...]
    ppermute x6 -> x3, starting transfers between devices: 9.39 us -> 6.43 us  [per_device(): lax.ppermute(query_t, 'dp', [(i, (i - shift) % groups) for i in range(gro...]
    all_to_all x1, waiting for transfers between devices: 13.4 us -> 11.1 us  [per_device(): lax.all_to_all(spread.reshape(owners, stride, count), 'entity', 0, 0, til...]
    all_to_all x1, starting transfers between devices: 5.74 us -> 3.46 us  [per_device(): lax.all_to_all(jnp.broadcast_to(info[None], (groups,) + info.shape), 'dp'...]
    convert_element_type x3 -> x1, other arithmetic: 2.5 us -> 2.39 us  [per_device(): held, rounded = lax.optimization_barrier((held, table.astype(bf16)))]
  transfers between devices with their start and end apart: 10 -> 7, of which waited for: 5 -> 4; matrix products, arithmetic and copies ran while one was open for 2% -> 3% of each run, Pallas kernels for 6% -> 13%
where the time goes in v6:
time: 103 us
  Pallas kernels  27.3 us (27%)
  waiting for transfers between devices  27.3 us (27%)
  starting transfers between devices  26.5 us (26%)
  blocking collectives  17.9 us (17%)
  other arithmetic  2.39 us (2%)
    all_to_all x1, blocking collectives, per_device(): lax.all_to_all(packed.reshape(PARTS, depth // PARTS, CAP * count), 'entit...  17.9 us
    all_to_all x1, waiting for transfers between devices, per_device(): lax.all_to_all(share.reshape(owners // 2, 16, count), 'entity', 0, 0, til...  12.9 us
    all_to_all x1, starting transfers between devices, per_device(): lax.all_to_all(spread.reshape(owners, stride, count), 'entity', 0, 0, til...  11.6 us
    all_to_all x1, waiting for transfers between devices, per_device(): lax.all_to_all(spread.reshape(owners, stride, count), 'entity', 0, 0, til...  11.1 us
    pallas_call x1, Pallas kernels, per_device(): pl.pallas_call(rest_kernel, out_shape=jax.ShapeDtypeStruct((quarter, dept...  9.22 us
    pallas_call x1, Pallas kernels, per_device(): pl.pallas_call(stats_kernel, out_shape=jax.ShapeDtypeStruct((32, count),...  7.36 us
    ppermute x3, starting transfers between devices, per_device(): lax.ppermute(query_t, 'dp', [(i, (i - shift) % groups) for i in range(gro...  6.43 us
    all_to_all x1, starting transfers between devices, per_device(): lax.all_to_all(share.reshape(owners // 2, 16, count), 'entity', 0, 0, til...  4.95 us
  transfers between devices with their start and end apart: 7, of which 4 were waited for; matrix products, arithmetic and copies ran while one was open for 3% of the time, Pallas kernels for 13%

profile of v6, /device:TPU:32, one launch (start us, length us, event | category | flops | bytes accessed | tf_op | source)
XLA Modules:
  0.0 103.0 jit_solution(16945101092152889637)
XLA Ops:
  0.6 0.0 copy-start.1
  0.6 0.0 copy-start
  0.7 4.1 %query.1 = bf16[1536,128]{1,0:T(8,128)(2,1)} custom-call(s32[128]{0:T(128)} %heads.1, f32[4096,256]{1,0:T(8,128)} %bitcast.22, f32[4,256,256]{2,1,0:T(8,128)} %operators.1, s32[1,128]{1,0:T(1,128)} %bitcast.24, s32[1,128]{1,0:T(1,128)} %bitcast.25), custom_call_target="tpu_custom_call" | custom-call | tf_op jit(solution)/shard_map/query/pallas_call | solution.py:295
  4.7 11.6 %all-to-all-start = ((bf16[64,24,128]{2,1,0:T(8,128)(2,1)}), bf16[64,24,128]{2,1,0:T(8,128)(2,1)S(1)}, u32[]{:S(2)}, u32[]{:S(2)}) async-start(bf16[64,24,128]{2,1,0:T(8,128)(2,1)} %bitcast.23), calls=%async_computation | async-start | bytes 786432 | tf_op jit(solution)/shard_map/all_to_all | solution.py:308
  16.3 0.0 copy-done.1
  16.3 0.0 copy-done
  16.3 0.6 plan.1
  17.0 2.4 %bitcast_convert_fusion.table = bf16[4096,256]{1,0:T(8,128)(2,1)S(1)} fusion(f32[1,4096,256]{2,1,0:T(8,128)} %param.7), kind=kLoop, calls=%fused_computation | loop fusion | flops 1048576 | bytes 6291456 | tf_op jit(solution)/shard_map/convert_element_type | solution.py:324
  19.4 11.1 %all-to-all-done = bf16[64,24,128]{2,1,0:T(8,128)(2,1)S(1)} async-done(((bf16[64,24,128]{2,1,0:T(8,128)(2,1)}), bf16[64,24,128]{2,1,0:T(8,128)(2,1)S(1)}, u32[]{:S(2)}, u32[]{:S(2)}) %all-to-all-start) | async-done | bytes 393248 | tf_op jit(solution)/shard_map/all_to_all | solution.py:308
  30.4 1.0 pack.1
  31.4 17.9 %all_to_all.20 = bf16[16,16,1536]{2,1,0:T(8,128)(2,1)S(1)} all-to-all(bf16[16,16,1536]{2,1,0:T(8,128)(2,1)S(1)} %bitcast.20), channel_id=1, replica_groups={{0,1,2,3,4,5,6,7,8,9,10,11,12,13,14,15},{16,17,18,19,20,21,22,23,24,25,..., dimensions={0} | all-to-all | bytes 1572864 | tf_op jit(solution)/shard_map/all_to_all | solution.py:341
  49.3 3.2 %collective-permute-start.3 = (bf16[256,1536]{1,0:T(8,128)(2,1)S(1)}, bf16[256,1536]{1,0:T(8,128)(2,1)}, u32[]{:S(2)}, u32[]{:S(2)}) collective-permute-start(bf16[256,1536]{1,0:T(8,128)(2,1)S(1)} %bitcast.14), channel_id=1, source_target_pairs={{0,128},{64,192},{128,0},{192,64},{1,129},{65,193},{129,1},{193,65... | collective-permute-start | bytes 2359304 | tf_op jit(solution)/shard_map/ppermute | solution.py:351
  52.5 0.7 collective-permute-start.2
  53.2 2.6 %collective-permute-start.1 = (bf16[256,1536]{1,0:T(8,128)(2,1)S(1)}, bf16[256,1536]{1,0:T(8,128)(2,1)}, u32[]{:S(2)}, u32[]{:S(2)}) collective-permute-start(bf16[256,1536]{1,0:T(8,128)(2,1)S(1)} %bitcast.16), channel_id=1, source_target_pairs={{0,192},{64,0},{128,64},{192,128},{1,193},{65,1},{129,65},{193,129... | collective-permute-start | bytes 2359304 | tf_op jit(solution)/shard_map/ppermute | solution.py:351
  55.8 7.4 %stats.1.mine = f32[32,128]{1,0:T(8,128)S(1)} custom-call(bf16[256,1536]{1,0:T(8,128)(2,1)S(1)} %bitcast.17, bf16[4096,256]{1,0:T(8,128)(2,1)S(1)} %bitcast_convert_fusion.table, s32[16,128]{1,0:T(8,128)S(1)} %get-tuple-element.17.targets), custom_call_target="tpu_custom_call" | custom-call | tf_op jit(solution)/shard_map/stats/pallas_call | solution.py:354
  63.1 0.1 collective-permute-start
  63.2 1.2 %collective-permute-done.other = f32[32,128]{1,0:T(8,128)S(1)} collective-permute-done((f32[32,128]{1,0:T(8,128)S(1)}, f32[32,128]{1,0:T(8,128)S(1)}, u32[]{:S(2)}, u32[]{:S(2)}) %collective-permute-start) | collective-permute-done | bytes 16416 | tf_op jit(solution)/shard_map/ppermute | solution.py:363
  64.4 1.3 %share.1 = f32[512,128]{1,0:T(8,128)} custom-call(f32[2,512,32]{2,1,0:T(8,128)S(1)} %get-tuple-element.11.matches, f32[32,128]{1,0:T(8,128)S(1)} %stats.1.mine, f32[32,128]{1,0:T(8,128)S(1)} %collective-permute-done.other), custom_call_target="tpu_custom_call" | custom-call | tf_op jit(solution)/shard_map/share/pallas_call | solution.py:364
  65.7 5.0 %all-to-all-start.2 = ((f32[32,16,128]{2,1,0:T(8,128)}), f32[32,16,128]{2,1,0:T(8,128)S(1)}, u32[]{:S(2)}, u32[]{:S(2)}) async-start(f32[32,16,128]{2,1,0:T(8,128)} %bitcast.9), calls=%async_computation.2 | async-start | bytes 524288 | tf_op jit(solution)/shard_map/all_to_all | solution.py:372
  70.7 12.9 %all-to-all-done.2.received = f32[32,16,128]{2,1,0:T(8,128)S(1)} async-done(((f32[32,16,128]{2,1,0:T(8,128)}), f32[32,16,128]{2,1,0:T(8,128)S(1)}, u32[]{:S(2)}, u32[]{:S(2)}) %all-to-all-start.2) | async-done | bytes 262176 | tf_op jit(solution)/shard_map/all_to_all | solution.py:372
  83.6 0.6 merge.1
  84.1 0.6 broadcast_in_dim.4
  84.8 3.5 %all-to-all-start.3 = ((f32[4,32,128]{2,1,0:T(8,128)}), f32[4,32,128]{2,1,0:T(8,128)S(1)}, u32[]{:S(2)}, u32[]{:S(2)}) async-start(f32[4,32,128]{2,1,0:T(8,128)} %broadcast_in_dim.4), calls=%async_computation.3 | async-start | bytes 131072 | tf_op jit(solution)/shard_map/all_to_all | solution.py:386
  88.2 3.2 %own.1 = f32[1024,256]{1,0:T(8,128)} custom-call(s32[1]{0:T(128)} %bitcast.11.group, f32[32,128]{1,0:T(8,128)S(1)} %get-tuple-element.19.info, bf16[4096,256]{1,0:T(8,128)(2,1)S(1)} %bitcast_convert_fusion.table, bf16[256,1536]{1,0:T(8,128)(2,1)S(1)} %bitcast.18), custom_call_target="tpu_custom_call" | custom-call | flops 1610612736 | bytes 2883584 | tf_op jit(solution)/shard_map/own/pallas_call | solution.py:397
  91.4 2.2 %all-to-all-done.3.infos = f32[4,32,128]{2,1,0:T(8,128)S(1)} async-done(((f32[4,32,128]{2,1,0:T(8,128)}), f32[4,32,128]{2,1,0:T(8,128)S(1)}, u32[]{:S(2)}, u32[]{:S(2)}) %all-to-all-start.3) | async-done | bytes 65568 | tf_op jit(solution)/shard_map/all_to_all | solution.py:386
  93.6 0.0 collective-permute-done.3.far_t
  93.6 0.0 collective-permute-done.2.last_t
  93.6 0.0 collective-permute-done.1.next_t
  93.6 9.2 %rest.1 = f32[1024,256]{1,0:T(8,128)} custom-call(s32[1]{0:T(128)} %bitcast.11.group, f32[4,32,128]{2,1,0:T(8,128)S(1)} %all-to-all-done.3.infos, bf16[4096,256]{1,0:T(8,128)(2,1)S(1)} %bitcast_convert_fusion.table, f32[1024,256]{1,0:T(8,128)} %own.1, bf16[256,1536]{1,0:T(8,128)(2,1)} %collective-permute-done.1.next_t, ...), custom_call_target="tpu_custom_call", output_to_operand_aliasing={{}: (3, {})} | custom-call | flops 4831838208 | bytes 4456448 | tf_op jit(solution)/shard_map/rest/pallas_call | solution.py:406
Async XLA Ops:
  0.6 15.7 %copy-start.1 = (s32[1,64]{1,0:T(1,128)S(1)}, s32[1,64]{1,0:T(1,128)}, u32[]{:S(2)}) copy-start(s32[1,64]{1,0:T(1,128)} %lengths.1) | copy-start | bytes 772
  0.6 15.7 %copy-start = (s32[64,8]{0,1:T(8,128)S(1)}, s32[64,8]{0,1:T(8,128)}, u32[]{:S(2)}) copy-start(s32[64,8]{0,1:T(8,128)} %param.9) | copy-start | bytes 6148
  4.7 25.7 %all-to-all-start = ((bf16[64,24,128]{2,1,0:T(8,128)(2,1)}), bf16[64,24,128]{2,1,0:T(8,128)(2,1)S(1)}, u32[]{:S(2)}, u32[]{:S(2)}) async-start(bf16[64,24,128]{2,1,0:T(8,128)(2,1)} %bitcast.23), calls=%async_computation | async-start | bytes 786432 | tf_op jit(solution)/shard_map/all_to_all | solution.py:308
  49.3 44.3 %collective-permute-start.3 = (bf16[256,1536]{1,0:T(8,128)(2,1)S(1)}, bf16[256,1536]{1,0:T(8,128)(2,1)}, u32[]{:S(2)}, u32[]{:S(2)}) collective-permute-start(bf16[256,1536]{1,0:T(8,128)(2,1)S(1)} %bitcast.14), channel_id=1, source_target_pairs={{0,128},{64,192},{128,0},{192,64},{1,129},{65,193},{129,1},{193,65... | collective-permute-start | bytes 2359304 | tf_op jit(solution)/shard_map/ppermute | solution.py:351
  52.5 41.1 %collective-permute-start.2 = (bf16[256,1536]{1,0:T(8,128)(2,1)S(1)}, bf16[256,1536]{1,0:T(8,128)(2,1)}, u32[]{:S(2)}, u32[]{:S(2)}) collective-permute-start(bf16[256,1536]{1,0:T(8,128)(2,1)S(1)} %bitcast.15), channel_id=1, source_target_pairs={{0,64},{64,128},{128,192},{192,0},{1,65},{65,129},{129,193},{193,1... | collective-permute-start | bytes 2359304 | tf_op jit(solution)/shard_map/ppermute | solution.py:351
  53.2 40.4 %collective-permute-start.1 = (bf16[256,1536]{1,0:T(8,128)(2,1)S(1)}, bf16[256,1536]{1,0:T(8,128)(2,1)}, u32[]{:S(2)}, u32[]{:S(2)}) collective-permute-start(bf16[256,1536]{1,0:T(8,128)(2,1)S(1)} %bitcast.16), channel_id=1, source_target_pairs={{0,192},{64,0},{128,64},{192,128},{1,193},{65,1},{129,65},{193,129... | collective-permute-start | bytes 2359304 | tf_op jit(solution)/shard_map/ppermute | solution.py:351
  63.1 1.3 %collective-permute-start = (f32[32,128]{1,0:T(8,128)S(1)}, f32[32,128]{1,0:T(8,128)S(1)}, u32[]{:S(2)}, u32[]{:S(2)}) collective-permute-start(f32[32,128]{1,0:T(8,128)S(1)} %stats.1.mine), channel_id=1, source_target_pairs={{0,1},{1,0},{2,3},{3,2},{4,5},{5,4},{6,7},{7,6},{8,9},{9,8},{10,11... | collective-permute-start | bytes 49160 | tf_op jit(solution)/shard_map/ppermute | solution.py:363
  65.7 17.8 %all-to-all-start.2 = ((f32[32,16,128]{2,1,0:T(8,128)}), f32[32,16,128]{2,1,0:T(8,128)S(1)}, u32[]{:S(2)}, u32[]{:S(2)}) async-start(f32[32,16,128]{2,1,0:T(8,128)} %bitcast.9), calls=%async_computation.2 | async-start | bytes 524288 | tf_op jit(solution)/shard_map/all_to_all | solution.py:372
  84.8 8.9 %all-to-all-start.3 = ((f32[4,32,128]{2,1,0:T(8,128)}), f32[4,32,128]{2,1,0:T(8,128)S(1)}, u32[]{:S(2)}, u32[]{:S(2)}) async-start(f32[4,32,128]{2,1,0:T(8,128)} %broadcast_in_dim.4), calls=%async_computation.3 | async-start | bytes 131072 | tf_op jit(solution)/shard_map/all_to_all | solution.py:386

commit v7 on v6

--- a/solution.py
+++ b/solution.py
@@ -8,6 +8,7 @@
 f32, bf16, i32 = jnp.float32, jnp.bfloat16, jnp.int32
 CAP = 12
 PARTS = 16
+OWN_FACTOR = 6
 WIDE = 4
 TILE = 1024
 CHUNK = 128
@@ -200,15 +201,18 @@
     best = jnp.max(values, axis=0)
     mass = jnp.sum(jnp.exp(values - best[None]), axis=0)
     norm = best + jnp.log(mass)
-    info[0:16, :] = jnp.where(best <= 0.5 * NEG, -NEG, norm)
-    info[16:32, :] = targets[...].astype(f32)
+    for group in range(info.shape[0]):
+        info[group, 0:16, :] = jnp.where(best <= 0.5 * NEG, -NEG, norm)
+        info[group, 16:32, :] = targets[...].astype(f32)
     target = jnp.sum(values[:, CAP + 1, :], axis=0, keepdims=True)
     loss[...] = norm[CAP : CAP + 1, :] - target
 
 
-def rows_gradient(start, rows, info, query_t, coefficients):
+def rows_gradient(start, rows, info, query_t, coefficients, arrived=None):
     count = rows.shape[0]
     for p in range(CAP // WIDE):
+        if arrived is not None:
+            arrived(p)
         columns = slice(p * WIDE * 128, (p + 1) * WIDE * 128)
         weights = query_t[:, columns]
         norm = slot_lanes(info, p)
@@ -229,7 +233,7 @@
     for h in range(out.shape[0] // half):
         start = pl.multiple_of(group[0] * out.shape[0] + h * half, half)
         rows = table[pl.ds(start, half), :]
-        out[h * half : (h + 1) * half, :] = rows_gradient(start, rows, info, query_t, coefficients)
+        out[h * half : (h + 1) * half, :] = rows_gradient(start, rows, info.at[0], query_t, coefficients)
 
 
 def rest_kernel(
@@ -237,14 +241,19 @@
 ):
     half = coefficients.shape[0]
     groups = infos.shape[0]
+    third = queries.shape[2] // 3
     loads = [
-        pltpu.make_async_copy(query_t, queries.at[i], load_sems.at[i])
+        [
+            pltpu.make_async_copy(
+                query_t.at[:, pl.ds(k * third, third)], queries.at[i, :, pl.ds(k * third, third)], load_sems.at[i, k]
+            )
+            for k in range(3)
+        ]
         for i, query_t in enumerate((next_t, last_t, far_t))
     ]
-    for load in loads:
+    own_load = pltpu.make_async_copy(own, total, own_sem)
+    for load in loads[0]:
         load.start()
-    own_load = pltpu.make_async_copy(own, total, own_sem)
-    own_load.start()
     copies = []
     for h in range(out.shape[0] // half):
         start = pl.multiple_of(group[0] * out.shape[0] + h * half, half)
@@ -252,10 +261,17 @@
         here = slice(h * half, (h + 1) * half)
         gradient = jnp.zeros((half, out.shape[1]), f32)
         for i, shift in enumerate((1, 3, 2)):
-            if h == 0:
-                loads[i].wait()
+
+            def arrived(p, h=h, i=i):
+                if h == 0:
+                    loads[i][p].wait()
+                    if i < 2:
+                        loads[i + 1][p].start()
+                    elif p == 0:
+                        own_load.start()
+
             info = infos.at[(group[0] + shift) % groups]
-            gradient = gradient + rows_gradient(start, rows, info, queries.at[i], coefficients)
+            gradient = gradient + rows_gradient(start, rows, info, queries.at[i], coefficients, arrived)
         if h == 0:
             own_load.wait()
         total[here, :] = total[here, :] + gradient
@@ -346,10 +362,6 @@
         tiled=True,
         axis_index_groups=planes,
     ).reshape(depth, CAP * count)
-    assert groups == 4
-    far_t, next_t, last_t = (
-        lax.ppermute(query_t, "dp", [(i, (i - shift) % groups) for i in range(groups)]) for shift in (2, 1, 3)
-    )
 
     local = pl.pallas_call(
         stats_kernel,
@@ -368,6 +380,11 @@
         compiler_params=params(8),
         name="share",
     )(matches, local, other)
+    assert groups == 4
+    share, sent_t = lax.optimization_barrier((share, query_t))
+    far_t, next_t, last_t = (
+        lax.ppermute(sent_t, "dp", [(i, (i - shift) % groups) for i in range(groups)]) for shift in (2, 1, 3)
+    )
     cores = [[i for i in range(owners) if i % 2 == core] for core in range(2)]
     shared = lax.all_to_all(
         share.reshape(owners // 2, 16, count), "entity", 0, 0, tiled=True, axis_index_groups=cores
@@ -375,7 +392,7 @@
 
     info, loss = pl.pallas_call(
         merge_kernel,
-        out_shape=(jax.ShapeDtypeStruct((32, count), f32), jax.ShapeDtypeStruct((1, count), f32)),
+        out_shape=(jax.ShapeDtypeStruct((groups, 32, count), f32), jax.ShapeDtypeStruct((1, count), f32)),
         compiler_params=params(8),
         name="merge",
     )(shared, targets)
@@ -383,11 +400,10 @@
     quarter = block_rows // groups
     half = quarter // 2
     mine_first = group.reshape(1)
-    infos = lax.all_to_all(
-        jnp.broadcast_to(info[None], (groups,) + info.shape), "dp", 0, 0, tiled=True
-    )
-
-    def cost(several):
+    infos = lax.all_to_all(info, "dp", 0, 0, tiled=True)
+
+    def cost(several, factor=1):
+        several = several * factor
         return pl.CostEstimate(
             flops=several * 4 * quarter * CAP * count * depth,
             transcendentals=several * quarter * CAP * count,
@@ -400,7 +416,7 @@
         in_specs=[smem] + [vmem] * 3,
         scratch_shapes=[pltpu.VMEM((half, CAP * count), bf16)],
         compiler_params=params(16),
-        cost_estimate=cost(1),
+        cost_estimate=cost(1, OWN_FACTOR),
         name="own",
     )(mine_first, info, rounded, query_t)
     gradient = pl.pallas_call(
@@ -412,7 +428,7 @@
             pltpu.VMEM((quarter, depth), f32),
             pltpu.VMEM((groups - 1, depth, CAP * count), bf16),
             pltpu.VMEM((half, CAP * count), bf16),
-            pltpu.SemaphoreType.DMA((groups - 1,)),
+            pltpu.SemaphoreType.DMA((groups - 1, 3)),
             pltpu.SemaphoreType.DMA,
             pltpu.SemaphoreType.DMA((2,)),
         ],

time: 103 us -> 115 us (1.12); the launches traced: 103 us -> 114 us
  waiting for transfers between devices: 27.3 us -> 35.1 us
  Pallas kernels: 27.3 us -> 29.6 us
  starting transfers between devices: 26.5 us -> 27.7 us
    all_to_all x1, waiting for transfers between devices: 2.24 us -> 16.6 us  [per_device(): infos = lax.all_to_all(info, 'dp', 0, 0, tiled=True)]
    all_to_all x1, waiting for transfers between devices: 12.9 us -> 6.34 us  [per_device(): lax.all_to_all(share.reshape(owners // 2, 16, count), 'entity', 0, 0, til...]
    pallas_call x1, Pallas kernels: 9.22 us -> 10.5 us  [per_device(): pl.pallas_call(rest_kernel, out_shape=jax.ShapeDtypeStruct((quarter, dept...]
  transfers between devices with their start and end apart: 7 -> 7, of which waited for: 4 -> 4; matrix products, arithmetic and copies ran while one was open for 3% -> 2% of each run, Pallas kernels for 13% -> 5%
where the time goes in v7:
time: 115 us; the launch traced here: 114 us
  waiting for transfers between devices  35.1 us (31%)
  Pallas kernels  29.6 us (26%)
  starting transfers between devices  27.7 us (24%)
  blocking collectives  17.9 us (16%)
  other arithmetic  2.39 us (2%)
    all_to_all x1, blocking collectives, per_device(): lax.all_to_all(packed.reshape(PARTS, depth // PARTS, CAP * count), 'entit...  17.9 us
    all_to_all x1, waiting for transfers between devices, per_device(): infos = lax.all_to_all(info, 'dp', 0, 0, tiled=True)  16.6 us
    all_to_all x1, starting transfers between devices, per_device(): lax.all_to_all(spread.reshape(owners, stride, count), 'entity', 0, 0, til...  11.6 us
    all_to_all x1, waiting for transfers between devices, per_device(): lax.all_to_all(spread.reshape(owners, stride, count), 'entity', 0, 0, til...  11.1 us
    pallas_call x1, Pallas kernels, per_device(): pl.pallas_call(rest_kernel, out_shape=jax.ShapeDtypeStruct((quarter, dept...  10.5 us
    pallas_call x1, Pallas kernels, per_device(): pl.pallas_call(stats_kernel, out_shape=jax.ShapeDtypeStruct((32, count),...  7.34 us
    ppermute x3, starting transfers between devices, per_device(): lax.ppermute(sent_t, 'dp', [(i, (i - shift) % groups) for i in range(grou...  6.51 us
    all_to_all x1, waiting for transfers between devices, per_device(): lax.all_to_all(share.reshape(owners // 2, 16, count), 'entity', 0, 0, til...  6.34 us
  transfers between devices with their start and end apart: 7, of which 4 were waited for; matrix products, arithmetic and copies ran while one was open for 2% of the time, Pallas kernels for 5%

profile of v7, /device:TPU:32, one launch (start us, length us, event | category | flops | bytes accessed | tf_op | source)
XLA Modules:
  0.0 113.6 jit_solution(16717607417812508809)
XLA Ops:
  0.6 0.0 copy-start.1
  0.6 0.0 copy-start
  0.7 4.1 %query.1 = bf16[1536,128]{1,0:T(8,128)(2,1)} custom-call(s32[128]{0:T(128)} %heads.1, f32[4096,256]{1,0:T(8,128)} %bitcast.22, f32[4,256,256]{2,1,0:T(8,128)} %operators.1, s32[1,128]{1,0:T(1,128)} %bitcast.24, s32[1,128]{1,0:T(1,128)} %bitcast.25), custom_call_target="tpu_custom_call" | custom-call | tf_op jit(solution)/shard_map/query/pallas_call | solution.py:311
  4.7 11.6 %all-to-all-start = ((bf16[64,24,128]{2,1,0:T(8,128)(2,1)}), bf16[64,24,128]{2,1,0:T(8,128)(2,1)S(1)}, u32[]{:S(2)}, u32[]{:S(2)}) async-start(bf16[64,24,128]{2,1,0:T(8,128)(2,1)} %bitcast.23), calls=%async_computation | async-start | bytes 786432 | tf_op jit(solution)/shard_map/all_to_all | solution.py:324
  16.3 0.0 copy-done.1
  16.3 0.0 copy-done
  16.3 0.6 plan.1
  17.0 2.4 %bitcast_convert_fusion.table = bf16[4096,256]{1,0:T(8,128)(2,1)S(1)} fusion(f32[1,4096,256]{2,1,0:T(8,128)} %param.7), kind=kLoop, calls=%fused_computation | loop fusion | flops 1048576 | bytes 6291456 | tf_op jit(solution)/shard_map/convert_element_type | solution.py:340
  19.4 11.1 %all-to-all-done = bf16[64,24,128]{2,1,0:T(8,128)(2,1)S(1)} async-done(((bf16[64,24,128]{2,1,0:T(8,128)(2,1)}), bf16[64,24,128]{2,1,0:T(8,128)(2,1)S(1)}, u32[]{:S(2)}, u32[]{:S(2)}) %all-to-all-start) | async-done | bytes 393248 | tf_op jit(solution)/shard_map/all_to_all | solution.py:324
  30.4 1.0 pack.1
  31.4 17.9 %all_to_all.20 = bf16[16,16,1536]{2,1,0:T(8,128)(2,1)S(1)} all-to-all(bf16[16,16,1536]{2,1,0:T(8,128)(2,1)S(1)} %bitcast.20), channel_id=1, replica_groups={{0,1,2,3,4,5,6,7,8,9,10,11,12,13,14,15},{16,17,18,19,20,21,22,23,24,25,..., dimensions={0} | all-to-all | bytes 1572864 | tf_op jit(solution)/shard_map/all_to_all | solution.py:357
  49.3 7.3 %stats.1.mine = f32[32,128]{1,0:T(8,128)S(1)} custom-call(bf16[256,1536]{1,0:T(8,128)(2,1)S(1)} %bitcast.14, bf16[4096,256]{1,0:T(8,128)(2,1)S(1)} %bitcast_convert_fusion.table, s32[16,128]{1,0:T(8,128)S(1)} %get-tuple-element.19.targets), custom_call_target="tpu_custom_call" | custom-call | tf_op jit(solution)/shard_map/stats/pallas_call | solution.py:366
  56.7 0.2 collective-permute-start
  56.8 1.1 collective-permute-done.other
  58.0 1.3 %share.1 = f32[512,128]{1,0:T(8,128)} custom-call(f32[2,512,32]{2,1,0:T(8,128)S(1)} %get-tuple-element.13.matches, f32[32,128]{1,0:T(8,128)S(1)} %stats.1.mine, f32[32,128]{1,0:T(8,128)S(1)} %collective-permute-done.other), custom_call_target="tpu_custom_call" | custom-call | tf_op jit(solution)/shard_map/share/pallas_call | solution.py:376
  59.3 5.0 %all-to-all-start.2 = ((f32[32,16,128]{2,1,0:T(8,128)}), f32[32,16,128]{2,1,0:T(8,128)S(1)}, u32[]{:S(2)}, u32[]{:S(2)}) async-start(f32[32,16,128]{2,1,0:T(8,128)} %bitcast.9), calls=%async_computation.2 | async-start | bytes 524288 | tf_op jit(solution)/shard_map/all_to_all | solution.py:389
  64.3 3.3 %collective-permute-start.3 = (bf16[256,1536]{1,0:T(8,128)(2,1)S(1)}, bf16[256,1536]{1,0:T(8,128)(2,1)}, u32[]{:S(2)}, u32[]{:S(2)}) collective-permute-start(bf16[256,1536]{1,0:T(8,128)(2,1)S(1)} %bitcast.15), channel_id=1, source_target_pairs={{0,128},{64,192},{128,0},{192,64},{1,129},{65,193},{129,1},{193,65... | collective-permute-start | bytes 2359304 | tf_op jit(solution)/shard_map/ppermute | solution.py:386
  67.5 0.7 collective-permute-start.2
  68.2 2.6 %collective-permute-start.1 = (bf16[256,1536]{1,0:T(8,128)(2,1)S(1)}, bf16[256,1536]{1,0:T(8,128)(2,1)}, u32[]{:S(2)}, u32[]{:S(2)}) collective-permute-start(bf16[256,1536]{1,0:T(8,128)(2,1)S(1)} %bitcast.17), channel_id=1, source_target_pairs={{0,192},{64,0},{128,64},{192,128},{1,193},{65,1},{129,65},{193,129... | collective-permute-start | bytes 2359304 | tf_op jit(solution)/shard_map/ppermute | solution.py:386
  70.8 6.3 %all-to-all-done.2.received = f32[32,16,128]{2,1,0:T(8,128)S(1)} async-done(((f32[32,16,128]{2,1,0:T(8,128)}), f32[32,16,128]{2,1,0:T(8,128)S(1)}, u32[]{:S(2)}, u32[]{:S(2)}) %all-to-all-start.2) | async-done | bytes 262176 | tf_op jit(solution)/shard_map/all_to_all | solution.py:389
  77.1 0.7 merge.1
  77.8 4.5 %all-to-all-start.3 = ((f32[4,32,128]{2,1,0:T(8,128)}), f32[4,32,128]{2,1,0:T(8,128)S(1)}, u32[]{:S(2)}, u32[]{:S(2)}) async-start(f32[4,32,128]{2,1,0:T(8,128)} %get-tuple-element.22.info), calls=%async_computation.3 | async-start | bytes 131072 | tf_op jit(solution)/shard_map/all_to_all | solution.py:403
  82.3 4.0 %own.1 = f32[1024,256]{1,0:T(8,128)} custom-call(s32[1]{0:T(128)} %bitcast.11.group, f32[4,32,128]{2,1,0:T(8,128)} %get-tuple-element.22.info, bf16[4096,256]{1,0:T(8,128)(2,1)S(1)} %bitcast_convert_fusion.table, bf16[256,1536]{1,0:T(8,128)(2,1)S(1)} %bitcast.18), custom_call_target="tpu_custom_call" | custom-call | flops 9663676416 | bytes 6815744 | tf_op jit(solution)/shard_map/own/pallas_call | solution.py:413
  86.3 16.6 %all-to-all-done.3.infos = f32[4,32,128]{2,1,0:T(8,128)S(1)} async-done(((f32[4,32,128]{2,1,0:T(8,128)}), f32[4,32,128]{2,1,0:T(8,128)S(1)}, u32[]{:S(2)}, u32[]{:S(2)}) %all-to-all-start.3) | async-done | bytes 65568 | tf_op jit(solution)/shard_map/all_to_all | solution.py:403
  103.0 0.0 collective-permute-done.3.far_t
  103.0 0.0 collective-permute-done.2.last_t
  103.0 0.0 collective-permute-done.1.next_t
  103.0 10.5 %rest.1 = f32[1024,256]{1,0:T(8,128)} custom-call(s32[1]{0:T(128)} %bitcast.11.group, f32[4,32,128]{2,1,0:T(8,128)S(1)} %all-to-all-done.3.infos, bf16[4096,256]{1,0:T(8,128)(2,1)S(1)} %bitcast_convert_fusion.table, f32[1024,256]{1,0:T(8,128)} %own.1, bf16[256,1536]{1,0:T(8,128)(2,1)} %collective-permute-done.1.next_t, ...), custom_call_target="tpu_custom_call", output_to_operand_aliasing={{}: (3, {})} | custom-call | flops 4831838208 | bytes 4456448 | tf_op jit(solution)/shard_map/rest/pallas_call | solution.py:422
Async XLA Ops:
  0.6 15.7 %copy-start.1 = (s32[1,64]{1,0:T(1,128)S(1)}, s32[1,64]{1,0:T(1,128)}, u32[]{:S(2)}) copy-start(s32[1,64]{1,0:T(1,128)} %lengths.1) | copy-start | bytes 772
  0.6 15.7 %copy-start = (s32[64,8]{0,1:T(8,128)S(1)}, s32[64,8]{0,1:T(8,128)}, u32[]{:S(2)}) copy-start(s32[64,8]{0,1:T(8,128)} %param.9) | copy-start | bytes 6148
  4.7 25.7 %all-to-all-start = ((bf16[64,24,128]{2,1,0:T(8,128)(2,1)}), bf16[64,24,128]{2,1,0:T(8,128)(2,1)S(1)}, u32[]{:S(2)}, u32[]{:S(2)}) async-start(bf16[64,24,128]{2,1,0:T(8,128)(2,1)} %bitcast.23), calls=%async_computation | async-start | bytes 786432 | tf_op jit(solution)/shard_map/all_to_all | solution.py:324
  56.7 1.3 %collective-permute-start = (f32[32,128]{1,0:T(8,128)S(1)}, f32[32,128]{1,0:T(8,128)S(1)}, u32[]{:S(2)}, u32[]{:S(2)}) collective-permute-start(f32[32,128]{1,0:T(8,128)S(1)} %stats.1.mine), channel_id=1, source_target_pairs={{0,1},{1,0},{2,3},{3,2},{4,5},{5,4},{6,7},{7,6},{8,9},{9,8},{10,11... | collective-permute-start | bytes 49160 | tf_op jit(solution)/shard_map/ppermute | solution.py:375
  59.3 17.9 %all-to-all-start.2 = ((f32[32,16,128]{2,1,0:T(8,128)}), f32[32,16,128]{2,1,0:T(8,128)S(1)}, u32[]{:S(2)}, u32[]{:S(2)}) async-start(f32[32,16,128]{2,1,0:T(8,128)} %bitcast.9), calls=%async_computation.2 | async-start | bytes 524288 | tf_op jit(solution)/shard_map/all_to_all | solution.py:389
  64.3 38.7 %collective-permute-start.3 = (bf16[256,1536]{1,0:T(8,128)(2,1)S(1)}, bf16[256,1536]{1,0:T(8,128)(2,1)}, u32[]{:S(2)}, u32[]{:S(2)}) collective-permute-start(bf16[256,1536]{1,0:T(8,128)(2,1)S(1)} %bitcast.15), channel_id=1, source_target_pairs={{0,128},{64,192},{128,0},{192,64},{1,129},{65,193},{129,1},{193,65... | collective-permute-start | bytes 2359304 | tf_op jit(solution)/shard_map/ppermute | solution.py:386
  67.5 35.4 %collective-permute-start.2 = (bf16[256,1536]{1,0:T(8,128)(2,1)S(1)}, bf16[256,1536]{1,0:T(8,128)(2,1)}, u32[]{:S(2)}, u32[]{:S(2)}) collective-permute-start(bf16[256,1536]{1,0:T(8,128)(2,1)S(1)} %bitcast.16), channel_id=1, source_target_pairs={{0,64},{64,128},{128,192},{192,0},{1,65},{65,129},{129,193},{193,1... | collective-permute-start | bytes 2359304 | tf_op jit(solution)/shard_map/ppermute | solution.py:386
  68.2 34.7 %collective-permute-start.1 = (bf16[256,1536]{1,0:T(8,128)(2,1)S(1)}, bf16[256,1536]{1,0:T(8,128)(2,1)}, u32[]{:S(2)}, u32[]{:S(2)}) collective-permute-start(bf16[256,1536]{1,0:T(8,128)(2,1)S(1)} %bitcast.17), channel_id=1, source_target_pairs={{0,192},{64,0},{128,64},{192,128},{1,193},{65,1},{129,65},{193,129... | collective-permute-start | bytes 2359304 | tf_op jit(solution)/shard_map/ppermute | solution.py:386
  77.8 25.1 %all-to-all-start.3 = ((f32[4,32,128]{2,1,0:T(8,128)}), f32[4,32,128]{2,1,0:T(8,128)S(1)}, u32[]{:S(2)}, u32[]{:S(2)}) async-start(f32[4,32,128]{2,1,0:T(8,128)} %get-tuple-element.22.info), calls=%async_computation.3 | async-start | bytes 131072 | tf_op jit(solution)/shard_map/all_to_all | solution.py:403

commit v8 on v6

--- a/solution.py
+++ b/solution.py
@@ -200,8 +200,9 @@
     best = jnp.max(values, axis=0)
     mass = jnp.sum(jnp.exp(values - best[None]), axis=0)
     norm = best + jnp.log(mass)
-    info[0:16, :] = jnp.where(best <= 0.5 * NEG, -NEG, norm)
-    info[16:32, :] = targets[...].astype(f32)
+    for group in range(info.shape[0]):
+        info[group, 0:16, :] = jnp.where(best <= 0.5 * NEG, -NEG, norm)
+        info[group, 16:32, :] = targets[...].astype(f32)
     target = jnp.sum(values[:, CAP + 1, :], axis=0, keepdims=True)
     loss[...] = norm[CAP : CAP + 1, :] - target
 
@@ -229,22 +230,34 @@
     for h in range(out.shape[0] // half):
         start = pl.multiple_of(group[0] * out.shape[0] + h * half, half)
         rows = table[pl.ds(start, half), :]
-        out[h * half : (h + 1) * half, :] = rows_gradient(start, rows, info, query_t, coefficients)
+        out[h * half : (h + 1) * half, :] = rows_gradient(start, rows, info.at[0], query_t, coefficients)
 
 
 def rest_kernel(
-    group, infos, table, own, next_t, last_t, far_t, out, total, queries, coefficients, load_sems, own_sem, sems
+    group, infos, table, own, next_t, last_t, far_low, far_high, out, total, queries, coefficients, load_sems, own_sem, sems
 ):
     half = coefficients.shape[0]
     groups = infos.shape[0]
+    low = far_low.shape[0]
     loads = [
-        pltpu.make_async_copy(query_t, queries.at[i], load_sems.at[i])
-        for i, query_t in enumerate((next_t, last_t, far_t))
+        [pltpu.make_async_copy(next_t, queries.at[0], load_sems.at[0])],
+        [pltpu.make_async_copy(last_t, queries.at[1], load_sems.at[1])],
+        [
+            pltpu.make_async_copy(far_low, queries.at[2, pl.ds(0, low), :], load_sems.at[2]),
+            pltpu.make_async_copy(far_high, queries.at[2, pl.ds(low, low), :], load_sems.at[3]),
+        ],
+        [pltpu.make_async_copy(own, total, own_sem)],
     ]
-    for load in loads:
-        load.start()
-    own_load = pltpu.make_async_copy(own, total, own_sem)
-    own_load.start()
+
+    def start_all(i):
+        for load in loads[i]:
+            load.start()
+
+    def wait_all(i):
+        for load in loads[i]:
+            load.wait()
+
+    start_all(0)
     copies = []
     for h in range(out.shape[0] // half):
         start = pl.multiple_of(group[0] * out.shape[0] + h * half, half)
@@ -253,11 +266,12 @@
         gradient = jnp.zeros((half, out.shape[1]), f32)
         for i, shift in enumerate((1, 3, 2)):
             if h == 0:
-                loads[i].wait()
+                wait_all(i)
+                start_all(i + 1)
             info = infos.at[(group[0] + shift) % groups]
             gradient = gradient + rows_gradient(start, rows, info, queries.at[i], coefficients)
         if h == 0:
-            own_load.wait()
+            wait_all(groups - 1)
         total[here, :] = total[here, :] + gradient
         copies.append(pltpu.make_async_copy(total.at[here, :], out.at[here, :], sems.at[h]))
         copies[-1].start()
@@ -347,9 +361,9 @@
         axis_index_groups=planes,
     ).reshape(depth, CAP * count)
     assert groups == 4
-    far_t, next_t, last_t = (
-        lax.ppermute(query_t, "dp", [(i, (i - shift) % groups) for i in range(groups)]) for shift in (2, 1, 3)
-    )
+    up = [(i, (i + 1) % groups) for i in range(groups)]
+    down = [(i, (i - 1) % groups) for i in range(groups)]
+    last_t, next_t = lax.ppermute(query_t, "dp", up), lax.ppermute(query_t, "dp", down)
 
     local = pl.pallas_call(
         stats_kernel,
@@ -368,6 +382,9 @@
         compiler_params=params(8),
         name="share",
     )(matches, local, other)
+    _, relay_last, relay_next = lax.optimization_barrier((share, last_t, next_t))
+    far_low = lax.ppermute(relay_last[: depth // 2], "dp", up)
+    far_high = lax.ppermute(relay_next[depth // 2 :], "dp", down)
     cores = [[i for i in range(owners) if i % 2 == core] for core in range(2)]
     shared = lax.all_to_all(
         share.reshape(owners // 2, 16, count), "entity", 0, 0, tiled=True, axis_index_groups=cores
@@ -375,7 +392,7 @@
 
     info, loss = pl.pallas_call(
         merge_kernel,
-        out_shape=(jax.ShapeDtypeStruct((32, count), f32), jax.ShapeDtypeStruct((1, count), f32)),
+        out_shape=(jax.ShapeDtypeStruct((groups, 32, count), f32), jax.ShapeDtypeStruct((1, count), f32)),
         compiler_params=params(8),
         name="merge",
     )(shared, targets)
@@ -383,9 +400,7 @@
     quarter = block_rows // groups
     half = quarter // 2
     mine_first = group.reshape(1)
-    infos = lax.all_to_all(
-        jnp.broadcast_to(info[None], (groups,) + info.shape), "dp", 0, 0, tiled=True
-    )
+    infos = lax.all_to_all(info, "dp", 0, 0, tiled=True)
 
     def cost(several):
         return pl.CostEstimate(
@@ -406,13 +421,13 @@
     gradient = pl.pallas_call(
         rest_kernel,
         out_shape=jax.ShapeDtypeStruct((quarter, depth), f32),
-        in_specs=[smem] + [vmem] * 2 + [pl.BlockSpec(memory_space=pltpu.HBM)] * 4,
+        in_specs=[smem] + [vmem] * 2 + [pl.BlockSpec(memory_space=pltpu.HBM)] * 5,
         out_specs=pl.BlockSpec(memory_space=pltpu.HBM),
         scratch_shapes=[
             pltpu.VMEM((quarter, depth), f32),
             pltpu.VMEM((groups - 1, depth, CAP * count), bf16),
             pltpu.VMEM((half, CAP * count), bf16),
-            pltpu.SemaphoreType.DMA((groups - 1,)),
+            pltpu.SemaphoreType.DMA((groups,)),
             pltpu.SemaphoreType.DMA,
             pltpu.SemaphoreType.DMA((2,)),
         ],
@@ -420,7 +435,7 @@
         compiler_params=params(16),
         cost_estimate=cost(groups - 1),
         name="rest",
-    )(mine_first, infos, rounded, own, next_t, last_t, far_t)
+    )(mine_first, infos, rounded, own, next_t, last_t, far_low, far_high)
     return (loss.reshape(count), gradient[None])
 
 

time: 103 us -> 100 us (0.971)
  waiting for transfers between devices: 27.3 us -> 20.7 us
  local copies, waits for them, and re-layouts: 0.63 us -> 2.8 us
  Pallas kernels: 27.3 us -> 28.6 us
    all_to_all x1, waiting for transfers between devices: 12.9 us -> 4.46 us  [per_device(): lax.all_to_all(share.reshape(owners // 2, 16, count), 'entity', 0, 0, til...]
    slice x0 -> x2, local copies, waits for them, and re-layouts: none -> 2.79 us  [the longest x1 1.77 us: per_device(): far_high = lax.ppermute(relay_next[depth // 2:], 'dp', down)]
    ppermute x3 -> x4, waiting for transfers between devices: 0.01 us -> 2.68 us  [the longest x1 2.65 us: per_device(): lax.ppermute(query_t, 'dp', up)]
    ppermute x3 -> x4, starting transfers between devices: 6.43 us -> 6.17 us  [the longest x1 2.93 us: per_device(): far_high = lax.ppermute(relay_next[depth // 2:], 'dp', down)]
  transfers between devices with their start and end apart: 7 -> 8, of which waited for: 4 -> 5; matrix products, arithmetic and copies ran while one was open for 3% -> 5% of each run, Pallas kernels for 13% -> 14%
where the time goes in v8:
time: 100 us; the launch traced here: 99.7 us
  Pallas kernels  28.6 us (29%)
  starting transfers between devices  26.3 us (26%)
  waiting for transfers between devices  20.7 us (21%)
  blocking collectives  17.9 us (18%)
  local copies, waits for them, and re-layouts  2.8 us (3%)
  other arithmetic  2.39 us (2%)
    all_to_all x1, blocking collectives, per_device(): lax.all_to_all(packed.reshape(PARTS, depth // PARTS, CAP * count), 'entit...  17.9 us
    all_to_all x1, starting transfers between devices, per_device(): lax.all_to_all(spread.reshape(owners, stride, count), 'entity', 0, 0, til...  11.6 us
    all_to_all x1, waiting for transfers between devices, per_device(): lax.all_to_all(spread.reshape(owners, stride, count), 'entity', 0, 0, til...  11.1 us
    pallas_call x1, Pallas kernels, per_device(): pl.pallas_call(rest_kernel, out_shape=jax.ShapeDtypeStruct((quarter, dept...  9.53 us
    pallas_call x1, Pallas kernels, per_device(): pl.pallas_call(stats_kernel, out_shape=jax.ShapeDtypeStruct((32, count),...  7.37 us
    all_to_all x1, starting transfers between devices, per_device(): lax.all_to_all(share.reshape(owners // 2, 16, count), 'entity', 0, 0, til...  4.97 us
    all_to_all x1, waiting for transfers between devices, per_device(): lax.all_to_all(share.reshape(owners // 2, 16, count), 'entity', 0, 0, til...  4.46 us
    pallas_call x1, Pallas kernels, per_device(): pl.pallas_call(query_kernel, out_shape=jax.ShapeDtypeStruct((owners * str...  4.05 us
  transfers between devices with their start and end apart: 8, of which 5 were waited for; matrix products, arithmetic and copies ran while one was open for 5% of the time, Pallas kernels for 14%

profile of v8, /device:TPU:32, one launch (start us, length us, event | category | flops | bytes accessed | tf_op | source)
XLA Modules:
  0.0 99.7 jit_solution(15895490969456418384)
XLA Ops:
  0.6 0.0 copy-start.1
  0.6 0.0 copy-start
  0.7 4.1 %query.1 = bf16[1536,128]{1,0:T(8,128)(2,1)} custom-call(s32[128]{0:T(128)} %heads.1, f32[4096,256]{1,0:T(8,128)} %bitcast.21, f32[4,256,256]{2,1,0:T(8,128)} %operators.1, s32[1,128]{1,0:T(1,128)} %bitcast.23, s32[1,128]{1,0:T(1,128)} %bitcast.24), custom_call_target="tpu_custom_call" | custom-call | tf_op jit(solution)/shard_map/query/pallas_call | solution.py:309
  4.7 11.6 %all-to-all-start = ((bf16[64,24,128]{2,1,0:T(8,128)(2,1)}), bf16[64,24,128]{2,1,0:T(8,128)(2,1)S(1)}, u32[]{:S(2)}, u32[]{:S(2)}) async-start(bf16[64,24,128]{2,1,0:T(8,128)(2,1)} %bitcast.22), calls=%async_computation | async-start | bytes 786432 | tf_op jit(solution)/shard_map/all_to_all | solution.py:322
  16.3 0.0 copy-done.1
  16.3 0.0 copy-done
  16.3 0.6 plan.1
  17.0 2.4 %bitcast_convert_fusion.table = bf16[4096,256]{1,0:T(8,128)(2,1)S(1)} fusion(f32[1,4096,256]{2,1,0:T(8,128)} %param.7), kind=kLoop, calls=%fused_computation | loop fusion | flops 1048576 | bytes 6291456 | tf_op jit(solution)/shard_map/convert_element_type | solution.py:338
  19.4 11.1 %all-to-all-done = bf16[64,24,128]{2,1,0:T(8,128)(2,1)S(1)} async-done(((bf16[64,24,128]{2,1,0:T(8,128)(2,1)}), bf16[64,24,128]{2,1,0:T(8,128)(2,1)S(1)}, u32[]{:S(2)}, u32[]{:S(2)}) %all-to-all-start) | async-done | bytes 393248 | tf_op jit(solution)/shard_map/all_to_all | solution.py:322
  30.4 1.0 pack.1
  31.4 17.9 %all_to_all.20 = bf16[16,16,1536]{2,1,0:T(8,128)(2,1)S(1)} all-to-all(bf16[16,16,1536]{2,1,0:T(8,128)(2,1)S(1)} %bitcast.19), channel_id=1, replica_groups={{0,1,2,3,4,5,6,7,8,9,10,11,12,13,14,15},{16,17,18,19,20,21,22,23,24,25,..., dimensions={0} | all-to-all | bytes 1572864 | tf_op jit(solution)/shard_map/all_to_all | solution.py:355
  49.3 1.6 %collective-permute-start.2 = (bf16[256,1536]{1,0:T(8,128)(2,1)S(1)}, bf16[256,1536]{1,0:T(8,128)(2,1)}, u32[]{:S(2)}, u32[]{:S(2)}) collective-permute-start(bf16[256,1536]{1,0:T(8,128)(2,1)S(1)} %bitcast.14), channel_id=1, source_target_pairs={{0,64},{64,128},{128,192},{192,0},{1,65},{65,129},{129,193},{193,1... | collective-permute-start | bytes 2359304 | tf_op jit(solution)/shard_map/ppermute | solution.py:366
  50.9 1.7 %collective-permute-start.1 = (bf16[256,1536]{1,0:T(8,128)(2,1)S(1)}, bf16[256,1536]{1,0:T(8,128)(2,1)}, u32[]{:S(2)}, u32[]{:S(2)}) collective-permute-start(bf16[256,1536]{1,0:T(8,128)(2,1)S(1)} %bitcast.15), channel_id=1, source_target_pairs={{0,192},{64,0},{128,64},{192,128},{1,193},{65,1},{129,65},{193,129... | collective-permute-start | bytes 2359304 | tf_op jit(solution)/shard_map/ppermute | solution.py:366
  52.6 7.4 %stats.1.mine = f32[32,128]{1,0:T(8,128)S(1)} custom-call(bf16[256,1536]{1,0:T(8,128)(2,1)S(1)} %bitcast.16, bf16[4096,256]{1,0:T(8,128)(2,1)S(1)} %bitcast_convert_fusion.table, s32[16,128]{1,0:T(8,128)S(1)} %get-tuple-element.19.targets), custom_call_target="tpu_custom_call" | custom-call | tf_op jit(solution)/shard_map/stats/pallas_call | solution.py:368
  59.9 0.1 collective-permute-start
  60.0 1.2 %collective-permute-done.other = f32[32,128]{1,0:T(8,128)S(1)} collective-permute-done((f32[32,128]{1,0:T(8,128)S(1)}, f32[32,128]{1,0:T(8,128)S(1)}, u32[]{:S(2)}, u32[]{:S(2)}) %collective-permute-start) | collective-permute-done | bytes 16416 | tf_op jit(solution)/shard_map/ppermute | solution.py:377
  61.2 1.3 %share.1 = f32[512,128]{1,0:T(8,128)} custom-call(f32[2,512,32]{2,1,0:T(8,128)S(1)} %get-tuple-element.13.matches, f32[32,128]{1,0:T(8,128)S(1)} %stats.1.mine, f32[32,128]{1,0:T(8,128)S(1)} %collective-permute-done.other), custom_call_target="tpu_custom_call" | custom-call | tf_op jit(solution)/shard_map/share/pallas_call | solution.py:378
  62.5 5.0 %all-to-all-start.2 = ((f32[32,16,128]{2,1,0:T(8,128)}), f32[32,16,128]{2,1,0:T(8,128)S(1)}, u32[]{:S(2)}, u32[]{:S(2)}) async-start(f32[32,16,128]{2,1,0:T(8,128)} %bitcast.9), calls=%async_computation.2 | async-start | bytes 524288 | tf_op jit(solution)/shard_map/all_to_all | solution.py:389
  67.5 2.7 %collective-permute-done.2.last_t = bf16[256,1536]{1,0:T(8,128)(2,1)} collective-permute-done((bf16[256,1536]{1,0:T(8,128)(2,1)S(1)}, bf16[256,1536]{1,0:T(8,128)(2,1)}, u32[]{:S(2)}, u32[]{:S(2)}) %collective-permute-start.2) | collective-permute-done | bytes 786464 | tf_op jit(solution)/shard_map/ppermute | solution.py:366
  70.2 0.0 collective-permute-done.1.next_t
  70.2 1.0 %slice.6 = bf16[128,1536]{1,0:T(8,128)(2,1)S(1)} slice(bf16[256,1536]{1,0:T(8,128)(2,1)} %collective-permute-done.2.last_t), slice={[0:128], [0:1536]} | slice | bytes 786432 | tf_op jit(solution)/shard_map/slice | solution.py:386
  71.2 1.8 %slice.7 = bf16[128,1536]{1,0:T(8,128)(2,1)} slice(bf16[256,1536]{1,0:T(8,128)(2,1)} %collective-permute-done.1.next_t), slice={[128:256], [0:1536]} | slice | bytes 786432 | tf_op jit(solution)/shard_map/slice | solution.py:387
  73.0 2.9 %collective-permute-start.4 = (bf16[128,1536]{1,0:T(8,128)(2,1)}, bf16[128,1536]{1,0:T(8,128)(2,1)}, u32[]{:S(2)}, u32[]{:S(2)}) collective-permute-start(bf16[128,1536]{1,0:T(8,128)(2,1)} %slice.7), channel_id=1, source_target_pairs={{0,192},{64,0},{128,64},{192,128},{1,193},{65,1},{129,65},{193,129... | collective-permute-start | bytes 1179656 | tf_op jit(solution)/shard_map/ppermute | solution.py:387
  75.9 0.0 collective-permute-start.3
  75.9 4.5 %all-to-all-done.2.received = f32[32,16,128]{2,1,0:T(8,128)S(1)} async-done(((f32[32,16,128]{2,1,0:T(8,128)}), f32[32,16,128]{2,1,0:T(8,128)S(1)}, u32[]{:S(2)}, u32[]{:S(2)}) %all-to-all-start.2) | async-done | bytes 262176 | tf_op jit(solution)/shard_map/all_to_all | solution.py:389
  80.4 0.7 merge.1
  81.1 3.5 %all-to-all-start.3 = ((f32[4,32,128]{2,1,0:T(8,128)}), f32[4,32,128]{2,1,0:T(8,128)S(1)}, u32[]{:S(2)}, u32[]{:S(2)}) async-start(f32[4,32,128]{2,1,0:T(8,128)} %get-tuple-element.21.info), calls=%async_computation.3 | async-start | bytes 131072 | tf_op jit(solution)/shard_map/all_to_all | solution.py:403
  84.6 4.0 %own.1 = f32[1024,256]{1,0:T(8,128)} custom-call(s32[1]{0:T(128)} %bitcast.11.group, f32[4,32,128]{2,1,0:T(8,128)} %get-tuple-element.21.info, bf16[4096,256]{1,0:T(8,128)(2,1)S(1)} %bitcast_convert_fusion.table, bf16[256,1536]{1,0:T(8,128)(2,1)S(1)} %bitcast.17), custom_call_target="tpu_custom_call" | custom-call | flops 1610612736 | bytes 2883584 | tf_op jit(solution)/shard_map/own/pallas_call | solution.py:412
  88.6 1.4 %all-to-all-done.3.infos = f32[4,32,128]{2,1,0:T(8,128)S(1)} async-done(((f32[4,32,128]{2,1,0:T(8,128)}), f32[4,32,128]{2,1,0:T(8,128)S(1)}, u32[]{:S(2)}, u32[]{:S(2)}) %all-to-all-start.3) | async-done | bytes 65568 | tf_op jit(solution)/shard_map/all_to_all | solution.py:403
  90.0 0.0 collective-permute-done.4.far_high
  90.0 0.0 collective-permute-done.3.far_low
  90.0 9.5 %rest.1 = f32[1024,256]{1,0:T(8,128)} custom-call(s32[1]{0:T(128)} %bitcast.11.group, f32[4,32,128]{2,1,0:T(8,128)S(1)} %all-to-all-done.3.infos, bf16[4096,256]{1,0:T(8,128)(2,1)S(1)} %bitcast_convert_fusion.table, f32[1024,256]{1,0:T(8,128)} %own.1, bf16[256,1536]{1,0:T(8,128)(2,1)} %collective-permute-done.1.next_t, ...), custom_call_target="tpu_custom_call", output_to_operand_aliasing={{}: (3, {})} | custom-call | flops 4831838208 | bytes 4456448 | tf_op jit(solution)/shard_map/rest/pallas_call | solution.py:421
Async XLA Ops:
  0.6 15.7 %copy-start.1 = (s32[1,64]{1,0:T(1,128)S(1)}, s32[1,64]{1,0:T(1,128)}, u32[]{:S(2)}) copy-start(s32[1,64]{1,0:T(1,128)} %lengths.1) | copy-start | bytes 772
  0.6 15.7 %copy-start = (s32[64,8]{0,1:T(8,128)S(1)}, s32[64,8]{0,1:T(8,128)}, u32[]{:S(2)}) copy-start(s32[64,8]{0,1:T(8,128)} %param.9) | copy-start | bytes 6148
  4.7 25.7 %all-to-all-start = ((bf16[64,24,128]{2,1,0:T(8,128)(2,1)}), bf16[64,24,128]{2,1,0:T(8,128)(2,1)S(1)}, u32[]{:S(2)}, u32[]{:S(2)}) async-start(bf16[64,24,128]{2,1,0:T(8,128)(2,1)} %bitcast.22), calls=%async_computation | async-start | bytes 786432 | tf_op jit(solution)/shard_map/all_to_all | solution.py:322
  49.3 20.8 %collective-permute-start.2 = (bf16[256,1536]{1,0:T(8,128)(2,1)S(1)}, bf16[256,1536]{1,0:T(8,128)(2,1)}, u32[]{:S(2)}, u32[]{:S(2)}) collective-permute-start(bf16[256,1536]{1,0:T(8,128)(2,1)S(1)} %bitcast.14), channel_id=1, source_target_pairs={{0,64},{64,128},{128,192},{192,0},{1,65},{65,129},{129,193},{193,1... | collective-permute-start | bytes 2359304 | tf_op jit(solution)/shard_map/ppermute | solution.py:366
  50.9 19.3 %collective-permute-start.1 = (bf16[256,1536]{1,0:T(8,128)(2,1)S(1)}, bf16[256,1536]{1,0:T(8,128)(2,1)}, u32[]{:S(2)}, u32[]{:S(2)}) collective-permute-start(bf16[256,1536]{1,0:T(8,128)(2,1)S(1)} %bitcast.15), channel_id=1, source_target_pairs={{0,192},{64,0},{128,64},{192,128},{1,193},{65,1},{129,65},{193,129... | collective-permute-start | bytes 2359304 | tf_op jit(solution)/shard_map/ppermute | solution.py:366
  59.9 1.3 %collective-permute-start = (f32[32,128]{1,0:T(8,128)S(1)}, f32[32,128]{1,0:T(8,128)S(1)}, u32[]{:S(2)}, u32[]{:S(2)}) collective-permute-start(f32[32,128]{1,0:T(8,128)S(1)} %stats.1.mine), channel_id=1, source_target_pairs={{0,1},{1,0},{2,3},{3,2},{4,5},{5,4},{6,7},{7,6},{8,9},{9,8},{10,11... | collective-permute-start | bytes 49160 | tf_op jit(solution)/shard_map/ppermute | solution.py:377
  62.5 17.8 %all-to-all-start.2 = ((f32[32,16,128]{2,1,0:T(8,128)}), f32[32,16,128]{2,1,0:T(8,128)S(1)}, u32[]{:S(2)}, u32[]{:S(2)}) async-start(f32[32,16,128]{2,1,0:T(8,128)} %bitcast.9), calls=%async_computation.2 | async-start | bytes 524288 | tf_op jit(solution)/shard_map/all_to_all | solution.py:389
  73.0 17.0 %collective-permute-start.4 = (bf16[128,1536]{1,0:T(8,128)(2,1)}, bf16[128,1536]{1,0:T(8,128)(2,1)}, u32[]{:S(2)}, u32[]{:S(2)}) collective-permute-start(bf16[128,1536]{1,0:T(8,128)(2,1)} %slice.7), channel_id=1, source_target_pairs={{0,192},{64,0},{128,64},{192,128},{1,193},{65,1},{129,65},{193,129... | collective-permute-start | bytes 1179656 | tf_op jit(solution)/shard_map/ppermute | solution.py:387
  75.9 14.1 %collective-permute-start.3 = (bf16[128,1536]{1,0:T(8,128)(2,1)S(1)}, bf16[128,1536]{1,0:T(8,128)(2,1)}, u32[]{:S(2)}, u32[]{:S(2)}) collective-permute-start(bf16[128,1536]{1,0:T(8,128)(2,1)S(1)} %slice.6), channel_id=1, source_target_pairs={{0,64},{64,128},{128,192},{192,0},{1,65},{65,129},{129,193},{193,1... | collective-permute-start | bytes 1179656 | tf_op jit(solution)/shard_map/ppermute | solution.py:386
  81.1 8.9 %all-to-all-start.3 = ((f32[4,32,128]{2,1,0:T(8,128)}), f32[4,32,128]{2,1,0:T(8,128)S(1)}, u32[]{:S(2)}, u32[]{:S(2)}) async-start(f32[4,32,128]{2,1,0:T(8,128)} %get-tuple-element.21.info), calls=%async_computation.3 | async-start | bytes 131072 | tf_op jit(solution)/shard_map/all_to_all | solution.py:403

commit v9 on v8

--- a/solution.py
+++ b/solution.py
@@ -9,7 +9,7 @@
 CAP = 12
 PARTS = 16
 WIDE = 4
-TILE = 1024
+TILE = 2048
 CHUNK = 128
 NEG = -1e30
 NONE_ROW = 14
@@ -258,21 +258,24 @@
             load.wait()
 
     start_all(0)
+    wait_all(0)
+    start_all(groups - 1)
+    start_all(1)
     copies = []
     for h in range(out.shape[0] // half):
         start = pl.multiple_of(group[0] * out.shape[0] + h * half, half)
         rows = table[pl.ds(start, half), :]
         here = slice(h * half, (h + 1) * half)
-        gradient = jnp.zeros((half, out.shape[1]), f32)
         for i, shift in enumerate((1, 3, 2)):
-            if h == 0:
+            if h == 0 and i > 0:
                 wait_all(i)
-                start_all(i + 1)
+            if h == 0 and i == 1:
+                start_all(2)
             info = infos.at[(group[0] + shift) % groups]
-            gradient = gradient + rows_gradient(start, rows, info, queries.at[i], coefficients)
-        if h == 0:
-            wait_all(groups - 1)
-        total[here, :] = total[here, :] + gradient
+            gradient = rows_gradient(start, rows, info, queries.at[i], coefficients)
+            if h == 0 and i == 0:
+                wait_all(groups - 1)
+            total[here, :] = total[here, :] + gradient
         copies.append(pltpu.make_async_copy(total.at[here, :], out.at[here, :], sems.at[h]))
         copies[-1].start()
     for copy in copies:

time: 100 us -> 99 us (0.990)
  Pallas kernels: 28.6 us -> 27.3 us
    pallas_call x1, Pallas kernels: 9.53 us -> 8.3 us  [per_device(): pl.pallas_call(rest_kernel, out_shape=jax.ShapeDtypeStruct((quarter, dept...]
where the time goes in v9:
time: 99 us; the launch traced here: 98.3 us
  Pallas kernels  27.3 us (28%)
  starting transfers between devices  26.3 us (27%)
  waiting for transfers between devices  20.7 us (21%)
  blocking collectives  17.9 us (18%)
  local copies, waits for them, and re-layouts  2.8 us (3%)
  other arithmetic  2.39 us (2%)
    all_to_all x1, blocking collectives, per_device(): lax.all_to_all(packed.reshape(PARTS, depth // PARTS, CAP * count), 'entit...  17.9 us
    all_to_all x1, starting transfers between devices, per_device(): lax.all_to_all(spread.reshape(owners, stride, count), 'entity', 0, 0, til...  11.6 us
    all_to_all x1, waiting for transfers between devices, per_device(): lax.all_to_all(spread.reshape(owners, stride, count), 'entity', 0, 0, til...  11.1 us
    pallas_call x1, Pallas kernels, per_device(): pl.pallas_call(rest_kernel, out_shape=jax.ShapeDtypeStruct((quarter, dept...  8.3 us
    pallas_call x1, Pallas kernels, per_device(): pl.pallas_call(stats_kernel, out_shape=jax.ShapeDtypeStruct((32, count),...  7.3 us
    all_to_all x1, starting transfers between devices, per_device(): lax.all_to_all(share.reshape(owners // 2, 16, count), 'entity', 0, 0, til...  4.94 us
    all_to_all x1, waiting for transfers between devices, per_device(): lax.all_to_all(share.reshape(owners // 2, 16, count), 'entity', 0, 0, til...  4.37 us
    pallas_call x1, Pallas kernels, per_device(): pl.pallas_call(query_kernel, out_shape=jax.ShapeDtypeStruct((owners * str...  4.05 us
  transfers between devices with their start and end apart: 8, of which 5 were waited for; matrix products, arithmetic and copies ran while one was open for 5% of the time, Pallas kernels for 14%

profile of v9, /device:TPU:32, one launch (start us, length us, event | category | flops | bytes accessed | tf_op | source)
XLA Modules:
  0.0 98.3 jit_solution(13846777356599242978)
XLA Ops:
  0.6 0.0 copy-start.1
  0.6 0.0 copy-start
  0.7 4.1 %query.1 = bf16[1536,128]{1,0:T(8,128)(2,1)} custom-call(s32[128]{0:T(128)} %heads.1, f32[4096,256]{1,0:T(8,128)} %bitcast.21, f32[4,256,256]{2,1,0:T(8,128)} %operators.1, s32[1,128]{1,0:T(1,128)} %bitcast.23, s32[1,128]{1,0:T(1,128)} %bitcast.24), custom_call_target="tpu_custom_call" | custom-call | tf_op jit(solution)/shard_map/query/pallas_call | solution.py:312
  4.7 11.6 %all-to-all-start = ((bf16[64,24,128]{2,1,0:T(8,128)(2,1)}), bf16[64,24,128]{2,1,0:T(8,128)(2,1)S(1)}, u32[]{:S(2)}, u32[]{:S(2)}) async-start(bf16[64,24,128]{2,1,0:T(8,128)(2,1)} %bitcast.22), calls=%async_computation | async-start | bytes 786432 | tf_op jit(solution)/shard_map/all_to_all | solution.py:325
  16.3 0.0 copy-done.1
  16.3 0.0 copy-done
  16.3 0.6 plan.1
  17.0 2.4 %bitcast_convert_fusion.table = bf16[4096,256]{1,0:T(8,128)(2,1)S(1)} fusion(f32[1,4096,256]{2,1,0:T(8,128)} %param.7), kind=kLoop, calls=%fused_computation | loop fusion | flops 1048576 | bytes 6291456 | tf_op jit(solution)/shard_map/convert_element_type | solution.py:341
  19.4 11.1 %all-to-all-done = bf16[64,24,128]{2,1,0:T(8,128)(2,1)S(1)} async-done(((bf16[64,24,128]{2,1,0:T(8,128)(2,1)}), bf16[64,24,128]{2,1,0:T(8,128)(2,1)S(1)}, u32[]{:S(2)}, u32[]{:S(2)}) %all-to-all-start) | async-done | bytes 393248 | tf_op jit(solution)/shard_map/all_to_all | solution.py:325
  30.4 1.0 %pack.1 = (bf16[256,1536]{1,0:T(8,128)(2,1)S(1)}, s32[16,128]{1,0:T(8,128)S(1)}) custom-call(s32[1]{0:T(128)} %bitcast.me.refs_0_, s32[16,128]{1,0:T(8,128)S(1)} %get-tuple-element.14.refs_1_, bf16[1536,128]{1,0:T(8,128)(2,1)S(1)} %bitcast.18, f32[16,128]{1,0:T(8,128)S(1)} %get-tuple-element.16.refs_3_), custom_call_target="tpu_custom_call" | custom-call | tf_op jit(solution)/shard_map/pack/pallas_call | solution.py:346
  31.4 17.9 %all_to_all.20 = bf16[16,16,1536]{2,1,0:T(8,128)(2,1)S(1)} all-to-all(bf16[16,16,1536]{2,1,0:T(8,128)(2,1)S(1)} %bitcast.19), channel_id=1, replica_groups={{0,1,2,3,4,5,6,7,8,9,10,11,12,13,14,15},{16,17,18,19,20,21,22,23,24,25,..., dimensions={0} | all-to-all | bytes 1572864 | tf_op jit(solution)/shard_map/all_to_all | solution.py:358
  49.3 1.6 %collective-permute-start.2 = (bf16[256,1536]{1,0:T(8,128)(2,1)S(1)}, bf16[256,1536]{1,0:T(8,128)(2,1)}, u32[]{:S(2)}, u32[]{:S(2)}) collective-permute-start(bf16[256,1536]{1,0:T(8,128)(2,1)S(1)} %bitcast.14), channel_id=1, source_target_pairs={{0,64},{64,128},{128,192},{192,0},{1,65},{65,129},{129,193},{193,1... | collective-permute-start | bytes 2359304 | tf_op jit(solution)/shard_map/ppermute | solution.py:369
  50.9 1.7 %collective-permute-start.1 = (bf16[256,1536]{1,0:T(8,128)(2,1)S(1)}, bf16[256,1536]{1,0:T(8,128)(2,1)}, u32[]{:S(2)}, u32[]{:S(2)}) collective-permute-start(bf16[256,1536]{1,0:T(8,128)(2,1)S(1)} %bitcast.15), channel_id=1, source_target_pairs={{0,192},{64,0},{128,64},{192,128},{1,193},{65,1},{129,65},{193,129... | collective-permute-start | bytes 2359304 | tf_op jit(solution)/shard_map/ppermute | solution.py:369
  52.6 7.3 %stats.1.mine = f32[32,128]{1,0:T(8,128)S(1)} custom-call(bf16[256,1536]{1,0:T(8,128)(2,1)S(1)} %bitcast.16, bf16[4096,256]{1,0:T(8,128)(2,1)S(1)} %bitcast_convert_fusion.table, s32[16,128]{1,0:T(8,128)S(1)} %get-tuple-element.19.targets), custom_call_target="tpu_custom_call" | custom-call | tf_op jit(solution)/shard_map/stats/pallas_call | solution.py:371
  59.9 0.1 collective-permute-start
  60.0 1.2 %collective-permute-done.other = f32[32,128]{1,0:T(8,128)S(1)} collective-permute-done((f32[32,128]{1,0:T(8,128)S(1)}, f32[32,128]{1,0:T(8,128)S(1)}, u32[]{:S(2)}, u32[]{:S(2)}) %collective-permute-start) | collective-permute-done | bytes 16416 | tf_op jit(solution)/shard_map/ppermute | solution.py:380
  61.2 1.3 %share.1 = f32[512,128]{1,0:T(8,128)} custom-call(f32[2,512,32]{2,1,0:T(8,128)S(1)} %get-tuple-element.13.matches, f32[32,128]{1,0:T(8,128)S(1)} %stats.1.mine, f32[32,128]{1,0:T(8,128)S(1)} %collective-permute-done.other), custom_call_target="tpu_custom_call" | custom-call | tf_op jit(solution)/shard_map/share/pallas_call | solution.py:381
  62.5 4.9 %all-to-all-start.2 = ((f32[32,16,128]{2,1,0:T(8,128)}), f32[32,16,128]{2,1,0:T(8,128)S(1)}, u32[]{:S(2)}, u32[]{:S(2)}) async-start(f32[32,16,128]{2,1,0:T(8,128)} %bitcast.9), calls=%async_computation.2 | async-start | bytes 524288 | tf_op jit(solution)/shard_map/all_to_all | solution.py:392
  67.4 2.7 %collective-permute-done.2.last_t = bf16[256,1536]{1,0:T(8,128)(2,1)} collective-permute-done((bf16[256,1536]{1,0:T(8,128)(2,1)S(1)}, bf16[256,1536]{1,0:T(8,128)(2,1)}, u32[]{:S(2)}, u32[]{:S(2)}) %collective-permute-start.2) | collective-permute-done | bytes 786464 | tf_op jit(solution)/shard_map/ppermute | solution.py:369
  70.2 0.0 collective-permute-done.1.next_t
  70.2 1.0 %slice.6 = bf16[128,1536]{1,0:T(8,128)(2,1)S(1)} slice(bf16[256,1536]{1,0:T(8,128)(2,1)} %collective-permute-done.2.last_t), slice={[0:128], [0:1536]} | slice | bytes 786432 | tf_op jit(solution)/shard_map/slice | solution.py:389
  71.2 1.8 %slice.7 = bf16[128,1536]{1,0:T(8,128)(2,1)} slice(bf16[256,1536]{1,0:T(8,128)(2,1)} %collective-permute-done.1.next_t), slice={[128:256], [0:1536]} | slice | bytes 786432 | tf_op jit(solution)/shard_map/slice | solution.py:390
  73.0 2.9 %collective-permute-start.4 = (bf16[128,1536]{1,0:T(8,128)(2,1)}, bf16[128,1536]{1,0:T(8,128)(2,1)}, u32[]{:S(2)}, u32[]{:S(2)}) collective-permute-start(bf16[128,1536]{1,0:T(8,128)(2,1)} %slice.7), channel_id=1, source_target_pairs={{0,192},{64,0},{128,64},{192,128},{1,193},{65,1},{129,65},{193,129... | collective-permute-start | bytes 1179656 | tf_op jit(solution)/shard_map/ppermute | solution.py:390
  75.9 0.0 collective-permute-start.3
  75.9 4.4 %all-to-all-done.2.received = f32[32,16,128]{2,1,0:T(8,128)S(1)} async-done(((f32[32,16,128]{2,1,0:T(8,128)}), f32[32,16,128]{2,1,0:T(8,128)S(1)}, u32[]{:S(2)}, u32[]{:S(2)}) %all-to-all-start.2) | async-done | bytes 262176 | tf_op jit(solution)/shard_map/all_to_all | solution.py:392
  80.3 0.7 merge.1
  81.0 3.5 %all-to-all-start.3 = ((f32[4,32,128]{2,1,0:T(8,128)}), f32[4,32,128]{2,1,0:T(8,128)S(1)}, u32[]{:S(2)}, u32[]{:S(2)}) async-start(f32[4,32,128]{2,1,0:T(8,128)} %get-tuple-element.21.info), calls=%async_computation.3 | async-start | bytes 131072 | tf_op jit(solution)/shard_map/all_to_all | solution.py:406
  84.5 4.0 %own.1 = f32[1024,256]{1,0:T(8,128)} custom-call(s32[1]{0:T(128)} %bitcast.11.group, f32[4,32,128]{2,1,0:T(8,128)} %get-tuple-element.21.info, bf16[4096,256]{1,0:T(8,128)(2,1)S(1)} %bitcast_convert_fusion.table, bf16[256,1536]{1,0:T(8,128)(2,1)S(1)} %bitcast.17), custom_call_target="tpu_custom_call" | custom-call | flops 1610612736 | bytes 2883584 | tf_op jit(solution)/shard_map/own/pallas_call | solution.py:415
  88.5 1.4 %all-to-all-done.3.infos = f32[4,32,128]{2,1,0:T(8,128)S(1)} async-done(((f32[4,32,128]{2,1,0:T(8,128)}), f32[4,32,128]{2,1,0:T(8,128)S(1)}, u32[]{:S(2)}, u32[]{:S(2)}) %all-to-all-start.3) | async-done | bytes 65568 | tf_op jit(solution)/shard_map/all_to_all | solution.py:406
  89.9 0.0 collective-permute-done.4.far_high
  89.9 0.0 collective-permute-done.3.far_low
  89.9 8.3 %rest.1 = f32[1024,256]{1,0:T(8,128)} custom-call(s32[1]{0:T(128)} %bitcast.11.group, f32[4,32,128]{2,1,0:T(8,128)S(1)} %all-to-all-done.3.infos, bf16[4096,256]{1,0:T(8,128)(2,1)S(1)} %bitcast_convert_fusion.table, f32[1024,256]{1,0:T(8,128)} %own.1, bf16[256,1536]{1,0:T(8,128)(2,1)} %collective-permute-done.1.next_t, ...), custom_call_target="tpu_custom_call", output_to_operand_aliasing={{}: (3, {})} | custom-call | flops 4831838208 | bytes 4456448 | tf_op jit(solution)/shard_map/rest/pallas_call | solution.py:424
Async XLA Ops:
  0.6 15.7 %copy-start.1 = (s32[1,64]{1,0:T(1,128)S(1)}, s32[1,64]{1,0:T(1,128)}, u32[]{:S(2)}) copy-start(s32[1,64]{1,0:T(1,128)} %lengths.1) | copy-start | bytes 772
  0.6 15.7 %copy-start = (s32[64,8]{0,1:T(8,128)S(1)}, s32[64,8]{0,1:T(8,128)}, u32[]{:S(2)}) copy-start(s32[64,8]{0,1:T(8,128)} %param.9) | copy-start | bytes 6148
  4.7 25.7 %all-to-all-start = ((bf16[64,24,128]{2,1,0:T(8,128)(2,1)}), bf16[64,24,128]{2,1,0:T(8,128)(2,1)S(1)}, u32[]{:S(2)}, u32[]{:S(2)}) async-start(bf16[64,24,128]{2,1,0:T(8,128)(2,1)} %bitcast.22), calls=%async_computation | async-start | bytes 786432 | tf_op jit(solution)/shard_map/all_to_all | solution.py:325
  49.3 20.8 %collective-permute-start.2 = (bf16[256,1536]{1,0:T(8,128)(2,1)S(1)}, bf16[256,1536]{1,0:T(8,128)(2,1)}, u32[]{:S(2)}, u32[]{:S(2)}) collective-permute-start(bf16[256,1536]{1,0:T(8,128)(2,1)S(1)} %bitcast.14), channel_id=1, source_target_pairs={{0,64},{64,128},{128,192},{192,0},{1,65},{65,129},{129,193},{193,1... | collective-permute-start | bytes 2359304 | tf_op jit(solution)/shard_map/ppermute | solution.py:369
  50.9 19.3 %collective-permute-start.1 = (bf16[256,1536]{1,0:T(8,128)(2,1)S(1)}, bf16[256,1536]{1,0:T(8,128)(2,1)}, u32[]{:S(2)}, u32[]{:S(2)}) collective-permute-start(bf16[256,1536]{1,0:T(8,128)(2,1)S(1)} %bitcast.15), channel_id=1, source_target_pairs={{0,192},{64,0},{128,64},{192,128},{1,193},{65,1},{129,65},{193,129... | collective-permute-start | bytes 2359304 | tf_op jit(solution)/shard_map/ppermute | solution.py:369
  59.9 1.3 %collective-permute-start = (f32[32,128]{1,0:T(8,128)S(1)}, f32[32,128]{1,0:T(8,128)S(1)}, u32[]{:S(2)}, u32[]{:S(2)}) collective-permute-start(f32[32,128]{1,0:T(8,128)S(1)} %stats.1.mine), channel_id=1, source_target_pairs={{0,1},{1,0},{2,3},{3,2},{4,5},{5,4},{6,7},{7,6},{8,9},{9,8},{10,11... | collective-permute-start | bytes 49160 | tf_op jit(solution)/shard_map/ppermute | solution.py:380
  62.5 17.8 %all-to-all-start.2 = ((f32[32,16,128]{2,1,0:T(8,128)}), f32[32,16,128]{2,1,0:T(8,128)S(1)}, u32[]{:S(2)}, u32[]{:S(2)}) async-start(f32[32,16,128]{2,1,0:T(8,128)} %bitcast.9), calls=%async_computation.2 | async-start | bytes 524288 | tf_op jit(solution)/shard_map/all_to_all | solution.py:392
  73.0 16.9 %collective-permute-start.4 = (bf16[128,1536]{1,0:T(8,128)(2,1)}, bf16[128,1536]{1,0:T(8,128)(2,1)}, u32[]{:S(2)}, u32[]{:S(2)}) collective-permute-start(bf16[128,1536]{1,0:T(8,128)(2,1)} %slice.7), channel_id=1, source_target_pairs={{0,192},{64,0},{128,64},{192,128},{1,193},{65,1},{129,65},{193,129... | collective-permute-start | bytes 1179656 | tf_op jit(solution)/shard_map/ppermute | solution.py:390
  75.9 14.0 %collective-permute-start.3 = (bf16[128,1536]{1,0:T(8,128)(2,1)S(1)}, bf16[128,1536]{1,0:T(8,128)(2,1)}, u32[]{:S(2)}, u32[]{:S(2)}) collective-permute-start(bf16[128,1536]{1,0:T(8,128)(2,1)S(1)} %slice.6), channel_id=1, source_target_pairs={{0,64},{64,128},{128,192},{192,0},{1,65},{65,129},{129,193},{193,1... | collective-permute-start | bytes 1179656 | tf_op jit(solution)/shard_map/ppermute | solution.py:389
  81.0 8.9 %all-to-all-start.3 = ((f32[4,32,128]{2,1,0:T(8,128)}), f32[4,32,128]{2,1,0:T(8,128)S(1)}, u32[]{:S(2)}, u32[]{:S(2)}) async-start(f32[4,32,128]{2,1,0:T(8,128)} %get-tuple-element.21.info), calls=%async_computation.3 | async-start | bytes 131072 | tf_op jit(solution)/shard_map/all_to_all | solution.py:406
